TPU v7x, 32 devices: a whole 2x2x4 slice. The times are simulated.
32 devices in a mesh: tm: 2 (over core), lat: 16 (over z, y, x).
Axes of the slice: x: 2, y: 2, z: 4, core: 2. Of those that a mesh axis runs over, the one named last changes fastest.
Arguments:
- spectral_state: float32 [4, 16, 2, 16, 256], P('tm', 'lat'), may hold values from -6 to 6
- legendre: bfloat16 [16, 16, 16], P('lat'), may hold values from -1.5 to 1.5
- wave_slots: int32 [16], replicated, may hold values from 0 to 15, each once
- lat_order: int32 [16], replicated, may hold values from 0 to 15, each once
- quad_weights: float32 [16], replicated, may hold values from 0.2 to 1
- available: int32 [4, 8, 16, 256], P('tm', None, 'lat'), may hold values 0 or 1
- targets: float32 [4, 4, 8], P('tm'), may hold values from -6 to 6
- w_first: float32 [256, 384], replicated, may hold values from -0.375 to 0.375
- w_mid: float32 [384, 384], replicated, may hold values from -0.3125 to 0.3125
- w_last: float32 [384, 256], replicated, may hold values from -0.3125 to 0.3125
- norm_bias: float32 [2, 1024], replicated, may hold values from -0.3 to 0.3
- mean_first: float32 [256, 384], replicated, may hold values from -0.00061035156 to 0.00061035156
- mean_mid: float32 [384, 384], replicated, may hold values from -0.00061035156 to 0.00061035156
- mean_last: float32 [384, 256], replicated, may hold values from -0.00061035156 to 0.00061035156
- mean_bias: float32 [2, 1024], replicated, may hold values from -0.00061035156 to 0.00061035156
- square_first: float32 [256, 384], replicated, may hold values from 3e-10 to 3e-08
- square_mid: float32 [384, 384], replicated, may hold values from 3e-10 to 3e-08
- square_last: float32 [384, 256], replicated, may hold values from 3e-10 to 3e-08
- square_bias: float32 [2, 1024], replicated, may hold values from 3e-10 to 3e-08
Outputs:
- loss: float32 [], replicated
- grad_norm: float32 [], replicated
- master_first: float32 [256, 384], replicated
- master_mid: float32 [384, 384], replicated
- master_last: float32 [384, 256], replicated
- master_bias: float32 [2, 1024], replicated
- new_mean_first: float32 [256, 384], replicated
- new_mean_mid: float32 [384, 384], replicated
- new_mean_last: float32 [384, 256], replicated
- new_mean_bias: float32 [2, 1024], replicated
- new_square_first: float32 [256, 384], replicated
- new_square_mid: float32 [384, 384], replicated
- new_square_last: float32 [384, 256], replicated
- new_square_bias: float32 [2, 1024], replicated
- half_first: bfloat16 [256, 384], replicated
- half_mid: bfloat16 [384, 384], replicated
- half_last: bfloat16 [384, 256], replicated
- half_bias: bfloat16 [2, 1024], replicated
Inputs may be any that keep to these rules, and one draw needn't show every extreme that they name: `wave_slots`: each wavenumber 0 to 15 stands in one slot; slot j lies on the device of index j // 1 of lat. `lat_order`: each latitude stands in one grid row.
All inputs are finite; a program needn't handle non-finite values. No bound on the sum of `available` on one device may be relied on, other than what follows from the above.
Results may differ from a plain program's by a relative error of at most 0.0082.
Values may be sent and summed in bfloat16 or wider, within the bound.
No kernel may reach another device: no remote copies, remote signals or barrier semaphores. Data moves between devices by JAX's collectives and lax.ppermute only.
A program may use at most 128 MiB of HBM per device.

v0:
```python
from functools import partial
import math

import jax
import jax.numpy as jnp
from jax import lax
from jax.sharding import PartitionSpec as P

STEPS = 4


EPS_NORM = 1e-05
STEP_SCALE = 0.5
CLIP_NORM = 1.0
LEARN_RATE = 0.01
BETA_ONE = 0.9
BETA_TWO = 0.95
EPS_ADAM = 1e-08
DECAY = 0.1
HIGH = lax.Precision.HIGHEST


def wave_tables(wave_slots, lon_count):
    product = wave_slots[:, None] * jnp.arange(lon_count, dtype=jnp.int32)[None, :] % lon_count
    phase = product.astype(jnp.float32) * (2.0 * math.pi / lon_count)
    inverse = jnp.stack([jnp.cos(phase), -jnp.sin(phase)], axis=1)
    scale = jnp.where(wave_slots == 0, 1.0, 2.0).astype(jnp.float32) / lon_count
    return (inverse.astype(jnp.bfloat16), (inverse * scale[:, None, None]).astype(jnp.bfloat16))


def layer_spans(chans, hidden):
    gains = [(0, chans), (chans, hidden), (chans + hidden, hidden)]
    biases = [(0, hidden), (hidden, hidden), (2 * hidden, chans)]
    return list(zip(gains, biases))


def norm_gain(x, gain):
    centre = x - jnp.mean(x, axis=-1, keepdims=True)
    return centre * lax.rsqrt(jnp.mean(centre * centre, axis=-1, keepdims=True) + EPS_NORM) * gain


def corrector_forward(x, weights, norm_bias):
    spans = layer_spans(weights[0].shape[0], weights[0].shape[1])
    saved = []
    for k in range(3):
        (gstart, gwidth), (bstart, bwidth) = spans[k]
        h_low = norm_gain(x, 1.0 + norm_bias[0, gstart : gstart + gwidth]).astype(jnp.bfloat16)
        z_val = (
            jnp.dot(h_low, weights[k], preferred_element_type=jnp.float32)
            + norm_bias[1, bstart : bstart + bwidth]
        )
        saved.append((x, h_low, z_val))
        x = jax.nn.gelu(z_val, approximate=False) if k < 2 else z_val
    return (x, saved)


def corrector_backward(grad, saved, weights, norm_bias):
    spans = layer_spans(weights[0].shape[0], weights[0].shape[1])
    weight_grads = [None, None, None]
    gain_parts = [None, None, None]
    bias_parts = [None, None, None]
    for k in (2, 1, 0):
        (gstart, gwidth), (bstart, bwidth) = spans[k]
        x, h_low, z_val = saved[k]
        if k < 2:
            grad = jax.vjp(partial(jax.nn.gelu, approximate=False), z_val)[1](grad)[0]
        grad_low = grad.astype(jnp.bfloat16)
        weight_grads[k] = lax.dot_general(
            h_low, grad_low, (((0,), (0,)), ((), ())), preferred_element_type=jnp.float32
        )
        bias_parts[k] = jnp.sum(grad_low, axis=0, dtype=jnp.float32)
        back_h = lax.dot_general(
            grad_low, weights[k], (((1,), (1,)), ((), ())), preferred_element_type=jnp.float32
        )
        grad, gain_parts[k] = jax.vjp(norm_gain, x, 1.0 + norm_bias[0, gstart : gstart + gwidth])[
            1
        ](back_h)
    vector_grad = jnp.stack([jnp.concatenate(gain_parts), jnp.concatenate(bias_parts)])
    return (grad, (weight_grads[0], weight_grads[1], weight_grads[2], vector_grad))


def adamw(weight, mean, square, grad):
    mean_new = BETA_ONE * mean + (1.0 - BETA_ONE) * grad
    square_new = BETA_TWO * square + (1.0 - BETA_TWO) * grad * grad
    weight_new = weight - LEARN_RATE * (
        mean_new / (jnp.sqrt(square_new) + EPS_ADAM) + DECAY * weight
    )
    return (weight_new, mean_new, square_new)


def per_device(
    spectral_state,
    legendre,
    wave_slots,
    lat_order,
    quad_weights,
    available,
    targets,
    w_first,
    w_mid,
    w_last,
    norm_bias,
    mean_first,
    mean_mid,
    mean_last,
    mean_bias,
    square_first,
    square_mid,
    square_last,
    square_bias,
):
    tdev, wdev, _, degrees, chans = spectral_state.shape
    fields = available.shape[1]
    rows_dev = available.shape[2]
    lon_count = available.shape[3]
    levels = chans // fields
    lat_index = lax.axis_index("lat")
    slots = lax.dynamic_slice_in_dim(wave_slots, lat_index * wdev, wdev)
    finv, ffw = wave_tables(wave_slots, lon_count)
    keep = (jnp.arange(degrees, dtype=jnp.int32)[None, :] >= slots[:, None]).astype(jnp.bfloat16)
    plg = jnp.take(legendre, lat_order, axis=2) * keep[:, :, None]
    qrow = jnp.take(quad_weights, lat_order)
    qlocal = lax.dynamic_slice_in_dim(qrow, lat_index * rows_dev, rows_dev)
    colw = qlocal[None, None, :, None] * available.astype(jnp.float32)
    den_part = jnp.sum(colw, axis=(2, 3))
    params = (w_first, w_mid, w_last, norm_bias)
    weights = (
        w_first.astype(jnp.bfloat16),
        w_mid.astype(jnp.bfloat16),
        w_last.astype(jnp.bfloat16),
    )

    def legendre_sum(piece):
        return jnp.einsum("mnr,tmprc->tmpnc", plg, piece, preferred_element_type=jnp.float32)

    def fourier_sum(table, piece):
        return jnp.einsum("mpk,tmprc->trkc", table, piece, preferred_element_type=jnp.float32)

    def to_grid(state):
        sums = jnp.einsum(
            "mnr,tmpnc->tmprc", plg, state.astype(jnp.bfloat16), preferred_element_type=jnp.float32
        ).astype(jnp.bfloat16)
        return fourier_sum(
            finv, lax.all_to_all(sums, "lat", split_axis=3, concat_axis=1, tiled=True)
        )

    def column_pass(grid):
        out, saved = corrector_forward(grid.reshape(-1, chans), weights, norm_bias)
        return (out.reshape(grid.shape), saved)

    states = []
    nums = []
    den_total = den_part
    state = spectral_state
    for s in range(STEPS):
        states.append(state)
        grid = to_grid(state)
        out, saved = column_pass(grid)
        pred = grid + STEP_SCALE * out
        num_part = jnp.einsum(
            "tfrk,trkfl->tf",
            colw,
            pred.reshape(tdev, rows_dev, lon_count, fields, levels),
            precision=HIGH,
        )
        num_total, den_total = lax.psum((num_part, den_part), "lat")
        nums.append(num_total)
        tend = (out * qlocal[None, :, None, None]).astype(jnp.bfloat16)
        coeff = jnp.einsum("mpk,trkc->tmprc", ffw, tend, preferred_element_type=jnp.float32).astype(
            jnp.bfloat16
        )
        spec = legendre_sum(lax.all_to_all(coeff, "lat", split_axis=1, concat_axis=3, tiled=True))
        state = state + STEP_SCALE * spec
    num_all = jnp.stack(nums)
    bias = num_all / (levels * den_total[None]) - jnp.moveaxis(targets, 1, 0)
    loss = lax.psum(jnp.sum(bias * bias) / STEPS, "tm")
    grad_bias = 2.0 * bias / (STEPS * levels * den_total[None])
    totals = tuple((jnp.zeros_like(p) for p in params))
    back_state = None
    for s in reversed(range(STEPS)):
        grid = to_grid(states[s])
        out, saved = column_pass(grid)
        scaled = jnp.moveaxis(colw * grad_bias[s][:, :, None, None], 1, 3)
        back_pred = jnp.broadcast_to(scaled[..., None], scaled.shape + (levels,)).reshape(
            grid.shape
        )
        back_out = STEP_SCALE * back_pred
        if back_state is not None:
            back_spec = (STEP_SCALE * back_state).astype(jnp.bfloat16)
            back_coeff = jnp.einsum(
                "mnr,tmpnc->tmprc", plg, back_spec, preferred_element_type=jnp.float32
            ).astype(jnp.bfloat16)
            back_tend = fourier_sum(
                ffw, lax.all_to_all(back_coeff, "lat", split_axis=3, concat_axis=1, tiled=True)
            )
            back_out = back_out + qlocal[None, :, None, None] * back_tend
        back_in, grads = corrector_backward(back_out.reshape(-1, chans), saved, weights, norm_bias)
        totals = tuple((a + b for a, b in zip(totals, grads)))
        if s > 0:
            back_grid = (back_pred + back_in.reshape(grid.shape)).astype(jnp.bfloat16)
            back_sums = jnp.einsum(
                "mpk,trkc->tmprc", finv, back_grid, preferred_element_type=jnp.float32
            ).astype(jnp.bfloat16)
            back_low = legendre_sum(
                lax.all_to_all(back_sums, "lat", split_axis=1, concat_axis=3, tiled=True)
            )
            back_state = back_low if back_state is None else back_state + back_low
    means = (mean_first, mean_mid, mean_last, mean_bias)
    squares = (square_first, square_mid, square_last, square_bias)
    grads = lax.psum(totals, ("tm", "lat"))
    grad_norm = jnp.sqrt(sum((jnp.sum(g * g) for g in grads)))
    factor = CLIP_NORM / jnp.maximum(grad_norm, CLIP_NORM)
    results = [adamw(w, a, b, g * factor) for w, a, b, g in zip(params, means, squares, grads)]
    masters = [r[0] for r in results]
    new_means = [r[1] for r in results]
    new_squares = [r[2] for r in results]
    halves = [w.astype(jnp.bfloat16) for w in masters]
    return (
        loss,
        grad_norm,
        masters[0],
        masters[1],
        masters[2],
        masters[3],
        new_means[0],
        new_means[1],
        new_means[2],
        new_means[3],
        new_squares[0],
        new_squares[1],
        new_squares[2],
        new_squares[3],
        halves[0],
        halves[1],
        halves[2],
        halves[3],
    )


def solution(mesh):
    in_specs = (
        P("tm", "lat", None, None, None),
        P("lat", None, None),
        P(),
        P(),
        P(),
        P("tm", None, "lat", None),
        P("tm", None, None),
        P(),
        P(),
        P(),
        P(),
        P(),
        P(),
        P(),
        P(),
        P(),
        P(),
        P(),
        P(),
    )
    out_specs = (
        P(),
        P(),
        P(),
        P(),
        P(),
        P(),
        P(),
        P(),
        P(),
        P(),
        P(),
        P(),
        P(),
        P(),
        P(),
        P(),
        P(),
        P(),
    )
    return jax.shard_map(
        per_device, mesh=mesh, in_specs=in_specs, out_specs=out_specs, check_vma=False
    )
```

profile of v0, /device:TPU:0, one launch (start us, length us, event | category | flops | bytes accessed | tf_op | source)
XLA Modules:
  0.0 491.2 jit_solution(849199737556524078)
XLA Ops:
  11.4 8.3 %all-to-all-start = ((bf16[2,1,2,16,256]{4,2,0,1,3:T(2,128)(2,1)}), bf16[2,1,2,16,256]{4,2,0,1,3:T(2,128)(2,1)S(1)}, u32[]{:S(2)}, u32[]{:S(2)}) async-start(bf16[2,1,2,16,256]{4,2,0,1,3:T(2,128)(2,1)} %copy.194), calls=%async_computation | async-start | bytes 65536 | tf_op jit(solution)/shard_map/all_to_all | solution.py:144
  21.9 5.3 %all-to-all-done = bf16[2,1,2,16,256]{4,2,0,1,3:T(2,128)(2,1)S(1)} async-done(((bf16[2,1,2,16,256]{4,2,0,1,3:T(2,128)(2,1)}), bf16[2,1,2,16,256]{4,2,0,1,3:T(2,128)(2,1)S(1)}, u32[]{:S(2)}, u32[]{:S(2)}) %all-to-all-start) | async-done | bytes 32800 | tf_op jit(solution)/shard_map/all_to_all | solution.py:144
  28.0 3.0 fusion.214
  31.9 3.2 fusion.212
  37.8 10.0 %all_to_all.215 = bf16[2,16,2,1,256]{4,2,0,3,1:T(2,128)(2,1)S(1)} all-to-all(bf16[2,16,2,1,256]{4,2,0,3,1:T(2,128)(2,1)S(1)} %copy.198), channel_id=1, replica_groups=mesh['tm'=2,'lat'=16] {'lat'}, dimensions={1} | all-to-all | bytes 65536 | tf_op jit(solution)/shard_map/all_to_all | solution.py:172
  48.2 10.4 %all_to_all.216 = bf16[2,1,2,16,256]{4,2,0,1,3:T(2,128)(2,1)S(1)} all-to-all(bf16[2,1,2,16,256]{4,2,0,1,3:T(2,128)(2,1)S(1)} %copy.202), channel_id=1, replica_groups=mesh['tm'=2,'lat'=16] {'lat'}, dimensions={3} | all-to-all | bytes 65536 | tf_op jit(solution)/shard_map/all_to_all | solution.py:144
  60.9 3.0 fusion.210
  64.8 3.2 fusion.208
  70.8 10.0 %all_to_all.217 = bf16[2,16,2,1,256]{4,2,0,3,1:T(2,128)(2,1)S(1)} all-to-all(bf16[2,16,2,1,256]{4,2,0,3,1:T(2,128)(2,1)S(1)} %copy.206), channel_id=1, replica_groups=mesh['tm'=2,'lat'=16] {'lat'}, dimensions={1} | all-to-all | bytes 65536 | tf_op jit(solution)/shard_map/all_to_all | solution.py:172
  81.1 10.0 %all_to_all.218 = bf16[2,1,2,16,256]{4,2,0,1,3:T(2,128)(2,1)S(1)} all-to-all(bf16[2,1,2,16,256]{4,2,0,1,3:T(2,128)(2,1)S(1)} %copy.209), channel_id=1, replica_groups=mesh['tm'=2,'lat'=16] {'lat'}, dimensions={3} | all-to-all | bytes 65536 | tf_op jit(solution)/shard_map/all_to_all | solution.py:144
  93.7 3.1 fusion.206
  96.9 3.2 fusion.204
  102.4 10.0 %all_to_all.219 = bf16[2,16,2,1,256]{4,2,0,3,1:T(2,128)(2,1)S(1)} all-to-all(bf16[2,16,2,1,256]{4,2,0,3,1:T(2,128)(2,1)S(1)} %copy.213), channel_id=1, replica_groups=mesh['tm'=2,'lat'=16] {'lat'}, dimensions={1} | all-to-all | bytes 65536 | tf_op jit(solution)/shard_map/all_to_all | solution.py:172
  113.3 3.8 all-to-all-start.6
  136.5 3.1 fusion.202
  140.8 3.2 fusion.200
  150.7 42.5 %all-reduce.1 = (f32[1,2,8]{2,1,0:T(2,128)S(1)}, f32[1,2,8]{2,1,0:T(2,128)S(1)}, f32[1,2,8]{2,1,0:T(2,128)S(1)}, f32[1,2,8]{2,1,0:T(2,128)S(1)}, f32[2,8]{1,0:T(2,128)S(1)}) all-reduce(f32[1,2,8]{2,1,0:T(2,128)S(1)} %bitcast.673, f32[1,2,8]{2,1,0:T(2,128)S(1)} %bitcast.674, ...), channel_id=1, replica_groups=mesh['tm'=2,'lat'=16] {'lat'}, use_global_device_ids=true, to_apply=%region_31.32 | all-reduce | flops 80 | bytes 640 | tf_op jit(solution)/shard_map/psum | solution.py:166
  211.0 3.2 psum.75
  230.9 3.6 all-to-all-start.7
  235.3 6.7 %all-to-all-done.7 = bf16[2,16,2,1,256]{4,2,0,3,1:T(2,128)(2,1)S(1)} async-done(((bf16[2,16,2,1,256]{4,2,0,3,1:T(2,128)(2,1)}), bf16[2,16,2,1,256]{4,2,0,3,1:T(2,128)(2,1)S(1)}, u32[]{:S(2)}, u32[]{:S(2)}) %all-to-all-start.7) | async-done | bytes 32800 | tf_op jit(solution)/shard_map/all_to_all | solution.py:205
  242.9 3.5 all-to-all-start.8
  247.1 6.6 %all-to-all-done.8 = bf16[2,1,2,16,256]{4,2,0,1,3:T(2,128)(2,1)S(1)} async-done(((bf16[2,1,2,16,256]{4,2,0,1,3:T(2,128)(2,1)}), bf16[2,1,2,16,256]{4,2,0,1,3:T(2,128)(2,1)S(1)}, u32[]{:S(2)}, u32[]{:S(2)}) %all-to-all-start.8) | async-done | bytes 32800 | tf_op jit(solution)/shard_map/all_to_all | solution.py:194
  268.9 3.5 all-to-all-start.9
  272.5 7.4 %all-to-all-done.9 = bf16[2,16,2,1,256]{4,2,0,3,1:T(2,128)(2,1)S(1)} async-done(((bf16[2,16,2,1,256]{4,2,0,3,1:T(2,128)(2,1)}), bf16[2,16,2,1,256]{4,2,0,3,1:T(2,128)(2,1)S(1)}, u32[]{:S(2)}, u32[]{:S(2)}) %all-to-all-start.9) | async-done | bytes 32800 | tf_op jit(solution)/shard_map/all_to_all | solution.py:205
  280.8 3.5 all-to-all-start.10
  284.3 7.4 %all-to-all-done.10 = bf16[2,1,2,16,256]{4,2,0,1,3:T(2,128)(2,1)S(1)} async-done(((bf16[2,1,2,16,256]{4,2,0,1,3:T(2,128)(2,1)}), bf16[2,1,2,16,256]{4,2,0,1,3:T(2,128)(2,1)S(1)}, u32[]{:S(2)}, u32[]{:S(2)}) %all-to-all-start.10) | async-done | bytes 32800 | tf_op jit(solution)/shard_map/all_to_all | solution.py:194
  305.3 3.7 all-to-all-start.11
  311.2 5.2 %all-to-all-done.11 = bf16[2,16,2,1,256]{4,2,0,3,1:T(2,128)(2,1)S(1)} async-done(((bf16[2,16,2,1,256]{4,2,0,3,1:T(2,128)(2,1)}), bf16[2,16,2,1,256]{4,2,0,3,1:T(2,128)(2,1)S(1)}, u32[]{:S(2)}, u32[]{:S(2)}) %all-to-all-start.11) | async-done | bytes 32800 | tf_op jit(solution)/shard_map/all_to_all | solution.py:205
  317.3 3.5 all-to-all-start.12
  320.9 7.3 %all-to-all-done.12 = bf16[2,1,2,16,256]{4,2,0,1,3:T(2,128)(2,1)S(1)} async-done(((bf16[2,1,2,16,256]{4,2,0,1,3:T(2,128)(2,1)}), bf16[2,1,2,16,256]{4,2,0,1,3:T(2,128)(2,1)S(1)}, u32[]{:S(2)}, u32[]{:S(2)}) %all-to-all-start.12) | async-done | bytes 32800 | tf_op jit(solution)/shard_map/all_to_all | solution.py:194
  339.8 38.6 %psum.79 = f32[2,1024]{1,0:T(2,128)S(1)} all-reduce(f32[2,1024]{1,0:T(2,128)S(1)} %fusion.164), channel_id=1, replica_groups=mesh['tm'=2,'lat'=16] {'tm','lat'}, use_global_device_ids=true, to_apply=%region_88.89 | all-reduce | flops 2048 | bytes 16384 | tf_op jit(solution)/shard_map/psum | solution.py:210
  378.9 90.0 %all-reduce.4.cloned.1.call-done = (f32[256,384]{1,0:T(8,128)}, f32[384,384]{1,0:T(8,128)}, f32[384,256]{1,0:T(8,128)}) async-done(((f32[256,384]{1,0:T(8,128)}, f32[384,384]{1,0:T(8,128)}, f32[384,256]{1,0:T(8,128)}), (f32[256,384]{1,0:T(8,128)}, f32[384,384]{1,0:T(8,128)}, f32[384,256]{1,0:T(8,128)})) %all-reduce.4.cloned.1.call-update) | async-done | bytes 1376272 | tf_op jit(solution)/shard_map/psum | solution.py:210
  (528 shorter events, 142.0 us)
Async XLA Ops:
  9.2 11.4 %copy-start.37 = (f32[256,384]{1,0:T(8,128)S(1)}, f32[256,384]{1,0:T(8,128)}, u32[]{:S(2)}) copy-start(f32[256,384]{1,0:T(8,128)} %param.26) | copy-start | bytes 1179652
  10.6 9.1 %copy-start.91 = (f32[2,1024]{1,0:T(2,128)S(1)}, f32[2,1024]{1,0:T(2,128)}, u32[]{:S(2)}) copy-start(f32[2,1024]{1,0:T(2,128)} %param.29) | copy-start | bytes 24580
  10.8 9.9 %copy-start.39 = (f32[384,256]{1,0:T(8,128)S(1)}, f32[384,256]{1,0:T(8,128)}, u32[]{:S(2)}) copy-start(f32[384,256]{1,0:T(8,128)} %param.28) | copy-start | bytes 1179652
  11.4 15.8 %all-to-all-start = ((bf16[2,1,2,16,256]{4,2,0,1,3:T(2,128)(2,1)}), bf16[2,1,2,16,256]{4,2,0,1,3:T(2,128)(2,1)S(1)}, u32[]{:S(2)}, u32[]{:S(2)}) async-start(bf16[2,1,2,16,256]{4,2,0,1,3:T(2,128)(2,1)} %copy.194), calls=%async_computation | async-start | bytes 65536 | tf_op jit(solution)/shard_map/all_to_all | solution.py:144
  19.8 73.8 %copy-start.139 = (f32[384]{0:T(512)}, f32[384]{0:T(512)S(1)}, u32[]{:S(2)}) copy-start(f32[384]{0:T(512)S(1)} %get-tuple-element.47) | copy-start | bytes 4612
  19.8 77.1 %copy-start.137 = (f32[384]{0:T(512)}, f32[384]{0:T(512)S(1)}, u32[]{:S(2)}) copy-start(f32[384]{0:T(512)S(1)} %get-tuple-element.45) | copy-start | bytes 4612
  20.6 73.0 %copy-start.24 = (bf16[256,384]{1,0:T(8,128)(2,1)}, bf16[256,384]{1,0:T(8,128)(2,1)S(1)}, u32[]{:S(2)}) copy-start(bf16[256,384]{1,0:T(8,128)(2,1)S(1)} %convert_element_type.413) | copy-start | bytes 589828
  21.8 75.2 %copy-start.21 = (bf16[384,384]{1,0:T(8,128)(2,1)}, bf16[384,384]{1,0:T(8,128)(2,1)S(1)}, u32[]{:S(2)}) copy-start(bf16[384,384]{1,0:T(8,128)(2,1)S(1)} %convert_element_type.415) | copy-start | bytes 884740
  31.0 4.0 copy-start.4
  63.9 4.0 copy-start.6
  113.3 3.8 copy-start.123
  113.3 19.9 %all-to-all-start.6 = ((bf16[2,1,2,16,256]{4,2,0,1,3:T(2,128)(2,1)}), bf16[2,1,2,16,256]{4,2,0,1,3:T(2,128)(2,1)S(1)}, u32[]{:S(2)}, u32[]{:S(2)}) async-start(bf16[2,1,2,16,256]{4,2,0,1,3:T(2,128)(2,1)} %copy.216), calls=%async_computation.6 | async-start | bytes 65536 | tf_op jit(solution)/shard_map/all_to_all | solution.py:144
  133.6 71.9 %copy-start.87 = (f32[1,2,2,128]{3,1,2,0:T(2,128)}, f32[1,2,2,128]{3,1,2,0:T(2,128)S(1)}, u32[]{:S(2)}) copy-start(f32[1,2,2,128]{3,1,2,0:T(2,128)S(1)} %copy.333) | copy-start | bytes 6148
  135.3 70.2 %copy-start.89 = (f32[512]{0:T(512)}, f32[512]{0:T(512)S(1)}, u32[]{:S(2)}) copy-start(f32[512]{0:T(512)S(1)} %rsqrt.155) | copy-start | bytes 6148
  139.6 4.4 copy-start.2
  139.8 4.2 copy-start.113
  208.8 5.3 %copy-start.136 = (f32[2,8]{1,0:T(2,128)S(1)}, f32[2,8]{1,0:T(2,128)}, u32[]{:S(2)}) copy-start(f32[2,8]{1,0:T(2,128)} %get-tuple-element.143) | copy-start | bytes 196
  230.9 3.7 copy-start.128
  230.9 11.0 %all-to-all-start.7 = ((bf16[2,16,2,1,256]{4,2,0,3,1:T(2,128)(2,1)}), bf16[2,16,2,1,256]{4,2,0,3,1:T(2,128)(2,1)S(1)}, u32[]{:S(2)}, u32[]{:S(2)}) async-start(bf16[2,16,2,1,256]{4,2,0,3,1:T(2,128)(2,1)} %copy.228), calls=%async_computation.7 | async-start | bytes 65536 | tf_op jit(solution)/shard_map/all_to_all | solution.py:205
  242.9 10.9 %all-to-all-start.8 = ((bf16[2,1,2,16,256]{4,2,0,1,3:T(2,128)(2,1)}), bf16[2,1,2,16,256]{4,2,0,1,3:T(2,128)(2,1)S(1)}, u32[]{:S(2)}, u32[]{:S(2)}) async-start(bf16[2,1,2,16,256]{4,2,0,1,3:T(2,128)(2,1)} %copy.231), calls=%async_computation.8 | async-start | bytes 65536 | tf_op jit(solution)/shard_map/all_to_all | solution.py:194
  268.1 23.6 %copy-start.36 = (f32[2,1,256,256]{3,2,0,1:T(8,128)S(1)}, f32[2,1,256,256]{3,2,0,1:T(8,128)}, u32[]{:S(2)}) copy-start(f32[2,1,256,256]{3,2,0,1:T(8,128)} %copy.243) | copy-start | bytes 1572868
  268.9 10.9 %all-to-all-start.9 = ((bf16[2,16,2,1,256]{4,2,0,3,1:T(2,128)(2,1)}), bf16[2,16,2,1,256]{4,2,0,3,1:T(2,128)(2,1)S(1)}, u32[]{:S(2)}, u32[]{:S(2)}) async-start(bf16[2,16,2,1,256]{4,2,0,3,1:T(2,128)(2,1)} %copy.238), calls=%async_computation.9 | async-start | bytes 65536 | tf_op jit(solution)/shard_map/all_to_all | solution.py:205
  280.8 10.9 %all-to-all-start.10 = ((bf16[2,1,2,16,256]{4,2,0,1,3:T(2,128)(2,1)}), bf16[2,1,2,16,256]{4,2,0,1,3:T(2,128)(2,1)S(1)}, u32[]{:S(2)}, u32[]{:S(2)}) async-start(bf16[2,1,2,16,256]{4,2,0,1,3:T(2,128)(2,1)} %copy.241), calls=%async_computation.10 | async-start | bytes 65536 | tf_op jit(solution)/shard_map/all_to_all | solution.py:194
  304.4 4.6 copy-start.49
  305.3 11.1 %all-to-all-start.11 = ((bf16[2,16,2,1,256]{4,2,0,3,1:T(2,128)(2,1)}), bf16[2,16,2,1,256]{4,2,0,3,1:T(2,128)(2,1)S(1)}, u32[]{:S(2)}, u32[]{:S(2)}) async-start(bf16[2,16,2,1,256]{4,2,0,3,1:T(2,128)(2,1)} %copy.248), calls=%async_computation.11 | async-start | bytes 65536 | tf_op jit(solution)/shard_map/all_to_all | solution.py:205
  309.0 19.2 %copy-start.35 = (f32[2,1,256,256]{3,2,0,1:T(8,128)S(1)}, f32[2,1,256,256]{3,2,0,1:T(8,128)}, u32[]{:S(2)}) copy-start(f32[2,1,256,256]{3,2,0,1:T(8,128)} %copy.253) | copy-start | bytes 1572868
  317.3 10.9 %all-to-all-start.12 = ((bf16[2,1,2,16,256]{4,2,0,1,3:T(2,128)(2,1)}), bf16[2,1,2,16,256]{4,2,0,1,3:T(2,128)(2,1)S(1)}, u32[]{:S(2)}, u32[]{:S(2)}) async-start(bf16[2,1,2,16,256]{4,2,0,1,3:T(2,128)(2,1)} %copy.251), calls=%async_computation.12 | async-start | bytes 65536 | tf_op jit(solution)/shard_map/all_to_all | solution.py:194
  320.9 148.0 %all-reduce.4.cloned.1.call-start = ((), (), s32[]{:S(2)}) async-start(), calls=%async_computation.13 | async-start | bytes 2752512 | tf_op jit(solution)/shard_map/psum | solution.py:210
  339.3 137.3 %copy-start.72 = (f32[256,384]{1,0:T(8,128)S(1)}, f32[256,384]{1,0:T(8,128)}, u32[]{:S(2)}) copy-start(f32[256,384]{1,0:T(8,128)} %param.30) | copy-start | bytes 1179652
  468.9 7.7 %copy-start.71 = (f32[256,384]{1,0:T(8,128)S(1)}, f32[256,384]{1,0:T(8,128)}, u32[]{:S(2)}) copy-start(f32[256,384]{1,0:T(8,128)} %param.34) | copy-start | bytes 1179652
  470.6 6.0 %copy-start.38 = (f32[256,384]{1,0:T(8,128)S(1)}, f32[256,384]{1,0:T(8,128)}, u32[]{:S(2)}) copy-start(f32[256,384]{1,0:T(8,128)} %param.26) | copy-start | bytes 1179652
  472.5 3.4 copy-start.130
  (120 other events, 167.2 us)
Sparse Core Ops, SparseCore 0:
  339.4 129.4 all-reduce.3
where the time goes:
time: 499 us; the launch traced here: 491 us
  waiting for transfers between devices  136 us (27%)
  blocking collectives  135 us (27%)
  matrix products  61.3 us (12%)
  local copies, waits for them, and re-layouts  61.2 us (12%)
  other arithmetic  44.3 us (9%)
  starting transfers between devices  33.6 us (7%)
  between operations  20.5 us (4%)
    psum x1, waiting for transfers between devices, per_device(): grads = lax.psum(totals, ('tm', 'lat'))  90 us
    psum x1, blocking collectives, per_device(): num_total, den_total = lax.psum((num_part, den_part), 'lat')  42.5 us
    psum x1, blocking collectives, per_device(): grads = lax.psum(totals, ('tm', 'lat'))  38.6 us
    dot_general x12, matrix products, corrector_forward(): jnp.dot(h_low, weights[k], preferred_element_type=jnp.float32)  31.7 us
    all_to_all x3, blocking collectives, per_device(): lax.all_to_all(coeff, 'lat', split_axis=1, concat_axis=3, tiled=True)  29.9 us
    unnamed x297, local copies, waits for them, and re-layouts  29.6 us
    all_to_all x3, waiting for transfers between devices, per_device(): lax.all_to_all(back_coeff, 'lat', split_axis=3, concat_axis=1, tiled=True)  21.3 us
    all_to_all x2, blocking collectives, to_grid(): lax.all_to_all(sums, 'lat', split_axis=3, concat_axis=1, tiled=True)  20.4 us
  transfers between devices with their start and end apart: 9, of which 8 were waited for; matrix products, arithmetic and copies ran while one was open for 4% of the time, Pallas kernels for 0%

commit v1 on v0

--- a/solution.py
+++ b/solution.py
@@ -1,9 +1,12 @@
+from collections import namedtuple
 from functools import partial
 import math
 
 import jax
 import jax.numpy as jnp
 from jax import lax
+from jax.experimental import pallas as pl
+from jax.experimental.pallas import tpu as pltpu
 from jax.sharding import PartitionSpec as P
 
 STEPS = 4
@@ -88,7 +91,7 @@
     return (weight_new, mean_new, square_new)
 
 
-def per_device(
+def spread_device(
     spectral_state,
     legendre,
     wave_slots,
@@ -237,6 +240,718 @@
     )
 
 
+F32 = jnp.float32
+BF16 = jnp.bfloat16
+VM = pltpu.VMEM
+LANES = 128
+GROUP = 2
+SUB = 256
+ROWS_BLOCK = 2
+VMEM_LIMIT = 30 << 20
+SAVED_LIMIT = 96 << 20
+
+
+Plan = namedtuple("Plan", ("group", "rows", "waves", "degrees", "steps", "fields", "chans", "hidden", "lons"))
+
+
+def dot(a, b, dims=((1,), (0,))):
+    return lax.dot_general(a, b, (dims, ((), ())), preferred_element_type=F32)
+
+
+def norm_unit(x, eps):
+    centre = x - jnp.mean(x, axis=-1, keepdims=True)
+    scale = lax.rsqrt(jnp.mean(centre * centre, axis=-1, keepdims=True) + eps)
+    return centre * scale, scale
+
+
+def gelu_twice(z):
+    arg = z * math.sqrt(0.5)
+    cdf = 1.0 + lax.erf(arg)
+    pdf = jnp.exp2(arg * arg * -math.log2(math.e))
+    return z * cdf, cdf + (z * math.sqrt(2.0 / math.pi)) * pdf
+
+
+def whole(a):
+    return pl.BlockSpec(a.shape, lambda *_: (0,) * len(a.shape))
+
+
+def fold(v):
+    return jnp.sum(v.reshape(v.shape[0] // 8, 8, v.shape[1]), axis=0)
+
+
+def field_mask(fields, chans):
+    lane = lax.broadcasted_iota(jnp.int32, (fields, chans), 1)
+    row = lax.broadcasted_iota(jnp.int32, (fields, chans), 0) * (chans // fields)
+    return (lane >= row) & (lane < row + chans // fields)
+
+
+def splits(nb, chans, hidden):
+    gains = [1.0 + nb[0:1, a:b] for a, b in ((0, chans), (chans, chans + hidden), (chans + hidden, chans + 2 * hidden))]
+    biases = [nb[1:2, a:b] for a, b in ((0, hidden), (hidden, 2 * hidden), (2 * hidden, 2 * hidden + chans))]
+    return gains, biases
+
+
+def pair_rows(plan):
+    return ROWS_BLOCK if plan.rows % ROWS_BLOCK == 0 else 1
+
+
+def row_weight(plan, info, order, quad, row):
+    return quad[order[(info[1] * 2 + info[0]) * plan.rows + row]]
+
+
+def prepare_kernel(plan, info, slots, order, quad, got, got_o, inv, ffw, state, links, lt, avail, nums, table, ffw_t):
+    group, rows, waves, degrees, steps, fields, chans, _, _ = plan
+    members = 2 * group
+    core, member = info[0], info[1]
+    span = waves * degrees
+    mine = rows * waves
+    half = fields // 2
+    lats = rows * members
+    leg = jnp.zeros((waves, chans), F32)
+    row_of = lax.broadcasted_iota(jnp.int32, (waves, chans), 0)
+    pick = lax.broadcasted_iota(jnp.int32, (8, chans), 0) == half
+    for j in range(waves):
+        at = pl.ds(j * degrees, degrees)
+        for ref, p in ((got, core), (got_o, 1 - core)):
+            hi = ref[j, 0:degrees, :].astype(F32)
+            state[p, at, :] = hi + ref[j, degrees : 2 * degrees, :].astype(F32)
+        tail = got[j, 2 * degrees : 2 * degrees + 8, :].astype(F32)
+        line = jnp.sum(jnp.where(pick, tail, 0.0), axis=0, keepdims=True)
+        leg = jnp.where(row_of == j, line, leg)
+    iota = lambda d, s: lax.broadcasted_iota(jnp.int32, s, d)
+    shape = (span, span)
+    r0, r1 = iota(0, shape), iota(1, shape)
+    expand = (iota(0, (span, waves)) // degrees == iota(1, (span, waves))).astype(F32).astype(BF16)
+    rep = dot(expand, leg.astype(BF16))
+    rep = jnp.where(r1 // lats == r0 % degrees, rep, 0.0).astype(BF16)
+    lat_lane = jnp.zeros((8, span), jnp.int32)
+    lane = iota(1, (8, span)) // waves
+    for r in range(lats):
+        lat_lane = jnp.where(lane == r, order[r], lat_lane)
+    wave_row = jnp.zeros(shape, jnp.int32)
+    for j in range(waves):
+        wave_row = jnp.where(r0 // degrees == j, slots[j], wave_row)
+    choose = (r0 % lats == lat_lane[0:1, :]).astype(F32).astype(BF16)
+    plg = dot(rep, choose)
+    plg = jnp.where((r0 // degrees == r1 % waves) & (r0 % degrees >= wave_row), plg, 0.0)
+    flip = plg.T
+    spot = member * 2 + core
+    for role in range(members):
+        other = (member ^ (role & (group - 1))) * 2 + (core ^ (role // group))
+        piece = jnp.zeros((span, mine), F32)
+        for w in range(members):
+            piece = jnp.where(other == w, plg[:, w * mine : (w + 1) * mine], piece)
+        links[role] = piece.astype(BF16)
+    own = jnp.zeros((mine, span), F32)
+    for w in range(members):
+        own = jnp.where(spot == w, flip[w * mine : (w + 1) * mine, :], own)
+    lt[...] = own.astype(BF16)
+    den = jnp.zeros((fields, chans), F32)
+    for r in range(rows):
+        src = spot * rows + r
+        a = got[src, 2 * degrees : 2 * degrees + 8, :].astype(F32)
+        b = got_o[src, 2 * degrees : 2 * degrees + 8, :].astype(F32)
+        first = jnp.where(core == 0, a, b)[0:half]
+        second = jnp.where(core == 0, b, a)[0:half]
+        both = jnp.concatenate([first, second], axis=0)
+        avail[r] = both.astype(BF16)
+        den += quad[order[src]] * both
+    nums[...] = jnp.zeros_like(nums)
+    nums[steps * fields :, :] = jnp.broadcast_to(jnp.sum(den, axis=1, keepdims=True), (fields, nums.shape[1]))
+    table[...] = inv[...].T.astype(BF16)
+    ffw_t[...] = ffw[...].T.astype(BF16)
+
+
+def prepare_call(plan, info, slots, order, quad, got, got_o, inv, ffw):
+    group, rows, waves, degrees, steps, fields, chans, _, lons = plan
+    span, mine = waves * degrees, rows * waves
+    ins = [got, got_o, inv, ffw]
+    shapes = [
+        jax.ShapeDtypeStruct((2, span, chans), F32),
+        jax.ShapeDtypeStruct((2 * group, span, mine), BF16),
+        jax.ShapeDtypeStruct((mine, span), BF16),
+        jax.ShapeDtypeStruct((rows, fields, lons), BF16),
+        jax.ShapeDtypeStruct(((steps + 1) * fields, LANES), F32),
+        jax.ShapeDtypeStruct((lons, 2 * waves), BF16),
+        jax.ShapeDtypeStruct((lons, 2 * waves), BF16),
+    ]
+    return pl.pallas_call(
+        partial(prepare_kernel, plan),
+        out_shape=shapes,
+        grid_spec=pltpu.PrefetchScalarGridSpec(
+            num_scalar_prefetch=4,
+            grid=(1,),
+            in_specs=[whole(a) for a in ins],
+            out_specs=[whole(a) for a in shapes],
+        ),
+        compiler_params=kernel_params(),
+        name="prepare",
+    )(info, slots, order, quad, *ins)
+
+
+def kernel_params():
+    return pltpu.CompilerParams(vmem_limit_bytes=VMEM_LIMIT)
+
+
+def forward_kernel(plan, step, info, order, quad, *refs):
+    group, rows, waves, _, steps, fields, chans, hidden, lons = plan
+    first, last = step == 0, step == steps - 1
+    rows_blk = pair_rows(plan)
+    refs = list(refs)
+    take = lambda: refs.pop(0)
+    state, avail, nums_in, table, ffw, lt, w1, w2, w3, nb = [take() for _ in range(10)]
+    if not first:
+        links = take()
+        pieces = [take() for _ in range(2 * group)]
+    units, slopes, scales, nums = [take() for _ in range(4)]
+    if not last:
+        y_out = take()
+    if not first and not last:
+        state_out = take()
+    sums, num_acc = take(), take()
+    i = pl.program_id(0)
+
+    @pl.when(i == 0)
+    def _():
+        for p in range(2):
+            st = state[p]
+            if not first:
+                spec = dot(links[0], pieces[0][p])
+                for role in range(1, 2 * group):
+                    spec = spec + dot(links[role], pieces[role][p])
+                st = st + STEP_SCALE * spec
+                if not last:
+                    state_out[p] = st
+            sums[p] = dot(lt[...], st.astype(BF16)).astype(BF16)
+        num_acc[...] = jnp.zeros_like(num_acc)
+
+    gains, biases = splits(nb, chans, hidden)
+    for rr in range(rows_blk):
+        row = i * rows_blk + rr
+        at = pl.ds(pl.multiple_of(row * waves, waves), waves)
+        rhs = jnp.concatenate([sums[0, at, :], sums[1, at, :]], axis=0)
+        q = row_weight(plan, info, order, quad, row)
+        highs, lows, tends = [], [], []
+        for c0 in range(0, lons, SUB):
+            cs = slice(rr * lons + c0, rr * lons + c0 + SUB)
+            grid = dot(table[c0 : c0 + SUB, :], rhs)
+            u1, s1 = norm_unit(grid, EPS_NORM)
+            units[cs, 0:chans] = u1
+            scales[cs, :] = jnp.broadcast_to(s1, (SUB, LANES))
+            a1, d1 = gelu_twice(dot((u1 * gains[0]).astype(BF16), w1[...]) + biases[0])
+            u2, s2 = norm_unit(a1, 4.0 * EPS_NORM)
+            units[cs, chans : chans + hidden] = u2
+            slopes[cs, 0:hidden] = d1 * s2
+            a2, d2 = gelu_twice(dot((u2 * gains[1]).astype(BF16), w2[...]) + biases[1])
+            u3, s3 = norm_unit(a2, 4.0 * EPS_NORM)
+            units[cs, chans + hidden :] = u3
+            slopes[cs, hidden:] = d2 * s3
+            out = dot((u3 * gains[2]).astype(BF16), w3[...]) + biases[2]
+            pred = grid + STEP_SCALE * out
+            hi = pred.astype(BF16)
+            highs.append(hi)
+            lows.append((pred - hi.astype(F32)).astype(BF16))
+            tends.append((out * q).astype(BF16))
+        weigh = lambda parts: dot(avail[rr], jnp.concatenate(parts, axis=0))
+        num_acc[...] += q * (weigh(highs) + weigh(lows))
+        if not last:
+            coeff = dot(ffw[...], jnp.concatenate(tends, axis=0)).astype(BF16)
+            y_out[0, rr * waves : (rr + 1) * waves, :] = coeff[:waves]
+            y_out[1, rr * waves : (rr + 1) * waves, :] = coeff[waves:]
+
+    @pl.when(i == pl.num_programs(0) - 1)
+    def _():
+        kept = jnp.where(field_mask(fields, chans), num_acc[...], 0.0)
+        nums[...] = nums_in[...]
+        nums[step * fields : (step + 1) * fields, :] = jnp.broadcast_to(
+            jnp.sum(kept, axis=1, keepdims=True), (fields, LANES)
+        )
+
+
+def forward_call(plan, step, scalars, state, avail, nums, table, ffw, lt, weights, nb, links, pieces):
+    group, rows, waves, _, steps, fields, chans, hidden, lons = plan
+    first, last = step == 0, step == steps - 1
+    rows_blk = pair_rows(plan)
+    cols, blk = rows * lons, rows_blk * lons
+    ins = [state, avail, nums, table, ffw, lt, *weights, nb]
+    if not first:
+        ins += [links, *pieces]
+    specs = [whole(a) for a in ins]
+    specs[1] = pl.BlockSpec((rows_blk, fields, lons), lambda i, *_: (i, 0, 0))
+    shapes, ospecs = [], []
+    for width in (chans + 2 * hidden, 2 * hidden, LANES):
+        shapes.append(jax.ShapeDtypeStruct((cols, width), F32))
+        ospecs.append(pl.BlockSpec((blk, width), lambda i, *_: (i, 0)))
+    shapes.append(jax.ShapeDtypeStruct(nums.shape, F32))
+    ospecs.append(whole(nums))
+    if not last:
+        shapes.append(jax.ShapeDtypeStruct((2, rows * waves, chans), BF16))
+        ospecs.append(pl.BlockSpec((2, rows_blk * waves, chans), lambda i, *_: (0, i, 0)))
+    if not first and not last:
+        shapes.append(jax.ShapeDtypeStruct(state.shape, F32))
+        ospecs.append(whole(state))
+    return pl.pallas_call(
+        partial(forward_kernel, plan, step),
+        out_shape=shapes,
+        grid_spec=pltpu.PrefetchScalarGridSpec(
+            num_scalar_prefetch=3,
+            grid=(rows // rows_blk,),
+            in_specs=specs,
+            out_specs=ospecs,
+            scratch_shapes=[VM((2, rows * waves, chans), BF16), VM((fields, chans), F32)],
+        ),
+        compiler_params=kernel_params(),
+        name=f"forward_{step}",
+    )(*scalars, *ins)
+
+
+def packed_parts(plan):
+    parts, at = [], 0
+    sizes = ((plan.chans, plan.hidden), (plan.hidden, plan.hidden), (plan.hidden, plan.chans))
+    for which, (rows, cols) in enumerate(sizes):
+        for tile in range(cols // LANES):
+            parts.append((which, tile, at, rows))
+            at += rows
+    return parts, at
+
+
+def packed_block(plan, chips):
+    vectors = 2 * (plan.chans + 2 * plan.hidden) // LANES
+    need = packed_parts(plan)[1] + vectors
+    return -(-need // (2 * chips * 16)) * 16
+
+
+def both_halves(at, rows, half):
+    out, done = [], 0
+    while done < rows:
+        h = (at + done) // half
+        n = min(rows - done, (h + 1) * half - at - done)
+        out.append((h, at + done - h * half, done, n))
+        done += n
+    return out
+
+
+def backward_kernel(plan, step, info, order, quad, *refs):
+    group, rows, waves, _, steps, fields, chans, hidden, lons = plan
+    first, last = step == steps - 1, step == 0
+    fresh = step == steps - 2
+    rows_blk = pair_rows(plan)
+    members = 2 * group
+    levels = chans // fields
+    refs = list(refs)
+    take = lambda: refs.pop(0)
+    units, slopes, scales, avail, tgt, w1, w2, w3, nb = [take() for _ in range(9)]
+    counts = [take() for _ in range(members)]
+    if not first:
+        links, lt, ffw_t = [take() for _ in range(3)]
+        pieces = [take() for _ in range(members)]
+        if not fresh:
+            bstate = take()
+        before = [take() for _ in range(4)]
+    if not last:
+        inv = take()
+        grads = [take() for _ in range(4)]
+        b_out = take()
+        if not first:
+            bstate_out = take()
+    else:
+        mine, send = take(), take()
+    if first:
+        loss = take()
+    coef, gmask = take(), take()
+    if last:
+        grads = [take() for _ in range(4)]
+        packed = take()
+    d1, d2, d3, dv = grads
+    i = pl.program_id(0)
+
+    @pl.when(i == 0)
+    def _():
+        def total(s):
+            acc = [c[s * fields : (s + 1) * fields, :] for c in counts]
+            while len(acc) > 1:
+                acc = [a + b for a, b in zip(acc[::2], acc[1::2])]
+            return acc[0]
+
+        den = total(steps)
+        bias_of = lambda s: total(s) / (levels * den) - tgt[s * fields : (s + 1) * fields, :]
+        gb = 2.0 * bias_of(step) / (steps * levels * den)
+        gb = jnp.concatenate([gb] * (chans // LANES), axis=1)
+        gb = jnp.where(field_mask(fields, chans), gb, 0.0)
+        hi = gb.astype(BF16).astype(F32)
+        gmask[...] = jnp.concatenate([hi, gb - hi], axis=0).astype(BF16)
+        if first:
+            sq = bias_of(0) * bias_of(0)
+            for s in range(1, steps):
+                sq = sq + bias_of(s) * bias_of(s)
+            loss[...] = jnp.broadcast_to(jnp.sum(sq, axis=0, keepdims=True) / steps, loss.shape)
+            for d in grads:
+                d[...] = jnp.zeros_like(d)
+        else:
+            for d, b in zip(grads, before):
+                d[...] = b[...]
+            for p in range(2):
+                st = dot(links[0], pieces[0][p])
+                for role in range(1, members):
+                    st = st + dot(links[role], pieces[role][p])
+                if not fresh:
+                    st = bstate[p] + st
+                if not last:
+                    bstate_out[p] = st
+                coef[p] = dot(lt[...], (STEP_SCALE * st).astype(BF16)).astype(BF16)
+
+    gains, _ = splits(nb, chans, hidden)
+
+    def norm_back(back, gain, unit):
+        prod = back * unit
+        low = back * gain
+        m1 = jnp.mean(low, axis=-1, keepdims=True)
+        m2 = jnp.mean(prod * gain, axis=-1, keepdims=True)
+        return prod, low - m1 - unit * m2
+
+    for rr in range(rows_blk):
+        row = i * rows_blk + rr
+        q = row_weight(plan, info, order, quad, row)
+        av2 = jnp.concatenate([avail[rr].astype(F32)] * 2, axis=0).astype(BF16)
+        if not first:
+            at = pl.ds(pl.multiple_of(row * waves, waves), waves)
+            rhs = jnp.concatenate([coef[0, at, :], coef[1, at, :]], axis=0)
+        grids = []
+        for c0 in range(0, lons, SUB):
+            cs = slice(rr * lons + c0, rr * lons + c0 + SUB)
+            dpred = q * dot(av2[:, c0 : c0 + SUB], gmask[...], ((0,), (0,)))
+            dout = STEP_SCALE * dpred
+            if not first:
+                dout = dout + q * dot(ffw_t[c0 : c0 + SUB, :], rhs)
+            dz = dout.astype(BF16)
+            u = units[cs, chans + hidden :]
+            d3[...] += dot((u * gains[2]).astype(BF16), dz, ((0,), (0,)))
+            dv[8:16, 2 * hidden :] += fold(dz.astype(F32))
+            prod, dx = norm_back(dot(dz, w3[...], ((1,), (1,))), gains[2], u)
+            dv[0:8, chans + hidden :] += fold(prod)
+            dz = (dx * slopes[cs, hidden:]).astype(BF16)
+            u = units[cs, chans : chans + hidden]
+            d2[...] += dot((u * gains[1]).astype(BF16), dz, ((0,), (0,)))
+            dv[8:16, hidden : 2 * hidden] += fold(dz.astype(F32))
+            prod, dx = norm_back(dot(dz, w2[...], ((1,), (1,))), gains[1], u)
+            dv[0:8, chans : chans + hidden] += fold(prod)
+            dz = (dx * slopes[cs, 0:hidden]).astype(BF16)
+            u = units[cs, 0:chans]
+            d1[...] += dot((u * gains[0]).astype(BF16), dz, ((0,), (0,)))
+            dv[8:16, 0:hidden] += fold(dz.astype(F32))
+            back = dot(dz, w1[...], ((1,), (1,)))
+            if last:
+                dv[0:8, 0:chans] += fold(back * u)
+            else:
+                prod, dx = norm_back(back, gains[0], u)
+                dv[0:8, 0:chans] += fold(prod)
+                grids.append((dpred + dx * scales[cs, 0:1]).astype(BF16))
+        if not last:
+            coeff = dot(inv[...], jnp.concatenate(grids, axis=0)).astype(BF16)
+            b_out[0, rr * waves : (rr + 1) * waves, :] = coeff[:waves]
+            b_out[1, rr * waves : (rr + 1) * waves, :] = coeff[waves:]
+
+    if last:
+
+        @pl.when(i == pl.num_programs(0) - 1)
+        def _():
+            half = packed.shape[1]
+            parts, at = packed_parts(plan)
+            for which, tile, start, count in parts:
+                for h, dst, src, n in both_halves(start, count, half):
+                    packed[h, dst : dst + n, :] = grads[which][src : src + n, tile * LANES : (tile + 1) * LANES]
+            for v in range(2):
+                line = jnp.sum(dv[v * 8 : v * 8 + 8, :], axis=0, keepdims=True)
+                for tile in range(line.shape[1] // LANES):
+                    row = at - half
+                    packed[1, row : row + 1, :] = line[:, tile * LANES : (tile + 1) * LANES]
+                    at += 1
+            tail = at - half
+            packed[1, tail:, :] = jnp.zeros((half - tail, LANES), F32)
+            mine[...] = packed[info[0]]
+            send[...] = packed[1 - info[0]]
+
+
+def backward_call(plan, step, chips, scalars, saved, avail, tgt, weights, nb, counts, tables, pieces, bstate, before):
+    group, rows, waves, degrees, steps, fields, chans, hidden, lons = plan
+    first, last = step == steps - 1, step == 0
+    rows_blk = pair_rows(plan)
+    blk = rows_blk * lons
+    links, lt, ffw_t, inv = tables
+    ins = [*saved, avail, tgt, *weights, nb, *counts]
+    if not first:
+        ins += [links, lt, ffw_t, *pieces]
+        if step != steps - 2:
+            ins.append(bstate)
+        ins += before
+    if not last:
+        ins.append(inv)
+    specs = [whole(a) for a in ins]
+    for n in range(3):
+        specs[n] = pl.BlockSpec((blk, saved[n].shape[1]), lambda i, *_: (i, 0))
+    specs[3] = pl.BlockSpec((rows_blk, fields, lons), lambda i, *_: (i, 0, 0))
+    sums = [((chans, hidden), F32), ((hidden, hidden), F32), ((hidden, chans), F32), ((16, chans + 2 * hidden), F32)]
+    scratch = [VM((2, rows * waves, chans), BF16), VM((2 * fields, chans), BF16)]
+    if last:
+        half = chips * packed_block(plan, chips)
+        scratch += [VM(*s) for s in sums] + [VM((2, half, LANES), F32)]
+        shapes = [jax.ShapeDtypeStruct((half, LANES), F32)] * 2
+        ospecs = [whole(a) for a in shapes]
+    else:
+        shapes = [jax.ShapeDtypeStruct(*s) for s in sums]
+        ospecs = [whole(a) for a in shapes]
+        shapes.append(jax.ShapeDtypeStruct((2, rows * waves, chans), BF16))
+        ospecs.append(pl.BlockSpec((2, rows_blk * waves, chans), lambda i, *_: (0, i, 0)))
+        if not first:
+            shapes.append(jax.ShapeDtypeStruct((2, waves * degrees, chans), F32))
+            ospecs.append(whole(shapes[-1]))
+    if first:
+        shapes.append(jax.ShapeDtypeStruct((8, LANES), F32))
+        ospecs.append(whole(shapes[-1]))
+    return pl.pallas_call(
+        partial(backward_kernel, plan, step),
+        out_shape=shapes,
+        grid_spec=pltpu.PrefetchScalarGridSpec(
+            num_scalar_prefetch=3,
+            grid=(rows // rows_blk,),
+            in_specs=specs,
+            out_specs=ospecs,
+            scratch_shapes=scratch,
+        ),
+        compiler_params=kernel_params(),
+        name=f"backward_{step}",
+    )(*scalars, *ins)
+
+
+def pairs_kernel(chips, group, mine, got, loss, out):
+    blk = mine.shape[0] // chips
+    share = loss[...] * (1.0 / group)
+    row = lax.broadcasted_iota(jnp.int32, share.shape, 0)
+    high = share.astype(BF16).astype(F32)
+    rest = share - high
+    mid = rest.astype(BF16).astype(F32)
+    lines = jnp.where(row == 0, high, jnp.where(row == 1, mid, jnp.where(row == 2, rest - mid, 0.0)))
+    lines = jnp.concatenate([lines, jnp.zeros_like(lines)], axis=0).astype(BF16)
+    for c in range(chips):
+        at = slice(c * blk, (c + 1) * blk)
+        out[c, 0:blk, :] = (mine[at, :] + got[at, :]).astype(BF16)
+        out[c, blk:, :] = lines
+
+
+def chips_kernel(got, out, loss):
+    chips, blk = out.shape[0], out.shape[1]
+    total = got[0].astype(F32)
+    for c in range(1, chips):
+        total = total + got[c].astype(F32)
+    low = total[0:blk].astype(BF16)
+    for c in range(chips):
+        out[c] = low
+    loss[...] = jnp.broadcast_to(jnp.sum(total[blk:], axis=0, keepdims=True), loss.shape)
+
+
+def update_kernel(plan, info, part, part_o, *refs):
+    params, means, squares = refs[0:4], refs[4:8], refs[8:12]
+    norm = refs[12]
+    masters, new_means, new_squares, halves = refs[13:17], refs[17:21], refs[21:25], refs[25:29]
+    packed = refs[29]
+    packed[info[0]] = part[...]
+    packed[1 - info[0]] = part_o[...]
+    half = packed.shape[1]
+    acc = jnp.zeros((16, LANES), F32)
+    for h in range(2):
+        g = packed[h].astype(F32)
+        acc = acc + jnp.sum((g * g).reshape(half // 16, 16, LANES), axis=0)
+    total = jnp.sum(jnp.sum(acc, axis=0, keepdims=True), axis=1, keepdims=True)
+    root = jnp.sqrt(jnp.broadcast_to(total, (8, LANES)))
+    norm[...] = root
+    factor = (CLIP_NORM / jnp.maximum(root, CLIP_NORM))[0:1, :]
+
+    def apply(which, rs, cs, g):
+        w, a, b = adamw(params[which][rs, cs], means[which][rs, cs], squares[which][rs, cs], g * factor)
+        masters[which][rs, cs] = w
+        new_means[which][rs, cs] = a
+        new_squares[which][rs, cs] = b
+        halves[which][rs, cs] = w.astype(BF16)
+
+    parts, at = packed_parts(plan)
+    for which, tile, start, count in parts:
+        for h, src, dst, n in both_halves(start, count, half):
+            apply(which, slice(dst, dst + n), slice(tile * LANES, (tile + 1) * LANES), packed[h, src : src + n, :].astype(F32))
+    tiles = (plan.chans + 2 * plan.hidden) // LANES
+    rows = packed[1, at - half : at - half + 2 * tiles, :].astype(F32)
+    for tile in range(tiles):
+        g = jnp.concatenate([rows[tile : tile + 1], rows[tiles + tile : tiles + tile + 1]], axis=0)
+        apply(3, slice(0, 2), slice(tile * LANES, (tile + 1) * LANES), g)
+
+
+def small_call(kernel, name, shapes, ins, scalars=(), scratch=()):
+    return pl.pallas_call(
+        kernel,
+        out_shape=shapes,
+        grid_spec=pltpu.PrefetchScalarGridSpec(
+            num_scalar_prefetch=len(scalars),
+            grid=(1,),
+            in_specs=[whole(a) for a in ins],
+            out_specs=[whole(a) for a in shapes],
+            scratch_shapes=list(scratch),
+        ),
+        compiler_params=kernel_params(),
+        name=name,
+    )(*scalars, *ins)
+
+
+def grouped_device(
+    plan,
+    chips,
+    spectral_state,
+    legendre,
+    wave_slots,
+    lat_order,
+    quad_weights,
+    available,
+    targets,
+    *flat,
+):
+    group, rows, waves, degrees, steps, fields, chans, hidden, lons = plan
+    params, means, squares = flat[0:4], flat[4:8], flat[8:12]
+    weights = [w.astype(BF16) for w in params[:3]]
+    nb = params[3]
+    tdev = spectral_state.shape[0]
+    copies = waves // chips
+    core = lax.axis_index("tm")
+    chip = lax.axis_index("lat")
+    member = chip % group
+    info = jnp.stack([core, member]).astype(jnp.int32)
+    swap = [(0, 1), (1, 0)]
+    across = lambda a: lax.ppermute(a, "tm", swap)
+
+    def to_members(a):
+        out = [a]
+        bit = 1
+        while bit < group:
+            out += [lax.ppermute(v, "lat", [(n, n ^ bit) for n in range(waves)]) for v in out]
+            bit *= 2
+        return out + [across(v) for v in out]
+
+    half = fields // 2
+    pad = -(2 * degrees + half + 1) % 8
+    high = spectral_state[:, 0].astype(BF16)
+    low = (spectral_state[:, 0] - high.astype(F32)).astype(BF16)
+    seen = available[:, :, 0].reshape(tdev, 2, half, lons).astype(BF16)
+    leg = jnp.broadcast_to(legendre.reshape(1, 1, 1, chans), (tdev, 2, 1, chans))
+    pack = jnp.concatenate([high, low, seen, leg, jnp.zeros((tdev, 2, pad, chans), BF16)], axis=2)
+    keep = lax.dynamic_index_in_dim(pack, core, axis=1, keepdims=False)
+    other = across(lax.dynamic_index_in_dim(pack, 1 - core, axis=1, keepdims=False))
+    times = jnp.concatenate([jnp.where(core == 0, keep, other), jnp.where(core == 0, other, keep)], axis=0)
+    spread = jnp.broadcast_to(times[None, :, None], (copies, 2 * tdev, group, *times.shape[1:]))
+    got = lax.all_to_all(spread.reshape(waves, *times.shape[1:]), "lat", split_axis=0, concat_axis=0, tiled=True)
+    got_o = across(got)
+
+    def table(scaled):
+        product = wave_slots[:, None] * jnp.arange(lons, dtype=jnp.int32)[None, :] % lons
+        phase = product.astype(F32) * (2.0 * math.pi / lons)
+        inverse = jnp.concatenate([jnp.cos(phase), -jnp.sin(phase)], axis=0)
+        if not scaled:
+            return inverse
+        scale = jnp.where(wave_slots == 0, 1.0, 2.0).astype(F32) / lons
+        return inverse * jnp.concatenate([scale, scale])[:, None]
+
+    inv32, ffw32 = table(False), table(True)
+    inv, ffw = inv32.astype(BF16), ffw32.astype(BF16)
+    state, links, lt, avail, nums, inv_t, ffw_t = prepare_call(
+        plan, info, wave_slots, lat_order, quad_weights, got, got_o, inv32, ffw32
+    )
+    theirs = across(targets)
+    tgt_all = jnp.concatenate([jnp.where(core == 0, targets, theirs), jnp.where(core == 0, theirs, targets)], axis=0)
+    tgt = lax.dynamic_index_in_dim(tgt_all, (chip // group) % (2 * tdev), axis=0, keepdims=False)
+    tgt = jnp.broadcast_to(tgt.reshape(steps * fields, 1), (steps * fields, LANES))
+    scalars = (info, lat_order, quad_weights)
+
+    saved, pieces = [], None
+    for s in range(steps):
+        units, slopes, scales, nums, *rest = forward_call(
+            plan, s, scalars, state, avail, nums, inv_t, ffw, lt, weights, nb, links, pieces
+        )
+        saved.append((units, slopes, scales))
+        if s < steps - 1:
+            pieces = to_members(rest[0])
+        if 0 < s < steps - 1:
+            state = rest[1]
+    counts = to_members(nums)
+    before, bstate, loss = None, None, None
+    for s in reversed(range(steps)):
+        out = backward_call(
+            plan, s, chips, scalars, saved[s], avail, tgt, weights, nb, counts, (links, lt, ffw_t, inv), pieces, bstate, before
+        )
+        if s > 0:
+            before = out[:4]
+            pieces = to_members(out[4])
+            if s == steps - 1:
+                loss = out[5]
+            else:
+                bstate = out[5]
+    mine, send = out
+    blk = mine.shape[0] // chips
+    groups = [[c * chips + n for n in range(chips)] for c in range(copies)]
+    exchange = lambda a: lax.all_to_all(a, "lat", split_axis=0, concat_axis=0, tiled=True, axis_index_groups=groups)
+    (parts,) = small_call(
+        partial(pairs_kernel, chips, group),
+        "pairs",
+        [jax.ShapeDtypeStruct((chips, blk + 16, LANES), BF16)],
+        [mine, across(send), loss],
+    )
+    reduced, loss = small_call(
+        chips_kernel,
+        "chips",
+        [jax.ShapeDtypeStruct((chips, blk, LANES), BF16), jax.ShapeDtypeStruct((8, LANES), F32)],
+        [exchange(parts)],
+    )
+    part = exchange(reduced).reshape(chips * blk, LANES)
+    shapes = [jax.ShapeDtypeStruct((8, LANES), F32)]
+    for kind in (F32, F32, F32, BF16):
+        shapes += [jax.ShapeDtypeStruct(w.shape, kind) for w in params]
+    norm, *results = small_call(
+        partial(update_kernel, plan),
+        "update",
+        shapes,
+        [part, across(part), *params, *means, *squares],
+        (info,),
+        [VM((2, chips * blk, LANES), BF16)],
+    )
+    return (loss[0, 0], norm[0, 0], *results)
+
+
+def make_plan(mesh, args):
+    state, legendre, _, _, _, available, targets, w_first = args[:8]
+    times, waves, _, degrees, chans = state.shape
+    _, fields, lats, lons = available.shape
+    hidden = w_first.shape[1]
+    cores, chips_all = mesh.shape["tm"], mesh.shape["lat"]
+    group = GROUP
+    chips = group * times
+    rows, rest = divmod(lats, 2 * group)
+    fits = (
+        cores == 2
+        and times % cores == 0
+        and chips_all == waves == lats
+        and waves % chips == 0
+        and rest == 0
+        and fields == 8
+        and lons == chans == degrees * lats
+        and waves % 16 == 0
+        and degrees % 16 == 0
+        and chans % LANES == 0
+        and hidden % LANES == 0
+        and lons % SUB == 0
+    )
+    if not fits or legendre.shape != (waves, degrees, lats):
+        return None
+    steps = targets.shape[1]
+    if steps < 3 or steps * rows * lons * (chans + 4 * hidden + LANES) * 4 > SAVED_LIMIT:
+        return None
+    return Plan(group, rows, waves, degrees, steps, fields, chans, hidden, lons), chips
+
+
 def solution(mesh):
     in_specs = (
         P("tm", "lat", None, None, None),
@@ -246,39 +961,11 @@
         P(),
         P("tm", None, "lat", None),
         P("tm", None, None),
-        P(),
-        P(),
-        P(),
-        P(),
-        P(),
-        P(),
-        P(),
-        P(),
-        P(),
-        P(),
-        P(),
-        P(),
-    )
-    out_specs = (
-        P(),
-        P(),
-        P(),
-        P(),
-        P(),
-        P(),
-        P(),
-        P(),
-        P(),
-        P(),
-        P(),
-        P(),
-        P(),
-        P(),
-        P(),
-        P(),
-        P(),
-        P(),
-    )
-    return jax.shard_map(
-        per_device, mesh=mesh, in_specs=in_specs, out_specs=out_specs, check_vma=False
-    )
+    ) + (P(),) * 12
+
+    def run(*args):
+        made = make_plan(mesh, args)
+        body = spread_device if made is None else partial(grouped_device, *made)
+        return jax.shard_map(body, mesh=mesh, in_specs=in_specs, out_specs=(P(),) * 18, check_vma=False)(*args)
+
+    return run

time: 499 us -> 181 us (0.36); the launches traced: 491 us -> 181 us
  blocking collectives: 135 us -> 21.1 us
  waiting for transfers between devices: 136 us -> 45.9 us
  Pallas kernels: 0 us -> 66.7 us
  matrix products: 61.3 us -> 0 us
  other arithmetic: 44.3 us -> 6.5 us
  local copies, waits for them, and re-layouts: 61.2 us -> 25.7 us
  starting transfers between devices: 33.6 us -> 13.6 us
  between operations: 20.5 us -> 1.08 us
    psum x1 -> x0, waiting for transfers between devices: 90 us -> none  [per_device(): grads = lax.psum(totals, ('tm', 'lat'))]
    psum x3 -> x0, blocking collectives: 84.3 us -> none  [the longest x1 42.5 us: per_device(): num_total, den_total = lax.psum((num_part, den_part), 'lat')]
    pallas_call x0 -> x12, Pallas kernels: none -> 66.7 us  [the longest x4 30.9 us: forward_call(): pl.pallas_call(partial(forward_kernel, plan, step), out_shape=shapes, gri...]
    dot_general x60 -> x0, matrix products: 61.3 us -> none  [the longest x12 31.7 us: corrector_forward(): jnp.dot(h_low, weights[k], preferred_element_type=jnp.float32)]
    ppermute x0 -> x26, waiting for transfers between devices: none -> 39 us  [the longest x7 24.9 us: to_members(): lax.ppermute(v, 'lat', [(n, n ^ bit) for n in range(waves)])]
    all_to_all x8 -> x1, waiting for transfers between devices: 45.8 us -> 6.89 us  [grouped_device(): lax.all_to_all(spread.reshape(waves, *times.shape[1:]), 'lat', split_axis...]
    all_to_all x5 -> x2, blocking collectives: 50.3 us -> 21.1 us  [grouped_device(): lax.all_to_all(a, 'lat', split_axis=0, concat_axis=0, tiled=True, axis_in...]
    reduce_sum x42 -> x0, other arithmetic: 26.3 us -> none  [the longest x9 7.92 us: corrector_backward(): bias_parts[k] = jnp.sum(grad_low, axis=0, dtype=jnp.float32)]
  transfers between devices with their start and end apart: 9 -> 27, of which waited for: 8 -> 19; matrix products, arithmetic and copies ran while one was open for 4% -> 3% of each run, Pallas kernels for 0% -> 4%
where the time goes in v1:
time: 181 us
  Pallas kernels  66.7 us (37%)
  waiting for transfers between devices  45.9 us (25%)
  local copies, waits for them, and re-layouts  25.7 us (14%)
  blocking collectives  21.1 us (12%)
  starting transfers between devices  13.6 us (8%)
  other arithmetic  6.5 us (4%)
    pallas_call x4, Pallas kernels, forward_call(): pl.pallas_call(partial(forward_kernel, plan, step), out_shape=shapes, gri...  30.9 us
    pallas_call x4, Pallas kernels, backward_call(): pl.pallas_call(partial(backward_kernel, plan, step), out_shape=shapes, gr...  30.8 us
    ppermute x7, waiting for transfers between devices, to_members(): lax.ppermute(v, 'lat', [(n, n ^ bit) for n in range(waves)])  24.9 us
    unnamed x76, local copies, waits for them, and re-layouts  22.9 us
    all_to_all x2, blocking collectives, grouped_device(): lax.all_to_all(a, 'lat', split_axis=0, concat_axis=0, tiled=True, axis_in...  21.1 us
    ppermute x19, waiting for transfers between devices, grouped_device(): across = lambda a: lax.ppermute(a, 'tm', swap)  14.1 us
    all_to_all x1, starting transfers between devices, grouped_device(): lax.all_to_all(spread.reshape(waves, *times.shape[1:]), 'lat', split_axis...  8.2 us
    all_to_all x1, waiting for transfers between devices, grouped_device(): lax.all_to_all(spread.reshape(waves, *times.shape[1:]), 'lat', split_axis...  6.89 us
  transfers between devices with their start and end apart: 27, of which 19 were waited for; matrix products, arithmetic and copies ran while one was open for 3% of the time, Pallas kernels for 4%

profile of v1, /device:TPU:0, one launch (start us, length us, event | category | flops | bytes accessed | tf_op | source)
XLA Modules:
  0.0 180.5 jit_solution(17862325053891629030)
XLA Ops:
  5.4 8.2 %all-to-all-start = ((bf16[16,40,256]{2,1,0:T(8,128)(2,1)}), bf16[16,40,256]{2,1,0:T(8,128)(2,1)S(1)}, u32[]{:S(2)}, u32[]{:S(2)}) async-start(bf16[16,40,256]{2,1,0:T(8,128)(2,1)} %bitcast.5), calls=%async_computation | async-start | bytes 655360 | tf_op jit(solution)/shard_map/all_to_all | solution.py:847
  18.3 6.9 %all-to-all-done.got = bf16[16,40,256]{2,1,0:T(8,128)(2,1)S(1)} async-done(((bf16[16,40,256]{2,1,0:T(8,128)(2,1)}), bf16[16,40,256]{2,1,0:T(8,128)(2,1)S(1)}, u32[]{:S(2)}, u32[]{:S(2)}) %all-to-all-start) | async-done | bytes 327712 | tf_op jit(solution)/shard_map/all_to_all | solution.py:847
  25.4 1.5 collective-permute-done.1.got_o
  30.2 7.2 %forward_0.1 = (f32[1024,1024]{1,0:T(8,128)S(1)}, f32[1024,768]{1,0:T(8,128)S(1)}, f32[1024,128]{1,0:T(8,128)S(1)}, f32[40,128]{1,0:T(8,128)S(1)}, bf16[2,64,256]{2,1,0:T(8,128)(2,1)S(1)}) custom-call(s32[2]{0:T(128)S(1)} %pad_add_fusion.info, s32[16]{0:T(128)S(1)} %copy-done.30, f32[16]{0:T(128)S(1)} %copy-done.32, ...), custom_call_target="tpu_custom_call" | custom-call | tf_op jit(solution)/shard_map/forward_0/pallas_call | solution.py:493
  37.4 2.0 %copy-done.6 = f32[1024,1024]{1,0:T(8,128)} copy-done((f32[1024,1024]{1,0:T(8,128)}, f32[1024,1024]{1,0:T(8,128)S(1)}, u32[]{:S(2)}) %copy-start.6) | copy-done | bytes 4194328
  39.4 1.6 copy-done.12
  41.6 3.7 %collective-permute-done.3.refs_12_ = bf16[2,64,256]{2,1,0:T(8,128)(2,1)S(1)} collective-permute-done((bf16[2,64,256]{2,1,0:T(8,128)(2,1)S(1)}, bf16[2,64,256]{2,1,0:T(8,128)(2,1)S(1)}, u32[]{:S(2)}, u32[]{:S(2)}) %collective-permute-start.3) | collective-permute-done | bytes 65568 | tf_op jit(solution)/shard_map/ppermute | solution.py:832
  46.5 7.9 %forward_1.1 = (f32[1024,1024]{1,0:T(8,128)S(1)}, f32[1024,768]{1,0:T(8,128)S(1)}, f32[1024,128]{1,0:T(8,128)S(1)}, f32[40,128]{1,0:T(8,128)S(1)}, bf16[2,64,256...) custom-call(s32[2]{0:T(128)S(1)} %pad_add_fusion.info, s32[16]{0:T(128)S(1)} %copy-done.30, f32[16]{0:T(128)S(1)} %copy-done.32, ...), custom_call_target="tpu_custom_call" | custom-call | tf_op jit(solution)/shard_map/forward_1/pallas_call | solution.py:493
  54.5 2.0 %copy-done.2 = f32[1024,1024]{1,0:T(8,128)} copy-done((f32[1024,1024]{1,0:T(8,128)}, f32[1024,1024]{1,0:T(8,128)S(1)}, u32[]{:S(2)}) %copy-start.2) | copy-done | bytes 4194328
  56.5 1.7 copy-done.14
  58.8 3.7 %collective-permute-done.6.refs_12_ = bf16[2,64,256]{2,1,0:T(8,128)(2,1)S(1)} collective-permute-done((bf16[2,64,256]{2,1,0:T(8,128)(2,1)S(1)}, bf16[2,64,256]{2,1,0:T(8,128)(2,1)S(1)}, u32[]{:S(2)}, u32[]{:S(2)}) %collective-permute-start.6) | collective-permute-done | bytes 65568 | tf_op jit(solution)/shard_map/ppermute | solution.py:832
  63.7 7.9 %forward_2.1 = (f32[1024,1024]{1,0:T(8,128)S(1)}, f32[1024,768]{1,0:T(8,128)S(1)}, f32[1024,128]{1,0:T(8,128)S(1)}, f32[40,128]{1,0:T(8,128)S(1)}, bf16[2,64,256...) custom-call(s32[2]{0:T(128)S(1)} %pad_add_fusion.info, s32[16]{0:T(128)S(1)} %copy-done.30, f32[16]{0:T(128)S(1)} %copy-done.32, ...), custom_call_target="tpu_custom_call" | custom-call | tf_op jit(solution)/shard_map/forward_2/pallas_call | solution.py:493
  71.6 2.1 %copy-done = f32[1024,1024]{1,0:T(8,128)} copy-done((f32[1024,1024]{1,0:T(8,128)}, f32[1024,1024]{1,0:T(8,128)S(1)}, u32[]{:S(2)}) %copy-start) | copy-done | bytes 4194328
  73.7 1.7 copy-done.8
  76.5 3.2 %collective-permute-done.9.refs_12_ = bf16[2,64,256]{2,1,0:T(8,128)(2,1)S(1)} collective-permute-done((bf16[2,64,256]{2,1,0:T(8,128)(2,1)S(1)}, bf16[2,64,256]{2,1,0:T(8,128)(2,1)S(1)}, u32[]{:S(2)}, u32[]{:S(2)}) %collective-permute-start.9) | collective-permute-done | bytes 65568 | tf_op jit(solution)/shard_map/ppermute | solution.py:832
  81.0 7.9 %forward_3.1 = (f32[1024,1024]{1,0:T(8,128)S(1)}, f32[1024,768]{1,0:T(8,128)S(1)}, f32[1024,128]{1,0:T(8,128)S(1)}, f32[40,128]{1,0:T(8,128)S(1)}) custom-call(s32[2]{0:T(128)S(1)} %pad_add_fusion.info, s32[16]{0:T(128)S(1)} %copy-done.31, f32[16]{0:T(128)S(1)} %copy-done.33, f32[2,256,256]{2,1,0:T(8,128)S(1)} %get-tuple-element.99.refs_0_, ...), custom_call_target="tpu_custom_call" | custom-call | tf_op jit(solution)/shard_map/forward_3/pallas_call | solution.py:493
  88.9 1.9 %copy-done.4 = f32[1024,1024]{1,0:T(8,128)} copy-done((f32[1024,1024]{1,0:T(8,128)}, f32[1024,1024]{1,0:T(8,128)S(1)}, u32[]{:S(2)}) %copy-start.4) | copy-done | bytes 4194328
  90.9 1.8 copy-done.10
  94.0 3.2 %collective-permute-done.12.refs_10_ = f32[40,128]{1,0:T(8,128)S(1)} collective-permute-done((f32[40,128]{1,0:T(8,128)S(1)}, f32[40,128]{1,0:T(8,128)S(1)}, u32[]{:S(2)}, u32[]{:S(2)}) %collective-permute-start.12) | collective-permute-done | bytes 20512 | tf_op jit(solution)/shard_map/ppermute | solution.py:832
  98.5 2.2 %copy-done.5 = f32[1024,1024]{1,0:T(8,128)S(1)} copy-done((f32[1024,1024]{1,0:T(8,128)S(1)}, f32[1024,1024]{1,0:T(8,128)}, u32[]{:S(2)}) %copy-start.5) | copy-done | bytes 4194328
  100.7 1.9 %copy-done.11 = f32[1024,768]{1,0:T(8,128)S(1)} copy-done((f32[1024,768]{1,0:T(8,128)S(1)}, f32[1024,768]{1,0:T(8,128)}, u32[]{:S(2)}) %copy-start.11) | copy-done | bytes 3145752
  103.6 7.2 %backward_3.1 = (f32[256,384]{1,0:T(8,128)S(1)}, f32[384,384]{1,0:T(8,128)S(1)}, f32[384,256]{1,0:T(8,128)S(1)}, f32[16,1024]{1,0:T(8,128)S(1)}, bf16[2,64,256]{2,1,0:T(8,128)(2,1)S(1)}, /*index=5*/f32[8,128]{1,0:T(8,128)S(1)}) custom-call(s32[2]{0:T(128)S(1)} %pad_add_fusion.info, s32[16]{0:T(128)S(1)} %copy-done.31, f32[16]{0:T(128)S(1)} %copy-done.33, ...), custom_call_target="tpu_custom_call" | custom-call | tf_op jit(solution)/shard_map/backward_3/pallas_call | solution.py:711
  111.4 3.7 %collective-permute-done.15.refs_17_ = bf16[2,64,256]{2,1,0:T(8,128)(2,1)S(1)} collective-permute-done((bf16[2,64,256]{2,1,0:T(8,128)(2,1)S(1)}, bf16[2,64,256]{2,1,0:T(8,128)(2,1)S(1)}, u32[]{:S(2)}, u32[]{:S(2)}) %collective-permute-start.15) | collective-permute-done | bytes 65568 | tf_op jit(solution)/shard_map/ppermute | solution.py:832
  116.3 8.0 %backward_2.1 = (f32[256,384]{1,0:T(8,128)S(1)}, f32[384,384]{1,0:T(8,128)S(1)}, f32[384,256]{1,0:T(8,128)S(1)}, f32[16,1024]{1,0:T(8,128)S(1)}, bf16[2,64,256]{...) custom-call(s32[2]{0:T(128)S(1)} %pad_add_fusion.info, s32[16]{0:T(128)S(1)} %copy-done.31, f32[16]{0:T(128)S(1)} %copy-done.33, ...), custom_call_target="tpu_custom_call" | custom-call | tf_op jit(solution)/shard_map/backward_2/pallas_call | solution.py:711
  125.0 3.7 %collective-permute-done.18.refs_17_ = bf16[2,64,256]{2,1,0:T(8,128)(2,1)S(1)} collective-permute-done((bf16[2,64,256]{2,1,0:T(8,128)(2,1)S(1)}, bf16[2,64,256]{2,1,0:T(8,128)(2,1)S(1)}, u32[]{:S(2)}, u32[]{:S(2)}) %collective-permute-start.18) | collective-permute-done | bytes 65568 | tf_op jit(solution)/shard_map/ppermute | solution.py:832
  130.0 8.0 %backward_1.1 = (f32[256,384]{1,0:T(8,128)S(1)}, f32[384,384]{1,0:T(8,128)S(1)}, f32[384,256]{1,0:T(8,128)S(1)}, f32[16,1024]{1,0:T(8,128)S(1)}, bf16[2,64,256]{...) custom-call(s32[2]{0:T(128)S(1)} %pad_add_fusion.info, s32[16]{0:T(128)S(1)} %copy-done.31, f32[16]{0:T(128)S(1)} %copy-done.33, ...), custom_call_target="tpu_custom_call" | custom-call | tf_op jit(solution)/shard_map/backward_1/pallas_call | solution.py:711
  138.6 3.7 %collective-permute-done.21.refs_17_ = bf16[2,64,256]{2,1,0:T(8,128)(2,1)S(1)} collective-permute-done((bf16[2,64,256]{2,1,0:T(8,128)(2,1)S(1)}, bf16[2,64,256]{2,1,0:T(8,128)(2,1)S(1)}, u32[]{:S(2)}, u32[]{:S(2)}) %collective-permute-start.21) | collective-permute-done | bytes 65568 | tf_op jit(solution)/shard_map/ppermute | solution.py:832
  143.7 7.6 %backward_0.1 = (f32[1408,128]{1,0:T(8,128)S(1)}, f32[1408,128]{1,0:T(8,128)S(1)}) custom-call(s32[2]{0:T(128)S(1)} %pad_add_fusion.info, s32[16]{0:T(128)S(1)} %copy-done.31, f32[16]{0:T(128)S(1)} %copy-done.33, f32[1024,1024]{1,0:T(8,128)S(1)} %copy-done.7, f32[1024,768]{1,0:T(8,128)S(1)} %copy-done.13, f32[1024,128]{1,0:T(8,128)S(1)} %get-tuple-element.92.refs_2_, ...), custom_call_target="tpu_custom_call" | custom-call | tf_op jit(solution)/shard_map/backward_0/pallas_call | solution.py:711
  151.5 2.0 %collective-permute-done.24.got = f32[1408,128]{1,0:T(8,128)S(1)} collective-permute-done((f32[1408,128]{1,0:T(8,128)S(1)}, f32[1408,128]{1,0:T(8,128)S(1)}, u32[]{:S(2)}, u32[]{:S(2)}) %collective-permute-start.24) | collective-permute-done | bytes 720928 | tf_op jit(solution)/shard_map/ppermute | solution.py:826
  153.6 11.2 %all_to_all.15.got = bf16[8,192,128]{2,1,0:T(8,128)(2,1)S(1)} all-to-all(bf16[8,192,128]{2,1,0:T(8,128)(2,1)S(1)} %pairs.1), channel_id=1, replica_groups={{0,1,2,3,4,5,6,7},{8,9,10,11,12,13,14,15},{16,17,18,19,20,21,22,23},{24..., dimensions={0} | all-to-all | bytes 786432 | tf_op jit(solution)/shard_map/all_to_all | solution.py:896
  164.9 9.9 %all_to_all.16 = bf16[8,176,128]{2,1,0:T(8,128)(2,1)S(1)} all-to-all(bf16[8,176,128]{2,1,0:T(8,128)(2,1)S(1)} %get-tuple-element.134), channel_id=1, replica_groups={{0,1,2,3,4,5,6,7},{8,9,10,11,12,13,14,15},{16,17,18,19,20,21,22,23},{24..., dimensions={0} | all-to-all | bytes 720896 | tf_op jit(solution)/shard_map/all_to_all | solution.py:896
  176.5 3.5 %update.1 = (f32[8,128]{1,0:T(8,128)S(1)}, f32[256,384]{1,0:T(8,128)}, f32[384,384]{1,0:T(8,128)}, f32[384,256]{1,0:T(8,128)}, f32[2,1024]{1,0:T(2,128)}, /*inde...) custom-call(s32[2]{0:T(128)S(1)} %pad_add_fusion.info, ...), custom_call_target="tpu_custom_call" | custom-call | tf_op jit(solution)/shard_map/update/pallas_call | solution.py:788
  (138 shorter events, 30.7 us)
Async XLA Ops:
  3.2 1.4 collective-permute-start
  5.4 19.8 %all-to-all-start = ((bf16[16,40,256]{2,1,0:T(8,128)(2,1)}), bf16[16,40,256]{2,1,0:T(8,128)(2,1)S(1)}, u32[]{:S(2)}, u32[]{:S(2)}) async-start(bf16[16,40,256]{2,1,0:T(8,128)(2,1)} %bitcast.5), calls=%async_computation | async-start | bytes 655360 | tf_op jit(solution)/shard_map/all_to_all | solution.py:847
  13.6 62.5 %copy-start.37 = (f32[2,4,8]{2,1,0:T(4,128)S(1)}, f32[2,4,8]{2,1,0:T(4,128)}, u32[]{:S(2)}) copy-start(f32[2,4,8]{2,1,0:T(4,128)} %param.25) | copy-start | bytes 772
  13.6 67.4 %copy-start.31 = (s32[16]{0:T(128)S(1)}, s32[16]{0:T(128)}, u32[]{:S(2)}) copy-start(s32[16]{0:T(128)} %order.17) | copy-start | bytes 196
  13.6 67.4 %copy-start.33 = (f32[16]{0:T(128)S(1)}, f32[16]{0:T(128)}, u32[]{:S(2)}) copy-start(f32[16]{0:T(128)} %quad.17) | copy-start | bytes 196
  25.2 1.6 collective-permute-start.1
  41.0 4.3 %collective-permute-start.3 = (bf16[2,64,256]{2,1,0:T(8,128)(2,1)S(1)}, bf16[2,64,256]{2,1,0:T(8,128)(2,1)S(1)}, u32[]{:S(2)}, u32[]{:S(2)}) collective-permute-start(bf16[2,64,256]{2,1,0:T(8,128)(2,1)S(1)} %get-tuple-element.95.refs_11_), channel_id=1, source_target_pairs={{0,1},{1,0},{2,3},{3,2},{4,5},{5,4},{6,7},{7,6},{8,9},{9,8},{10,11... | collective-permute-start | bytes 196616 | tf_op jit(solution)/shard_map/ppermute | solution.py:832
  41.6 3.7 %collective-permute-start.4 = (bf16[2,64,256]{2,1,0:T(8,128)(2,1)S(1)}, bf16[2,64,256]{2,1,0:T(8,128)(2,1)S(1)}, u32[]{:S(2)}, u32[]{:S(2)}) collective-permute-start(bf16[2,64,256]{2,1,0:T(8,128)(2,1)S(1)} %get-tuple-element.95.refs_11_), channel_id=1, source_target_pairs={{0,16},{16,0},{1,17},{17,1},{2,18},{18,2},{3,19},{19,3},{4,20},{20... | collective-permute-start | bytes 196616 | tf_op jit(solution)/shard_map/ppermute | solution.py:826
  45.3 1.3 collective-permute-start.5
  58.2 4.3 %collective-permute-start.6 = (bf16[2,64,256]{2,1,0:T(8,128)(2,1)S(1)}, bf16[2,64,256]{2,1,0:T(8,128)(2,1)S(1)}, u32[]{:S(2)}, u32[]{:S(2)}) collective-permute-start(bf16[2,64,256]{2,1,0:T(8,128)(2,1)S(1)} %get-tuple-element.98.refs_11_), channel_id=1, source_target_pairs={{0,1},{1,0},{2,3},{3,2},{4,5},{5,4},{6,7},{7,6},{8,9},{9,8},{10,11... | collective-permute-start | bytes 196616 | tf_op jit(solution)/shard_map/ppermute | solution.py:832
  58.8 3.7 %collective-permute-start.7 = (bf16[2,64,256]{2,1,0:T(8,128)(2,1)S(1)}, bf16[2,64,256]{2,1,0:T(8,128)(2,1)S(1)}, u32[]{:S(2)}, u32[]{:S(2)}) collective-permute-start(bf16[2,64,256]{2,1,0:T(8,128)(2,1)S(1)} %get-tuple-element.98.refs_11_), channel_id=1, source_target_pairs={{0,16},{16,0},{1,17},{17,1},{2,18},{18,2},{3,19},{19,3},{4,20},{20... | collective-permute-start | bytes 196616 | tf_op jit(solution)/shard_map/ppermute | solution.py:826
  62.5 1.3 collective-permute-start.8
  75.5 4.3 %collective-permute-start.9 = (bf16[2,64,256]{2,1,0:T(8,128)(2,1)S(1)}, bf16[2,64,256]{2,1,0:T(8,128)(2,1)S(1)}, u32[]{:S(2)}, u32[]{:S(2)}) collective-permute-start(bf16[2,64,256]{2,1,0:T(8,128)(2,1)S(1)} %get-tuple-element.101.refs_11_), channel_id=1, source_target_pairs={{0,1},{1,0},{2,3},{3,2},{4,5},{5,4},{6,7},{7,6},{8,9},{9,8},{10,11... | collective-permute-start | bytes 196616 | tf_op jit(solution)/shard_map/ppermute | solution.py:832
  76.0 18.0 %collective-permute-start.2 = (f32[2,4,8]{2,1,0:T(4,128)S(1)}, f32[2,4,8]{2,1,0:T(4,128)S(1)}, u32[]{:S(2)}, u32[]{:S(2)}) collective-permute-start(f32[2,4,8]{2,1,0:T(4,128)S(1)} %copy-done.37), channel_id=1, source_target_pairs={{0,16},{16,0},{1,17},{17,1},{2,18},{18,2},{3,19},{19,3},{4,20},{20... | collective-permute-start | bytes 776 | tf_op jit(solution)/shard_map/ppermute | solution.py:826
  76.0 3.7 %collective-permute-start.10 = (bf16[2,64,256]{2,1,0:T(8,128)(2,1)S(1)}, bf16[2,64,256]{2,1,0:T(8,128)(2,1)S(1)}, u32[]{:S(2)}, u32[]{:S(2)}) collective-permute-start(bf16[2,64,256]{2,1,0:T(8,128)(2,1)S(1)} %get-tuple-element.101.refs_11_), channel_id=1, source_target_pairs={{0,16},{16,0},{1,17},{17,1},{2,18},{18,2},{3,19},{19,3},{4,20},{20... | collective-permute-start | bytes 196616 | tf_op jit(solution)/shard_map/ppermute | solution.py:826
  79.7 1.3 collective-permute-start.11
  93.4 3.8 %collective-permute-start.12 = (f32[40,128]{1,0:T(8,128)S(1)}, f32[40,128]{1,0:T(8,128)S(1)}, u32[]{:S(2)}, u32[]{:S(2)}) collective-permute-start(f32[40,128]{1,0:T(8,128)S(1)} %get-tuple-element.102.refs_9_), channel_id=1, source_target_pairs={{0,1},{1,0},{2,3},{3,2},{4,5},{5,4},{6,7},{7,6},{8,9},{9,8},{10,11... | collective-permute-start | bytes 61448 | tf_op jit(solution)/shard_map/ppermute | solution.py:832
  94.0 3.3 %collective-permute-start.13 = (f32[40,128]{1,0:T(8,128)S(1)}, f32[40,128]{1,0:T(8,128)S(1)}, u32[]{:S(2)}, u32[]{:S(2)}) collective-permute-start(f32[40,128]{1,0:T(8,128)S(1)} %get-tuple-element.102.refs_9_), channel_id=1, source_target_pairs={{0,16},{16,0},{1,17},{17,1},{2,18},{18,2},{3,19},{19,3},{4,20},{20... | collective-permute-start | bytes 61448 | tf_op jit(solution)/shard_map/ppermute | solution.py:826
  97.2 1.2 collective-permute-start.14
  110.8 4.3 %collective-permute-start.15 = (bf16[2,64,256]{2,1,0:T(8,128)(2,1)S(1)}, bf16[2,64,256]{2,1,0:T(8,128)(2,1)S(1)}, u32[]{:S(2)}, u32[]{:S(2)}) collective-permute-start(bf16[2,64,256]{2,1,0:T(8,128)(2,1)S(1)} %get-tuple-element.113.refs_16_), channel_id=1, source_target_pairs={{0,1},{1,0},{2,3},{3,2},{4,5},{5,4},{6,7},{7,6},{8,9},{9,8},{10,11... | collective-permute-start | bytes 196616 | tf_op jit(solution)/shard_map/ppermute | solution.py:832
  111.4 3.7 %collective-permute-start.16 = (bf16[2,64,256]{2,1,0:T(8,128)(2,1)S(1)}, bf16[2,64,256]{2,1,0:T(8,128)(2,1)S(1)}, u32[]{:S(2)}, u32[]{:S(2)}) collective-permute-start(bf16[2,64,256]{2,1,0:T(8,128)(2,1)S(1)} %get-tuple-element.113.refs_16_), channel_id=1, source_target_pairs={{0,16},{16,0},{1,17},{17,1},{2,18},{18,2},{3,19},{19,3},{4,20},{20... | collective-permute-start | bytes 196616 | tf_op jit(solution)/shard_map/ppermute | solution.py:826
  115.1 1.3 collective-permute-start.17
  124.4 4.3 %collective-permute-start.18 = (bf16[2,64,256]{2,1,0:T(8,128)(2,1)S(1)}, bf16[2,64,256]{2,1,0:T(8,128)(2,1)S(1)}, u32[]{:S(2)}, u32[]{:S(2)}) collective-permute-start(bf16[2,64,256]{2,1,0:T(8,128)(2,1)S(1)} %get-tuple-element.118.refs_16_), channel_id=1, source_target_pairs={{0,1},{1,0},{2,3},{3,2},{4,5},{5,4},{6,7},{7,6},{8,9},{9,8},{10,11... | collective-permute-start | bytes 196616 | tf_op jit(solution)/shard_map/ppermute | solution.py:832
  125.0 3.7 %collective-permute-start.19 = (bf16[2,64,256]{2,1,0:T(8,128)(2,1)S(1)}, bf16[2,64,256]{2,1,0:T(8,128)(2,1)S(1)}, u32[]{:S(2)}, u32[]{:S(2)}) collective-permute-start(bf16[2,64,256]{2,1,0:T(8,128)(2,1)S(1)} %get-tuple-element.118.refs_16_), channel_id=1, source_target_pairs={{0,16},{16,0},{1,17},{17,1},{2,18},{18,2},{3,19},{19,3},{4,20},{20... | collective-permute-start | bytes 196616 | tf_op jit(solution)/shard_map/ppermute | solution.py:826
  128.7 1.3 collective-permute-start.20
  138.0 4.3 %collective-permute-start.21 = (bf16[2,64,256]{2,1,0:T(8,128)(2,1)S(1)}, bf16[2,64,256]{2,1,0:T(8,128)(2,1)S(1)}, u32[]{:S(2)}, u32[]{:S(2)}) collective-permute-start(bf16[2,64,256]{2,1,0:T(8,128)(2,1)S(1)} %get-tuple-element.124.refs_16_), channel_id=1, source_target_pairs={{0,1},{1,0},{2,3},{3,2},{4,5},{5,4},{6,7},{7,6},{8,9},{9,8},{10,11... | collective-permute-start | bytes 196616 | tf_op jit(solution)/shard_map/ppermute | solution.py:832
  138.6 3.7 %collective-permute-start.22 = (bf16[2,64,256]{2,1,0:T(8,128)(2,1)S(1)}, bf16[2,64,256]{2,1,0:T(8,128)(2,1)S(1)}, u32[]{:S(2)}, u32[]{:S(2)}) collective-permute-start(bf16[2,64,256]{2,1,0:T(8,128)(2,1)S(1)} %get-tuple-element.124.refs_16_), channel_id=1, source_target_pairs={{0,16},{16,0},{1,17},{17,1},{2,18},{18,2},{3,19},{19,3},{4,20},{20... | collective-permute-start | bytes 196616 | tf_op jit(solution)/shard_map/ppermute | solution.py:826
  142.3 1.3 collective-permute-start.23
  143.6 32.8 %copy-start.16 = (f32[384,384]{1,0:T(8,128)S(1)}, f32[384,384]{1,0:T(8,128)}, u32[]{:S(2)}) copy-start(f32[384,384]{1,0:T(8,128)} %refs_1_.1) | copy-start | bytes 1769476
  143.6 32.8 %copy-start.17 = (f32[256,384]{1,0:T(8,128)S(1)}, f32[256,384]{1,0:T(8,128)}, u32[]{:S(2)}) copy-start(f32[256,384]{1,0:T(8,128)} %refs_0_.1) | copy-start | bytes 1179652
  151.3 2.3 %collective-permute-start.24 = (f32[1408,128]{1,0:T(8,128)S(1)}, f32[1408,128]{1,0:T(8,128)S(1)}, u32[]{:S(2)}, u32[]{:S(2)}) collective-permute-start(f32[1408,128]{1,0:T(8,128)S(1)} %get-tuple-element.131), channel_id=1, source_target_pairs={{0,16},{16,0},{1,17},{17,1},{2,18},{18,2},{3,19},{19,3},{4,20},{20... | collective-permute-start | bytes 2162696 | tf_op jit(solution)/shard_map/ppermute | solution.py:826
  174.7 1.7 collective-permute-start.25
  (33 other events, 454.7 us)

commit v2 on v1

--- a/solution.py
+++ b/solution.py
@@ -247,7 +247,7 @@
 GROUP = 2
 SUB = 256
 ROWS_BLOCK = 2
-VMEM_LIMIT = 30 << 20
+VMEM_LIMIT = 10 << 20
 SAVED_LIMIT = 96 << 20
 
 
@@ -299,7 +299,9 @@
     return quad[order[(info[1] * 2 + info[0]) * plan.rows + row]]
 
 
-def prepare_kernel(plan, info, slots, order, quad, got, got_o, inv, ffw, state, links, lt, avail, nums, table, ffw_t):
+def prepare_kernel(
+    plan, info, slots, order, quad, got, got_o, inv, ffw, wanted, state, links, lt, avail, nums, table, ffw_t, tgt
+):
     group, rows, waves, degrees, steps, fields, chans, _, _ = plan
     members = 2 * group
     core, member = info[0], info[1]
@@ -360,12 +362,13 @@
     nums[steps * fields :, :] = jnp.broadcast_to(jnp.sum(den, axis=1, keepdims=True), (fields, nums.shape[1]))
     table[...] = inv[...].T.astype(BF16)
     ffw_t[...] = ffw[...].T.astype(BF16)
-
-
-def prepare_call(plan, info, slots, order, quad, got, got_o, inv, ffw):
+    tgt[...] = wanted[...]
+
+
+def prepare_call(plan, info, slots, order, quad, got, got_o, inv, ffw, wanted):
     group, rows, waves, degrees, steps, fields, chans, _, lons = plan
     span, mine = waves * degrees, rows * waves
-    ins = [got, got_o, inv, ffw]
+    ins = [got, got_o, inv, ffw, wanted]
     shapes = [
         jax.ShapeDtypeStruct((2, span, chans), F32),
         jax.ShapeDtypeStruct((2 * group, span, mine), BF16),
@@ -374,6 +377,7 @@
         jax.ShapeDtypeStruct(((steps + 1) * fields, LANES), F32),
         jax.ShapeDtypeStruct((lons, 2 * waves), BF16),
         jax.ShapeDtypeStruct((lons, 2 * waves), BF16),
+        jax.ShapeDtypeStruct(wanted.shape, F32),
     ]
     return pl.pallas_call(
         partial(prepare_kernel, plan),
@@ -433,7 +437,7 @@
         q = row_weight(plan, info, order, quad, row)
         highs, lows, tends = [], [], []
         for c0 in range(0, lons, SUB):
-            cs = slice(rr * lons + c0, rr * lons + c0 + SUB)
+            cs = pl.ds(pl.multiple_of(row * lons + c0, SUB), SUB)
             grid = dot(table[c0 : c0 + SUB, :], rhs)
             u1, s1 = norm_unit(grid, EPS_NORM)
             units[cs, 0:chans] = u1
@@ -480,8 +484,8 @@
     specs[1] = pl.BlockSpec((rows_blk, fields, lons), lambda i, *_: (i, 0, 0))
     shapes, ospecs = [], []
     for width in (chans + 2 * hidden, 2 * hidden, LANES):
-        shapes.append(jax.ShapeDtypeStruct((cols, width), F32))
-        ospecs.append(pl.BlockSpec((blk, width), lambda i, *_: (i, 0)))
+        shapes.append(VM((cols, width), F32))
+        ospecs.append(pl.BlockSpec(memory_space=VM))
     shapes.append(jax.ShapeDtypeStruct(nums.shape, F32))
     ospecs.append(whole(nums))
     if not last:
@@ -618,7 +622,7 @@
             rhs = jnp.concatenate([coef[0, at, :], coef[1, at, :]], axis=0)
         grids = []
         for c0 in range(0, lons, SUB):
-            cs = slice(rr * lons + c0, rr * lons + c0 + SUB)
+            cs = pl.ds(pl.multiple_of(row * lons + c0, SUB), SUB)
             dpred = q * dot(av2[:, c0 : c0 + SUB], gmask[...], ((0,), (0,)))
             dout = STEP_SCALE * dpred
             if not first:
@@ -688,7 +692,7 @@
         ins.append(inv)
     specs = [whole(a) for a in ins]
     for n in range(3):
-        specs[n] = pl.BlockSpec((blk, saved[n].shape[1]), lambda i, *_: (i, 0))
+        specs[n] = pl.BlockSpec(memory_space=VM)
     specs[3] = pl.BlockSpec((rows_blk, fields, lons), lambda i, *_: (i, 0, 0))
     sums = [((chans, hidden), F32), ((hidden, hidden), F32), ((hidden, chans), F32), ((16, chans + 2 * hidden), F32)]
     scratch = [VM((2, rows * waves, chans), BF16), VM((2 * fields, chans), BF16)]
@@ -858,13 +862,13 @@
 
     inv32, ffw32 = table(False), table(True)
     inv, ffw = inv32.astype(BF16), ffw32.astype(BF16)
-    state, links, lt, avail, nums, inv_t, ffw_t = prepare_call(
-        plan, info, wave_slots, lat_order, quad_weights, got, got_o, inv32, ffw32
-    )
     theirs = across(targets)
     tgt_all = jnp.concatenate([jnp.where(core == 0, targets, theirs), jnp.where(core == 0, theirs, targets)], axis=0)
     tgt = lax.dynamic_index_in_dim(tgt_all, (chip // group) % (2 * tdev), axis=0, keepdims=False)
     tgt = jnp.broadcast_to(tgt.reshape(steps * fields, 1), (steps * fields, LANES))
+    state, links, lt, avail, nums, inv_t, ffw_t, tgt = prepare_call(
+        plan, info, wave_slots, lat_order, quad_weights, got, got_o, inv32, ffw32, tgt
+    )
     scalars = (info, lat_order, quad_weights)
 
     saved, pieces = [], None

time: 181 us -> 159 us (0.88)
  local copies, waits for them, and re-layouts: 25.7 us -> 2.85 us
    unnamed x76 -> x30, local copies, waits for them, and re-layouts: 22.9 us -> 0.08 us
  transfers between devices with their start and end apart: 27 -> 27, of which waited for: 19 -> 19; matrix products, arithmetic and copies ran while one was open for 3% -> 6% of each run, Pallas kernels for 4% -> 0%
where the time goes in v2:
time: 159 us; the launch traced here: 158 us
  Pallas kernels  66.4 us (42%)
  waiting for transfers between devices  46.3 us (29%)
  blocking collectives  21.1 us (13%)
  starting transfers between devices  13.2 us (8%)
  other arithmetic  7.18 us (5%)
  local copies, waits for them, and re-layouts  2.85 us (2%)
    pallas_call x4, Pallas kernels, forward_call(): pl.pallas_call(partial(forward_kernel, plan, step), out_shape=shapes, gri...  30.9 us
    pallas_call x4, Pallas kernels, backward_call(): pl.pallas_call(partial(backward_kernel, plan, step), out_shape=shapes, gr...  30.5 us
    ppermute x7, waiting for transfers between devices, to_members(): lax.ppermute(v, 'lat', [(n, n ^ bit) for n in range(waves)])  25.4 us
    all_to_all x2, blocking collectives, grouped_device(): lax.all_to_all(a, 'lat', split_axis=0, concat_axis=0, tiled=True, axis_in...  21.1 us
    ppermute x19, waiting for transfers between devices, grouped_device(): across = lambda a: lax.ppermute(a, 'tm', swap)  13.3 us
    all_to_all x1, starting transfers between devices, grouped_device(): lax.all_to_all(spread.reshape(waves, *times.shape[1:]), 'lat', split_axis...  8.01 us
    all_to_all x1, waiting for transfers between devices, grouped_device(): lax.all_to_all(spread.reshape(waves, *times.shape[1:]), 'lat', split_axis...  7.63 us
    ppermute x7, starting transfers between devices, to_members(): lax.ppermute(v, 'lat', [(n, n ^ bit) for n in range(waves)])  4.31 us
  transfers between devices with their start and end apart: 27, of which 19 were waited for; matrix products, arithmetic and copies ran while one was open for 6% of the time, Pallas kernels for 0%

profile of v2, /device:TPU:0, one launch (start us, length us, event | category | flops | bytes accessed | tf_op | source)
XLA Modules:
  0.0 158.0 jit_solution(3338927206516473890)
XLA Ops:
  5.8 8.0 %all-to-all-start = ((bf16[16,40,256]{2,1,0:T(8,128)(2,1)}), bf16[16,40,256]{2,1,0:T(8,128)(2,1)S(1)}, u32[]{:S(2)}, u32[]{:S(2)}) async-start(bf16[16,40,256]{2,1,0:T(8,128)(2,1)} %bitcast.5), calls=%async_computation | async-start | bytes 655360 | tf_op jit(solution)/shard_map/all_to_all | solution.py:851
  13.9 1.0 convert_element_type.41.refs_6_.refs_5_
  16.9 1.1 convert_element_type.42.refs_7_.refs_6_
  18.0 7.6 %all-to-all-done.got = bf16[16,40,256]{2,1,0:T(8,128)(2,1)S(1)} async-done(((bf16[16,40,256]{2,1,0:T(8,128)(2,1)}), bf16[16,40,256]{2,1,0:T(8,128)(2,1)S(1)}, u32[]{:S(2)}, u32[]{:S(2)}) %all-to-all-start) | async-done | bytes 327712 | tf_op jit(solution)/shard_map/all_to_all | solution.py:851
  27.4 1.4 prepare.1
  28.8 7.2 %forward_0.1 = (f32[1024,1024]{1,0:T(8,128)S(1)}, f32[1024,768]{1,0:T(8,128)S(1)}, f32[1024,128]{1,0:T(8,128)S(1)}, f32[40,128]{1,0:T(8,128)S(1)}, bf16[2,64,256]{2,1,0:T(8,128)(2,1)S(1)}) custom-call(s32[2]{0:T(128)S(1)} %pad_add_fusion.info, s32[16]{0:T(128)S(1)} %copy-done.10, f32[16]{0:T(128)S(1)} %copy-done.11, ...), custom_call_target="tpu_custom_call" | custom-call | tf_op jit(solution)/shard_map/forward_0/pallas_call | solution.py:497
  36.6 3.7 %collective-permute-done.3.refs_12_ = bf16[2,64,256]{2,1,0:T(8,128)(2,1)S(1)} collective-permute-done((bf16[2,64,256]{2,1,0:T(8,128)(2,1)S(1)}, bf16[2,64,256]{2,1,0:T(8,128)(2,1)S(1)}, u32[]{:S(2)}, u32[]{:S(2)}) %collective-permute-start.3) | collective-permute-done | bytes 65568 | tf_op jit(solution)/shard_map/ppermute | solution.py:836
  40.3 1.2 collective-permute-done.5.refs_14_
  41.5 7.9 %forward_1.1 = (f32[1024,1024]{1,0:T(8,128)S(1)}, f32[1024,768]{1,0:T(8,128)S(1)}, f32[1024,128]{1,0:T(8,128)S(1)}, f32[40,128]{1,0:T(8,128)S(1)}, bf16[2,64,256...) custom-call(s32[2]{0:T(128)S(1)} %pad_add_fusion.info, s32[16]{0:T(128)S(1)} %copy-done.10, f32[16]{0:T(128)S(1)} %copy-done.11, ...), custom_call_target="tpu_custom_call" | custom-call | tf_op jit(solution)/shard_map/forward_1/pallas_call | solution.py:497
  50.0 3.7 %collective-permute-done.6.refs_12_ = bf16[2,64,256]{2,1,0:T(8,128)(2,1)S(1)} collective-permute-done((bf16[2,64,256]{2,1,0:T(8,128)(2,1)S(1)}, bf16[2,64,256]{2,1,0:T(8,128)(2,1)S(1)}, u32[]{:S(2)}, u32[]{:S(2)}) %collective-permute-start.6) | collective-permute-done | bytes 65568 | tf_op jit(solution)/shard_map/ppermute | solution.py:836
  53.8 1.2 collective-permute-done.8.refs_14_
  55.0 7.9 %forward_2.1 = (f32[1024,1024]{1,0:T(8,128)S(1)}, f32[1024,768]{1,0:T(8,128)S(1)}, f32[1024,128]{1,0:T(8,128)S(1)}, f32[40,128]{1,0:T(8,128)S(1)}, bf16[2,64,256...) custom-call(s32[2]{0:T(128)S(1)} %pad_add_fusion.info, s32[16]{0:T(128)S(1)} %copy-done.10, f32[16]{0:T(128)S(1)} %copy-done.11, ...), custom_call_target="tpu_custom_call" | custom-call | tf_op jit(solution)/shard_map/forward_2/pallas_call | solution.py:497
  63.5 3.7 %collective-permute-done.9.refs_12_ = bf16[2,64,256]{2,1,0:T(8,128)(2,1)S(1)} collective-permute-done((bf16[2,64,256]{2,1,0:T(8,128)(2,1)S(1)}, bf16[2,64,256]{2,1,0:T(8,128)(2,1)S(1)}, u32[]{:S(2)}, u32[]{:S(2)}) %collective-permute-start.9) | collective-permute-done | bytes 65568 | tf_op jit(solution)/shard_map/ppermute | solution.py:836
  67.2 1.2 collective-permute-done.11.refs_14_
  68.5 7.9 %forward_3.1 = (f32[1024,1024]{1,0:T(8,128)S(1)}, f32[1024,768]{1,0:T(8,128)S(1)}, f32[1024,128]{1,0:T(8,128)S(1)}, f32[40,128]{1,0:T(8,128)S(1)}) custom-call(s32[2]{0:T(128)S(1)} %pad_add_fusion.info, s32[16]{0:T(128)S(1)} %copy-done.10, f32[16]{0:T(128)S(1)} %copy-done.11, f32[2,256,256]{2,1,0:T(8,128)S(1)} %get-tuple-element.101.refs_0_, ...), custom_call_target="tpu_custom_call" | custom-call | tf_op jit(solution)/shard_map/forward_3/pallas_call | solution.py:497
  77.0 3.2 %collective-permute-done.12.refs_10_ = f32[40,128]{1,0:T(8,128)S(1)} collective-permute-done((f32[40,128]{1,0:T(8,128)S(1)}, f32[40,128]{1,0:T(8,128)S(1)}, u32[]{:S(2)}, u32[]{:S(2)}) %collective-permute-start.12) | collective-permute-done | bytes 20512 | tf_op jit(solution)/shard_map/ppermute | solution.py:836
  80.2 1.2 collective-permute-done.14.refs_12_
  81.4 7.2 %backward_3.1 = (f32[256,384]{1,0:T(8,128)S(1)}, f32[384,384]{1,0:T(8,128)S(1)}, f32[384,256]{1,0:T(8,128)S(1)}, f32[16,1024]{1,0:T(8,128)S(1)}, bf16[2,64,256]{2,1,0:T(8,128)(2,1)S(1)}, /*index=5*/f32[8,128]{1,0:T(8,128)S(1)}) custom-call(s32[2]{0:T(128)S(1)} %pad_add_fusion.info, s32[16]{0:T(128)S(1)} %copy-done.10, f32[16]{0:T(128)S(1)} %copy-done.11, ...), custom_call_target="tpu_custom_call" | custom-call | tf_op jit(solution)/shard_map/backward_3/pallas_call | solution.py:715
  89.2 3.7 %collective-permute-done.15.refs_17_ = bf16[2,64,256]{2,1,0:T(8,128)(2,1)S(1)} collective-permute-done((bf16[2,64,256]{2,1,0:T(8,128)(2,1)S(1)}, bf16[2,64,256]{2,1,0:T(8,128)(2,1)S(1)}, u32[]{:S(2)}, u32[]{:S(2)}) %collective-permute-start.15) | collective-permute-done | bytes 65568 | tf_op jit(solution)/shard_map/ppermute | solution.py:836
  92.9 1.2 collective-permute-done.17.refs_19_
  94.2 8.0 %backward_2.1 = (f32[256,384]{1,0:T(8,128)S(1)}, f32[384,384]{1,0:T(8,128)S(1)}, f32[384,256]{1,0:T(8,128)S(1)}, f32[16,1024]{1,0:T(8,128)S(1)}, bf16[2,64,256]{...) custom-call(s32[2]{0:T(128)S(1)} %pad_add_fusion.info, s32[16]{0:T(128)S(1)} %copy-done.10, f32[16]{0:T(128)S(1)} %copy-done.11, ...), custom_call_target="tpu_custom_call" | custom-call | tf_op jit(solution)/shard_map/backward_2/pallas_call | solution.py:715
  102.8 3.7 %collective-permute-done.18.refs_17_ = bf16[2,64,256]{2,1,0:T(8,128)(2,1)S(1)} collective-permute-done((bf16[2,64,256]{2,1,0:T(8,128)(2,1)S(1)}, bf16[2,64,256]{2,1,0:T(8,128)(2,1)S(1)}, u32[]{:S(2)}, u32[]{:S(2)}) %collective-permute-start.18) | collective-permute-done | bytes 65568 | tf_op jit(solution)/shard_map/ppermute | solution.py:836
  106.5 1.2 collective-permute-done.20.refs_19_
  107.7 8.0 %backward_1.1 = (f32[256,384]{1,0:T(8,128)S(1)}, f32[384,384]{1,0:T(8,128)S(1)}, f32[384,256]{1,0:T(8,128)S(1)}, f32[16,1024]{1,0:T(8,128)S(1)}, bf16[2,64,256]{...) custom-call(s32[2]{0:T(128)S(1)} %pad_add_fusion.info, s32[16]{0:T(128)S(1)} %copy-done.10, f32[16]{0:T(128)S(1)} %copy-done.11, ...), custom_call_target="tpu_custom_call" | custom-call | tf_op jit(solution)/shard_map/backward_1/pallas_call | solution.py:715
  116.3 3.7 %collective-permute-done.21.refs_17_ = bf16[2,64,256]{2,1,0:T(8,128)(2,1)S(1)} collective-permute-done((bf16[2,64,256]{2,1,0:T(8,128)(2,1)S(1)}, bf16[2,64,256]{2,1,0:T(8,128)(2,1)S(1)}, u32[]{:S(2)}, u32[]{:S(2)}) %collective-permute-start.21) | collective-permute-done | bytes 65568 | tf_op jit(solution)/shard_map/ppermute | solution.py:836
  120.0 1.2 collective-permute-done.23.refs_19_
  121.4 7.4 %backward_0.1 = (f32[1408,128]{1,0:T(8,128)S(1)}, f32[1408,128]{1,0:T(8,128)S(1)}) custom-call(s32[2]{0:T(128)S(1)} %pad_add_fusion.info, s32[16]{0:T(128)S(1)} %copy-done.10, f32[16]{0:T(128)S(1)} %copy-done.11, f32[1024,1024]{1,0:T(8,128)S(1)} %get-tuple-element.91.refs_0_, f32[1024,768]{1,0:T(8,128)S(1)} %get-tuple-element.92.refs_1_, ...), custom_call_target="tpu_custom_call" | custom-call | tf_op jit(solution)/shard_map/backward_0/pallas_call | solution.py:715
  129.0 2.0 %collective-permute-done.24.got = f32[1408,128]{1,0:T(8,128)S(1)} collective-permute-done((f32[1408,128]{1,0:T(8,128)S(1)}, f32[1408,128]{1,0:T(8,128)S(1)}, u32[]{:S(2)}, u32[]{:S(2)}) %collective-permute-start.24) | collective-permute-done | bytes 720928 | tf_op jit(solution)/shard_map/ppermute | solution.py:830
  131.1 11.2 %all_to_all.15.got = bf16[8,192,128]{2,1,0:T(8,128)(2,1)S(1)} all-to-all(bf16[8,192,128]{2,1,0:T(8,128)(2,1)S(1)} %pairs.1), channel_id=1, replica_groups={{0,1,2,3,4,5,6,7},{8,9,10,11,12,13,14,15},{16,17,18,19,20,21,22,23},{24..., dimensions={0} | all-to-all | bytes 786432 | tf_op jit(solution)/shard_map/all_to_all | solution.py:900
  142.3 9.9 %all_to_all.16 = bf16[8,176,128]{2,1,0:T(8,128)(2,1)S(1)} all-to-all(bf16[8,176,128]{2,1,0:T(8,128)(2,1)S(1)} %get-tuple-element.136), channel_id=1, replica_groups={{0,1,2,3,4,5,6,7},{8,9,10,11,12,13,14,15},{16,17,18,19,20,21,22,23},{24..., dimensions={0} | all-to-all | bytes 720896 | tf_op jit(solution)/shard_map/all_to_all | solution.py:900
  152.7 1.2 collective-permute-done.25.part_o
  154.0 3.5 %update.1 = (f32[8,128]{1,0:T(8,128)S(1)}, f32[256,384]{1,0:T(8,128)}, f32[384,384]{1,0:T(8,128)}, f32[384,256]{1,0:T(8,128)}, f32[2,1024]{1,0:T(2,128)}, /*inde...) custom-call(s32[2]{0:T(128)S(1)} %pad_add_fusion.info, ...), custom_call_target="tpu_custom_call" | custom-call | tf_op jit(solution)/shard_map/update/pallas_call | solution.py:792
  (92 shorter events, 14.6 us)
Async XLA Ops:
  0.7 25.0 %collective-permute-start.2 = (f32[2,4,8]{2,1,0:T(4,128)}, f32[2,4,8]{2,1,0:T(4,128)S(1)}, u32[]{:S(2)}, u32[]{:S(2)}) collective-permute-start(f32[2,4,8]{2,1,0:T(4,128)} %param.25), channel_id=1, source_target_pairs={{0,16},{16,0},{1,17},{17,1},{2,18},{18,2},{3,19},{19,3},{4,20},{20... | collective-permute-start | bytes 776 | tf_op jit(solution)/shard_map/ppermute | solution.py:830
  3.7 1.3 collective-permute-start
  5.8 19.8 %all-to-all-start = ((bf16[16,40,256]{2,1,0:T(8,128)(2,1)}), bf16[16,40,256]{2,1,0:T(8,128)(2,1)S(1)}, u32[]{:S(2)}, u32[]{:S(2)}) async-start(bf16[16,40,256]{2,1,0:T(8,128)(2,1)} %bitcast.5), calls=%async_computation | async-start | bytes 655360 | tf_op jit(solution)/shard_map/all_to_all | solution.py:851
  25.7 1.6 %collective-permute-start.1 = (bf16[16,40,256]{2,1,0:T(8,128)(2,1)S(1)}, bf16[16,40,256]{2,1,0:T(8,128)(2,1)S(1)}, u32[]{:S(2)}, u32[]{:S(2)}) collective-permute-start(bf16[16,40,256]{2,1,0:T(8,128)(2,1)S(1)} %all-to-all-done.got), channel_id=1, source_target_pairs={{0,16},{16,0},{1,17},{17,1},{2,18},{18,2},{3,19},{19,3},{4,20},{20... | collective-permute-start | bytes 983048 | tf_op jit(solution)/shard_map/ppermute | solution.py:830
  35.9 4.3 %collective-permute-start.3 = (bf16[2,64,256]{2,1,0:T(8,128)(2,1)S(1)}, bf16[2,64,256]{2,1,0:T(8,128)(2,1)S(1)}, u32[]{:S(2)}, u32[]{:S(2)}) collective-permute-start(bf16[2,64,256]{2,1,0:T(8,128)(2,1)S(1)} %get-tuple-element.97.refs_11_), channel_id=1, source_target_pairs={{0,1},{1,0},{2,3},{3,2},{4,5},{5,4},{6,7},{7,6},{8,9},{9,8},{10,11... | collective-permute-start | bytes 196616 | tf_op jit(solution)/shard_map/ppermute | solution.py:836
  36.6 3.7 %collective-permute-start.4 = (bf16[2,64,256]{2,1,0:T(8,128)(2,1)S(1)}, bf16[2,64,256]{2,1,0:T(8,128)(2,1)S(1)}, u32[]{:S(2)}, u32[]{:S(2)}) collective-permute-start(bf16[2,64,256]{2,1,0:T(8,128)(2,1)S(1)} %get-tuple-element.97.refs_11_), channel_id=1, source_target_pairs={{0,16},{16,0},{1,17},{17,1},{2,18},{18,2},{3,19},{19,3},{4,20},{20... | collective-permute-start | bytes 196616 | tf_op jit(solution)/shard_map/ppermute | solution.py:830
  40.3 1.3 collective-permute-start.5
  49.4 4.3 %collective-permute-start.6 = (bf16[2,64,256]{2,1,0:T(8,128)(2,1)S(1)}, bf16[2,64,256]{2,1,0:T(8,128)(2,1)S(1)}, u32[]{:S(2)}, u32[]{:S(2)}) collective-permute-start(bf16[2,64,256]{2,1,0:T(8,128)(2,1)S(1)} %get-tuple-element.100.refs_11_), channel_id=1, source_target_pairs={{0,1},{1,0},{2,3},{3,2},{4,5},{5,4},{6,7},{7,6},{8,9},{9,8},{10,11... | collective-permute-start | bytes 196616 | tf_op jit(solution)/shard_map/ppermute | solution.py:836
  50.0 3.7 %collective-permute-start.7 = (bf16[2,64,256]{2,1,0:T(8,128)(2,1)S(1)}, bf16[2,64,256]{2,1,0:T(8,128)(2,1)S(1)}, u32[]{:S(2)}, u32[]{:S(2)}) collective-permute-start(bf16[2,64,256]{2,1,0:T(8,128)(2,1)S(1)} %get-tuple-element.100.refs_11_), channel_id=1, source_target_pairs={{0,16},{16,0},{1,17},{17,1},{2,18},{18,2},{3,19},{19,3},{4,20},{20... | collective-permute-start | bytes 196616 | tf_op jit(solution)/shard_map/ppermute | solution.py:830
  53.7 1.3 collective-permute-start.8
  62.9 4.3 %collective-permute-start.9 = (bf16[2,64,256]{2,1,0:T(8,128)(2,1)S(1)}, bf16[2,64,256]{2,1,0:T(8,128)(2,1)S(1)}, u32[]{:S(2)}, u32[]{:S(2)}) collective-permute-start(bf16[2,64,256]{2,1,0:T(8,128)(2,1)S(1)} %get-tuple-element.103.refs_11_), channel_id=1, source_target_pairs={{0,1},{1,0},{2,3},{3,2},{4,5},{5,4},{6,7},{7,6},{8,9},{9,8},{10,11... | collective-permute-start | bytes 196616 | tf_op jit(solution)/shard_map/ppermute | solution.py:836
  63.5 3.7 %collective-permute-start.10 = (bf16[2,64,256]{2,1,0:T(8,128)(2,1)S(1)}, bf16[2,64,256]{2,1,0:T(8,128)(2,1)S(1)}, u32[]{:S(2)}, u32[]{:S(2)}) collective-permute-start(bf16[2,64,256]{2,1,0:T(8,128)(2,1)S(1)} %get-tuple-element.103.refs_11_), channel_id=1, source_target_pairs={{0,16},{16,0},{1,17},{17,1},{2,18},{18,2},{3,19},{19,3},{4,20},{20... | collective-permute-start | bytes 196616 | tf_op jit(solution)/shard_map/ppermute | solution.py:830
  67.2 1.3 collective-permute-start.11
  76.4 3.8 %collective-permute-start.12 = (f32[40,128]{1,0:T(8,128)S(1)}, f32[40,128]{1,0:T(8,128)S(1)}, u32[]{:S(2)}, u32[]{:S(2)}) collective-permute-start(f32[40,128]{1,0:T(8,128)S(1)} %get-tuple-element.104.refs_9_), channel_id=1, source_target_pairs={{0,1},{1,0},{2,3},{3,2},{4,5},{5,4},{6,7},{7,6},{8,9},{9,8},{10,11... | collective-permute-start | bytes 61448 | tf_op jit(solution)/shard_map/ppermute | solution.py:836
  77.0 3.2 %collective-permute-start.13 = (f32[40,128]{1,0:T(8,128)S(1)}, f32[40,128]{1,0:T(8,128)S(1)}, u32[]{:S(2)}, u32[]{:S(2)}) collective-permute-start(f32[40,128]{1,0:T(8,128)S(1)} %get-tuple-element.104.refs_9_), channel_id=1, source_target_pairs={{0,16},{16,0},{1,17},{17,1},{2,18},{18,2},{3,19},{19,3},{4,20},{20... | collective-permute-start | bytes 61448 | tf_op jit(solution)/shard_map/ppermute | solution.py:830
  80.2 1.2 collective-permute-start.14
  88.6 4.3 %collective-permute-start.15 = (bf16[2,64,256]{2,1,0:T(8,128)(2,1)S(1)}, bf16[2,64,256]{2,1,0:T(8,128)(2,1)S(1)}, u32[]{:S(2)}, u32[]{:S(2)}) collective-permute-start(bf16[2,64,256]{2,1,0:T(8,128)(2,1)S(1)} %get-tuple-element.115.refs_16_), channel_id=1, source_target_pairs={{0,1},{1,0},{2,3},{3,2},{4,5},{5,4},{6,7},{7,6},{8,9},{9,8},{10,11... | collective-permute-start | bytes 196616 | tf_op jit(solution)/shard_map/ppermute | solution.py:836
  89.2 3.7 %collective-permute-start.16 = (bf16[2,64,256]{2,1,0:T(8,128)(2,1)S(1)}, bf16[2,64,256]{2,1,0:T(8,128)(2,1)S(1)}, u32[]{:S(2)}, u32[]{:S(2)}) collective-permute-start(bf16[2,64,256]{2,1,0:T(8,128)(2,1)S(1)} %get-tuple-element.115.refs_16_), channel_id=1, source_target_pairs={{0,16},{16,0},{1,17},{17,1},{2,18},{18,2},{3,19},{19,3},{4,20},{20... | collective-permute-start | bytes 196616 | tf_op jit(solution)/shard_map/ppermute | solution.py:830
  92.9 1.3 collective-permute-start.17
  102.1 4.3 %collective-permute-start.18 = (bf16[2,64,256]{2,1,0:T(8,128)(2,1)S(1)}, bf16[2,64,256]{2,1,0:T(8,128)(2,1)S(1)}, u32[]{:S(2)}, u32[]{:S(2)}) collective-permute-start(bf16[2,64,256]{2,1,0:T(8,128)(2,1)S(1)} %get-tuple-element.120.refs_16_), channel_id=1, source_target_pairs={{0,1},{1,0},{2,3},{3,2},{4,5},{5,4},{6,7},{7,6},{8,9},{9,8},{10,11... | collective-permute-start | bytes 196616 | tf_op jit(solution)/shard_map/ppermute | solution.py:836
  102.7 3.7 %collective-permute-start.19 = (bf16[2,64,256]{2,1,0:T(8,128)(2,1)S(1)}, bf16[2,64,256]{2,1,0:T(8,128)(2,1)S(1)}, u32[]{:S(2)}, u32[]{:S(2)}) collective-permute-start(bf16[2,64,256]{2,1,0:T(8,128)(2,1)S(1)} %get-tuple-element.120.refs_16_), channel_id=1, source_target_pairs={{0,16},{16,0},{1,17},{17,1},{2,18},{18,2},{3,19},{19,3},{4,20},{20... | collective-permute-start | bytes 196616 | tf_op jit(solution)/shard_map/ppermute | solution.py:830
  106.5 1.3 collective-permute-start.20
  115.7 4.3 %collective-permute-start.21 = (bf16[2,64,256]{2,1,0:T(8,128)(2,1)S(1)}, bf16[2,64,256]{2,1,0:T(8,128)(2,1)S(1)}, u32[]{:S(2)}, u32[]{:S(2)}) collective-permute-start(bf16[2,64,256]{2,1,0:T(8,128)(2,1)S(1)} %get-tuple-element.126.refs_16_), channel_id=1, source_target_pairs={{0,1},{1,0},{2,3},{3,2},{4,5},{5,4},{6,7},{7,6},{8,9},{9,8},{10,11... | collective-permute-start | bytes 196616 | tf_op jit(solution)/shard_map/ppermute | solution.py:836
  116.3 3.7 %collective-permute-start.22 = (bf16[2,64,256]{2,1,0:T(8,128)(2,1)S(1)}, bf16[2,64,256]{2,1,0:T(8,128)(2,1)S(1)}, u32[]{:S(2)}, u32[]{:S(2)}) collective-permute-start(bf16[2,64,256]{2,1,0:T(8,128)(2,1)S(1)} %get-tuple-element.126.refs_16_), channel_id=1, source_target_pairs={{0,16},{16,0},{1,17},{17,1},{2,18},{18,2},{3,19},{19,3},{4,20},{20... | collective-permute-start | bytes 196616 | tf_op jit(solution)/shard_map/ppermute | solution.py:830
  120.0 1.3 collective-permute-start.23
  121.3 32.6 %copy-start.4 = (f32[384,384]{1,0:T(8,128)S(1)}, f32[384,384]{1,0:T(8,128)}, u32[]{:S(2)}) copy-start(f32[384,384]{1,0:T(8,128)} %refs_5_.1) | copy-start | bytes 1769476
  121.3 32.6 %copy-start.5 = (f32[384,384]{1,0:T(8,128)S(1)}, f32[384,384]{1,0:T(8,128)}, u32[]{:S(2)}) copy-start(f32[384,384]{1,0:T(8,128)} %refs_9_.9) | copy-start | bytes 1769476
  121.3 32.6 %copy-start.6 = (f32[256,384]{1,0:T(8,128)S(1)}, f32[256,384]{1,0:T(8,128)}, u32[]{:S(2)}) copy-start(f32[256,384]{1,0:T(8,128)} %refs_4_.1) | copy-start | bytes 1179652
  121.3 32.6 %copy-start.7 = (f32[384,256]{1,0:T(8,128)S(1)}, f32[384,256]{1,0:T(8,128)}, u32[]{:S(2)}) copy-start(f32[384,256]{1,0:T(8,128)} %refs_6_.1) | copy-start | bytes 1179652
  121.3 32.6 %copy-start.8 = (f32[256,384]{1,0:T(8,128)S(1)}, f32[256,384]{1,0:T(8,128)}, u32[]{:S(2)}) copy-start(f32[256,384]{1,0:T(8,128)} %refs_8_.9) | copy-start | bytes 1179652
  128.7 2.3 %collective-permute-start.24 = (f32[1408,128]{1,0:T(8,128)S(1)}, f32[1408,128]{1,0:T(8,128)S(1)}, u32[]{:S(2)}, u32[]{:S(2)}) collective-permute-start(f32[1408,128]{1,0:T(8,128)S(1)} %get-tuple-element.133), channel_id=1, source_target_pairs={{0,16},{16,0},{1,17},{17,1},{2,18},{18,2},{3,19},{19,3},{4,20},{20... | collective-permute-start | bytes 2162696 | tf_op jit(solution)/shard_map/ppermute | solution.py:830
  152.2 1.7 %collective-permute-start.25 = (bf16[1408,128]{1,0:T(8,128)(2,1)S(1)}, bf16[1408,128]{1,0:T(8,128)(2,1)S(1)}, u32[]{:S(2)}, u32[]{:S(2)}) collective-permute-start(bf16[1408,128]{1,0:T(8,128)(2,1)S(1)} %bitcast.21), channel_id=1, source_target_pairs={{0,16},{16,0},{1,17},{17,1},{2,18},{18,2},{3,19},{19,3},{4,20},{20... | collective-permute-start | bytes 1081352 | tf_op jit(solution)/shard_map/ppermute | solution.py:830
  (10 other events, 303.7 us)

commit v3 on v2

--- a/solution.py
+++ b/solution.py
@@ -246,6 +246,7 @@
 LANES = 128
 GROUP = 2
 SUB = 256
+CHUNK = 32
 ROWS_BLOCK = 2
 VMEM_LIMIT = 10 << 20
 SAVED_LIMIT = 96 << 20
@@ -264,11 +265,18 @@
     return centre * scale, scale
 
 
-def gelu_twice(z):
+def gelu_parts(z):
     arg = z * math.sqrt(0.5)
-    cdf = 1.0 + lax.erf(arg)
-    pdf = jnp.exp2(arg * arg * -math.log2(math.e))
-    return z * cdf, cdf + (z * math.sqrt(2.0 / math.pi)) * pdf
+    return arg, 1.0 + lax.erf(arg)
+
+
+def slope_twice(z):
+    arg, cdf = gelu_parts(z)
+    return cdf + (z * math.sqrt(2.0 / math.pi)) * jnp.exp2(arg * arg * -math.log2(math.e))
+
+
+def wide(scale, width):
+    return jnp.concatenate([scale] * (width // LANES), axis=1)
 
 
 def whole(a):
@@ -289,6 +297,16 @@
     gains = [1.0 + nb[0:1, a:b] for a, b in ((0, chans), (chans, chans + hidden), (chans + hidden, chans + 2 * hidden))]
     biases = [nb[1:2, a:b] for a, b in ((0, hidden), (hidden, 2 * hidden), (2 * hidden, 2 * hidden + chans))]
     return gains, biases
+
+
+def stagger(chains):
+    live, waiting = [], list(chains)
+    while live or waiting:
+        if waiting:
+            live.append(waiting.pop(0))
+        for chain in list(live):
+            if next(chain, live) is live:
+                live.remove(chain)
 
 
 def pair_rows(plan):
@@ -328,26 +346,19 @@
     rep = jnp.where(r1 // lats == r0 % degrees, rep, 0.0).astype(BF16)
     lat_lane = jnp.zeros((8, span), jnp.int32)
     lane = iota(1, (8, span)) // waves
-    for r in range(lats):
-        lat_lane = jnp.where(lane == r, order[r], lat_lane)
+    for role in range(members):
+        other = (member ^ (role & (group - 1))) * 2 + (core ^ (role // group))
+        for r in range(rows):
+            lat_lane = jnp.where(lane == role * rows + r, order[other * rows + r], lat_lane)
     wave_row = jnp.zeros(shape, jnp.int32)
     for j in range(waves):
         wave_row = jnp.where(r0 // degrees == j, slots[j], wave_row)
     choose = (r0 % lats == lat_lane[0:1, :]).astype(F32).astype(BF16)
     plg = dot(rep, choose)
     plg = jnp.where((r0 // degrees == r1 % waves) & (r0 % degrees >= wave_row), plg, 0.0)
-    flip = plg.T
+    links[...] = plg.astype(BF16)
+    lt[...] = plg[:, 0:mine].T.astype(BF16)
     spot = member * 2 + core
-    for role in range(members):
-        other = (member ^ (role & (group - 1))) * 2 + (core ^ (role // group))
-        piece = jnp.zeros((span, mine), F32)
-        for w in range(members):
-            piece = jnp.where(other == w, plg[:, w * mine : (w + 1) * mine], piece)
-        links[role] = piece.astype(BF16)
-    own = jnp.zeros((mine, span), F32)
-    for w in range(members):
-        own = jnp.where(spot == w, flip[w * mine : (w + 1) * mine, :], own)
-    lt[...] = own.astype(BF16)
     den = jnp.zeros((fields, chans), F32)
     for r in range(rows):
         src = spot * rows + r
@@ -371,7 +382,7 @@
     ins = [got, got_o, inv, ffw, wanted]
     shapes = [
         jax.ShapeDtypeStruct((2, span, chans), F32),
-        jax.ShapeDtypeStruct((2 * group, span, mine), BF16),
+        jax.ShapeDtypeStruct((span, 2 * group * mine), BF16),
         jax.ShapeDtypeStruct((mine, span), BF16),
         jax.ShapeDtypeStruct((rows, fields, lons), BF16),
         jax.ShapeDtypeStruct(((steps + 1) * fields, LANES), F32),
@@ -397,22 +408,42 @@
     return pltpu.CompilerParams(vmem_limit_bytes=VMEM_LIMIT)
 
 
+def write_count(plan, step, nums_in, nums, acc):
+    fields, chans = plan.fields, plan.chans
+    kept = jnp.where(field_mask(fields, chans), acc, 0.0)
+    nums[...] = nums_in[...]
+    nums[step * fields : (step + 1) * fields, :] = jnp.broadcast_to(
+        jnp.sum(kept, axis=1, keepdims=True), (fields, LANES)
+    )
+
+
+def weighted_sum(weights, values):
+    hi = values.astype(BF16)
+    lo = (values - hi.astype(F32)).astype(BF16)
+    return dot(weights, hi) + dot(weights, lo)
+
+
 def forward_kernel(plan, step, info, order, quad, *refs):
     group, rows, waves, _, steps, fields, chans, hidden, lons = plan
     first, last = step == 0, step == steps - 1
     rows_blk = pair_rows(plan)
     refs = list(refs)
     take = lambda: refs.pop(0)
-    state, avail, nums_in, table, ffw, lt, w1, w2, w3, nb = [take() for _ in range(10)]
+    state, table, ffw, lt, w1, w2, w3, nb = [take() for _ in range(8)]
+    if last:
+        avail, nums_in = take(), take()
     if not first:
         links = take()
         pieces = [take() for _ in range(2 * group)]
-    units, slopes, scales, nums = [take() for _ in range(4)]
-    if not last:
-        y_out = take()
-    if not first and not last:
-        state_out = take()
-    sums, num_acc = take(), take()
+    units, inners, scales = [take() for _ in range(3)]
+    if last:
+        nums = take()
+    else:
+        sums, outs, y_out = [take() for _ in range(3)]
+        if not first:
+            state_out = take()
+    if last:
+        sums, num_acc = take(), take()
     i = pl.program_id(0)
 
     @pl.when(i == 0)
@@ -420,93 +451,145 @@
         for p in range(2):
             st = state[p]
             if not first:
-                spec = dot(links[0], pieces[0][p])
-                for role in range(1, 2 * group):
-                    spec = spec + dot(links[role], pieces[role][p])
+                spec = dot(links[...], jnp.concatenate([piece[p] for piece in pieces], axis=0))
                 st = st + STEP_SCALE * spec
                 if not last:
                     state_out[p] = st
             sums[p] = dot(lt[...], st.astype(BF16)).astype(BF16)
-        num_acc[...] = jnp.zeros_like(num_acc)
+        if last:
+            num_acc[...] = jnp.zeros_like(num_acc)
 
     gains, biases = splits(nb, chans, hidden)
-    for rr in range(rows_blk):
+    spans = ((0, chans), (chans, hidden), (chans + hidden, hidden))
+    weights = (w1, w2, w3)
+
+    def row_chain(rr):
         row = i * rows_blk + rr
         at = pl.ds(pl.multiple_of(row * waves, waves), waves)
         rhs = jnp.concatenate([sums[0, at, :], sums[1, at, :]], axis=0)
         q = row_weight(plan, info, order, quad, row)
-        highs, lows, tends = [], [], []
-        for c0 in range(0, lons, SUB):
-            cs = pl.ds(pl.multiple_of(row * lons + c0, SUB), SUB)
-            grid = dot(table[c0 : c0 + SUB, :], rhs)
-            u1, s1 = norm_unit(grid, EPS_NORM)
-            units[cs, 0:chans] = u1
-            scales[cs, :] = jnp.broadcast_to(s1, (SUB, LANES))
-            a1, d1 = gelu_twice(dot((u1 * gains[0]).astype(BF16), w1[...]) + biases[0])
-            u2, s2 = norm_unit(a1, 4.0 * EPS_NORM)
-            units[cs, chans : chans + hidden] = u2
-            slopes[cs, 0:hidden] = d1 * s2
-            a2, d2 = gelu_twice(dot((u2 * gains[1]).astype(BF16), w2[...]) + biases[1])
-            u3, s3 = norm_unit(a2, 4.0 * EPS_NORM)
-            units[cs, chans + hidden :] = u3
-            slopes[cs, hidden:] = d2 * s3
-            out = dot((u3 * gains[2]).astype(BF16), w3[...]) + biases[2]
-            pred = grid + STEP_SCALE * out
-            hi = pred.astype(BF16)
-            highs.append(hi)
-            lows.append((pred - hi.astype(F32)).astype(BF16))
-            tends.append((out * q).astype(BF16))
-        weigh = lambda parts: dot(avail[rr], jnp.concatenate(parts, axis=0))
-        num_acc[...] += q * (weigh(highs) + weigh(lows))
-        if not last:
+        grid = dot(table[...], rhs)
+        yield
+        x = [grid[c : c + CHUNK] for c in range(0, lons, CHUNK)]
+        for k in range(3):
+            low = []
+            for n, part in enumerate(x):
+                cs = pl.ds(pl.multiple_of(row * lons + n * CHUNK, CHUNK), CHUNK)
+                if k:
+                    part = part + biases[k - 1]
+                    inners[cs, (k - 1) * hidden : k * hidden] = part
+                    part = part * gelu_parts(part)[1]
+                unit, scale = norm_unit(part, 4.0 * EPS_NORM if k else EPS_NORM)
+                units[cs, spans[k][0] : spans[k][0] + spans[k][1]] = unit
+                scales[cs, k * LANES : (k + 1) * LANES] = jnp.broadcast_to(scale, (CHUNK, LANES))
+                low.append((unit * gains[k]).astype(BF16))
+            yield
+            z = dot(jnp.concatenate(low, axis=0), weights[k][...])
+            x = [z[c : c + CHUNK] for c in range(0, lons, CHUNK)]
+            yield
+        if last:
+            pred = grid + STEP_SCALE * (z + biases[2])
+            yield
+            num_acc[...] += q * weighted_sum(avail[row], pred)
+        else:
+            tends = []
+            for n, part in enumerate(x):
+                cs = pl.ds(pl.multiple_of(row * lons + n * CHUNK, CHUNK), CHUNK)
+                out = part + biases[2]
+                outs[cs, :] = out
+                tends.append((out * q).astype(BF16))
+            yield
             coeff = dot(ffw[...], jnp.concatenate(tends, axis=0)).astype(BF16)
-            y_out[0, rr * waves : (rr + 1) * waves, :] = coeff[:waves]
-            y_out[1, rr * waves : (rr + 1) * waves, :] = coeff[waves:]
-
-    @pl.when(i == pl.num_programs(0) - 1)
-    def _():
-        kept = jnp.where(field_mask(fields, chans), num_acc[...], 0.0)
-        nums[...] = nums_in[...]
-        nums[step * fields : (step + 1) * fields, :] = jnp.broadcast_to(
-            jnp.sum(kept, axis=1, keepdims=True), (fields, LANES)
-        )
+            y_out[0, at, :] = coeff[:waves]
+            y_out[1, at, :] = coeff[waves:]
+        yield
+
+    stagger([row_chain(rr) for rr in range(rows_blk)])
+
+    if last:
+
+        @pl.when(i == pl.num_programs(0) - 1)
+        def _():
+            write_count(plan, step, nums_in, nums, num_acc[...])
+
+
+def step_call(kernel, name, grid, shapes, ins, scalars, work, scratch=(), aliases=None):
+    cols, flops = work
+    return pl.pallas_call(
+        kernel,
+        out_shape=shapes,
+        grid_spec=pltpu.PrefetchScalarGridSpec(
+            num_scalar_prefetch=len(scalars),
+            grid=(grid,),
+            in_specs=[pl.BlockSpec(memory_space=VM)] * len(ins),
+            out_specs=[pl.BlockSpec(memory_space=VM)] * len(shapes),
+            scratch_shapes=list(scratch),
+        ),
+        input_output_aliases=aliases or {},
+        compiler_params=kernel_params(),
+        cost_estimate=pl.CostEstimate(flops=cols * flops, bytes_accessed=cols * 8192, transcendentals=cols * 1024),
+        name=name,
+    )(*scalars, *ins)
 
 
 def forward_call(plan, step, scalars, state, avail, nums, table, ffw, lt, weights, nb, links, pieces):
     group, rows, waves, _, steps, fields, chans, hidden, lons = plan
     first, last = step == 0, step == steps - 1
     rows_blk = pair_rows(plan)
-    cols, blk = rows * lons, rows_blk * lons
-    ins = [state, avail, nums, table, ffw, lt, *weights, nb]
+    cols = rows * lons
+    ins = [state, table, ffw, lt, *weights, nb]
+    if last:
+        ins += [avail, nums]
     if not first:
         ins += [links, *pieces]
-    specs = [whole(a) for a in ins]
-    specs[1] = pl.BlockSpec((rows_blk, fields, lons), lambda i, *_: (i, 0, 0))
-    shapes, ospecs = [], []
-    for width in (chans + 2 * hidden, 2 * hidden, LANES):
-        shapes.append(VM((cols, width), F32))
-        ospecs.append(pl.BlockSpec(memory_space=VM))
-    shapes.append(jax.ShapeDtypeStruct(nums.shape, F32))
-    ospecs.append(whole(nums))
-    if not last:
-        shapes.append(jax.ShapeDtypeStruct((2, rows * waves, chans), BF16))
-        ospecs.append(pl.BlockSpec((2, rows_blk * waves, chans), lambda i, *_: (0, i, 0)))
-    if not first and not last:
-        shapes.append(jax.ShapeDtypeStruct(state.shape, F32))
-        ospecs.append(whole(state))
-    return pl.pallas_call(
-        partial(forward_kernel, plan, step),
-        out_shape=shapes,
-        grid_spec=pltpu.PrefetchScalarGridSpec(
-            num_scalar_prefetch=3,
-            grid=(rows // rows_blk,),
-            in_specs=specs,
-            out_specs=ospecs,
-            scratch_shapes=[VM((2, rows * waves, chans), BF16), VM((fields, chans), F32)],
-        ),
-        compiler_params=kernel_params(),
-        name=f"forward_{step}",
-    )(*scalars, *ins)
+    shapes = [VM((cols, width), F32) for width in (chans + 2 * hidden, 2 * hidden, 3 * LANES)]
+    sums = (2, rows * waves, chans)
+    scratch = []
+    if last:
+        shapes.append(VM(nums.shape, F32))
+        scratch = [VM(sums, BF16), VM((fields, chans), F32)]
+    else:
+        shapes += [VM(sums, BF16), VM((cols, chans), F32), VM(sums, BF16)]
+        if not first:
+            shapes.append(VM(state.shape, F32))
+    flops = 2 * hidden * (2 * chans + hidden)
+    return step_call(
+        partial(forward_kernel, plan, step), f"forward_{step}", rows // rows_blk, shapes, ins, scalars, (cols, flops), scratch
+    )
+
+
+def slopes_kernel(plan, inners, scales, slopes):
+    rows, hidden, lons = plan.rows, plan.hidden, plan.lons
+    i = pl.program_id(0)
+    for n in range(lons // CHUNK):
+        cs = pl.ds(pl.multiple_of(i * lons + n * CHUNK, CHUNK), CHUNK)
+        for k in range(2):
+            at = slice(k * hidden, (k + 1) * hidden)
+            scale = wide(scales[cs, (k + 1) * LANES : (k + 2) * LANES], hidden)
+            slopes[cs, at] = slope_twice(inners[cs, at]) * scale
+
+
+def slopes_call(plan, step, inners, scales):
+    work = (plan.rows * plan.lons, 16 * plan.hidden)
+    return step_call(
+        partial(slopes_kernel, plan), f"slopes_{step}", plan.rows, [VM(inners.shape, F32)], [inners, scales], (), work, (), {0: 0}
+    )[0]
+
+
+def counts_kernel(plan, step, info, order, quad, sums, outs, avail, nums_in, table, nums):
+    rows, waves, fields, chans, lons = plan.rows, plan.waves, plan.fields, plan.chans, plan.lons
+    acc = jnp.zeros((fields, chans), F32)
+    for row in range(rows):
+        at = slice(row * waves, (row + 1) * waves)
+        grid = dot(table[...], jnp.concatenate([sums[0, at, :], sums[1, at, :]], axis=0))
+        pred = grid + STEP_SCALE * outs[row * lons : (row + 1) * lons, :]
+        acc = acc + row_weight(plan, info, order, quad, row) * weighted_sum(avail[row], pred)
+    write_count(plan, step, nums_in, nums, acc)
+
+
+def counts_call(plan, step, scalars, ins):
+    work = (plan.rows * plan.lons, 8 * plan.chans)
+    return step_call(partial(counts_kernel, plan, step), f"counts_{step}", 1, [VM(ins[3].shape, F32)], ins, scalars, work)[0]
 
 
 def packed_parts(plan):
@@ -544,29 +627,23 @@
     levels = chans // fields
     refs = list(refs)
     take = lambda: refs.pop(0)
-    units, slopes, scales, avail, tgt, w1, w2, w3, nb = [take() for _ in range(9)]
+    units, slopes, scales, avail, tgt, w2, w3, nb = [take() for _ in range(8)]
     counts = [take() for _ in range(members)]
     if not first:
         links, lt, ffw_t = [take() for _ in range(3)]
         pieces = [take() for _ in range(members)]
         if not fresh:
             bstate = take()
-        before = [take() for _ in range(4)]
     if not last:
-        inv = take()
-        grads = [take() for _ in range(4)]
+        w1, inv = take(), take()
+    dzs = take()
+    if not last:
         b_out = take()
         if not first:
             bstate_out = take()
-    else:
-        mine, send = take(), take()
     if first:
         loss = take()
     coef, gmask = take(), take()
-    if last:
-        grads = [take() for _ in range(4)]
-        packed = take()
-    d1, d2, d3, dv = grads
     i = pl.program_id(0)
 
     @pl.when(i == 0)
@@ -580,8 +657,7 @@
         den = total(steps)
         bias_of = lambda s: total(s) / (levels * den) - tgt[s * fields : (s + 1) * fields, :]
         gb = 2.0 * bias_of(step) / (steps * levels * den)
-        gb = jnp.concatenate([gb] * (chans // LANES), axis=1)
-        gb = jnp.where(field_mask(fields, chans), gb, 0.0)
+        gb = jnp.where(field_mask(fields, chans), wide(gb, chans), 0.0)
         hi = gb.astype(BF16).astype(F32)
         gmask[...] = jnp.concatenate([hi, gb - hi], axis=0).astype(BF16)
         if first:
@@ -589,15 +665,9 @@
             for s in range(1, steps):
                 sq = sq + bias_of(s) * bias_of(s)
             loss[...] = jnp.broadcast_to(jnp.sum(sq, axis=0, keepdims=True) / steps, loss.shape)
-            for d in grads:
-                d[...] = jnp.zeros_like(d)
         else:
-            for d, b in zip(grads, before):
-                d[...] = b[...]
             for p in range(2):
-                st = dot(links[0], pieces[0][p])
-                for role in range(1, members):
-                    st = st + dot(links[role], pieces[role][p])
+                st = dot(links[...], jnp.concatenate([piece[p] for piece in pieces], axis=0))
                 if not fresh:
                     st = bstate[p] + st
                 if not last:
@@ -607,124 +677,164 @@
     gains, _ = splits(nb, chans, hidden)
 
     def norm_back(back, gain, unit):
-        prod = back * unit
         low = back * gain
         m1 = jnp.mean(low, axis=-1, keepdims=True)
-        m2 = jnp.mean(prod * gain, axis=-1, keepdims=True)
-        return prod, low - m1 - unit * m2
-
-    for rr in range(rows_blk):
+        m2 = jnp.mean(low * unit, axis=-1, keepdims=True)
+        return low - m1 - unit * m2
+
+    def row_chain(rr):
         row = i * rows_blk + rr
+        at = pl.ds(pl.multiple_of(row * waves, waves), waves)
         q = row_weight(plan, info, order, quad, row)
-        av2 = jnp.concatenate([avail[rr].astype(F32)] * 2, axis=0).astype(BF16)
+        chunks = [pl.ds(pl.multiple_of(row * lons + c, CHUNK), CHUNK) for c in range(0, lons, CHUNK)]
+        cut = lambda v: [v[c : c + CHUNK] for c in range(0, lons, CHUNK)]
+        av2 = jnp.concatenate([avail[row].astype(F32)] * 2, axis=0).astype(BF16)
+        mask = dot(av2, gmask[...], ((0,), (0,)))
         if not first:
-            at = pl.ds(pl.multiple_of(row * waves, waves), waves)
-            rhs = jnp.concatenate([coef[0, at, :], coef[1, at, :]], axis=0)
-        grids = []
-        for c0 in range(0, lons, SUB):
-            cs = pl.ds(pl.multiple_of(row * lons + c0, SUB), SUB)
-            dpred = q * dot(av2[:, c0 : c0 + SUB], gmask[...], ((0,), (0,)))
+            tend = dot(ffw_t[...], jnp.concatenate([coef[0, at, :], coef[1, at, :]], axis=0))
+        yield
+        dpreds, low = [], []
+        for n, (cs, part) in enumerate(zip(chunks, cut(mask))):
+            dpred = q * part
             dout = STEP_SCALE * dpred
             if not first:
-                dout = dout + q * dot(ffw_t[c0 : c0 + SUB, :], rhs)
-            dz = dout.astype(BF16)
-            u = units[cs, chans + hidden :]
-            d3[...] += dot((u * gains[2]).astype(BF16), dz, ((0,), (0,)))
-            dv[8:16, 2 * hidden :] += fold(dz.astype(F32))
-            prod, dx = norm_back(dot(dz, w3[...], ((1,), (1,))), gains[2], u)
-            dv[0:8, chans + hidden :] += fold(prod)
-            dz = (dx * slopes[cs, hidden:]).astype(BF16)
-            u = units[cs, chans : chans + hidden]
-            d2[...] += dot((u * gains[1]).astype(BF16), dz, ((0,), (0,)))
-            dv[8:16, hidden : 2 * hidden] += fold(dz.astype(F32))
-            prod, dx = norm_back(dot(dz, w2[...], ((1,), (1,))), gains[1], u)
-            dv[0:8, chans : chans + hidden] += fold(prod)
-            dz = (dx * slopes[cs, 0:hidden]).astype(BF16)
-            u = units[cs, 0:chans]
-            d1[...] += dot((u * gains[0]).astype(BF16), dz, ((0,), (0,)))
-            dv[8:16, 0:hidden] += fold(dz.astype(F32))
-            back = dot(dz, w1[...], ((1,), (1,)))
-            if last:
-                dv[0:8, 0:chans] += fold(back * u)
-            else:
-                prod, dx = norm_back(back, gains[0], u)
-                dv[0:8, 0:chans] += fold(prod)
-                grids.append((dpred + dx * scales[cs, 0:1]).astype(BF16))
+                dout = dout + q * cut(tend)[n]
+            dpreds.append(dpred)
+            low.append(dout.astype(BF16))
+            dzs[cs, 2 * hidden :] = low[-1]
+        yield
+        for k, weight in ((2, w3), (1, w2)):
+            back = dot(jnp.concatenate(low, axis=0), weight[...], ((1,), (1,)))
+            yield
+            low = []
+            span = slice(chans + (k - 1) * hidden, chans + k * hidden)
+            inner = slice((k - 1) * hidden, k * hidden)
+            for cs, part in zip(chunks, cut(back)):
+                dx = norm_back(part, gains[k], units[cs, span])
+                low.append((dx * slopes[cs, inner]).astype(BF16))
+                dzs[cs, inner] = low[-1]
+            yield
         if not last:
+            back = dot(jnp.concatenate(low, axis=0), w1[...], ((1,), (1,)))
+            yield
+            grids = []
+            for n, (cs, part) in enumerate(zip(chunks, cut(back))):
+                dx = norm_back(part, gains[0], units[cs, 0:chans])
+                grids.append((dpreds[n] + dx * wide(scales[cs, 0:LANES], chans)).astype(BF16))
+            yield
             coeff = dot(inv[...], jnp.concatenate(grids, axis=0)).astype(BF16)
-            b_out[0, rr * waves : (rr + 1) * waves, :] = coeff[:waves]
-            b_out[1, rr * waves : (rr + 1) * waves, :] = coeff[waves:]
-
-    if last:
-
-        @pl.when(i == pl.num_programs(0) - 1)
-        def _():
-            half = packed.shape[1]
-            parts, at = packed_parts(plan)
-            for which, tile, start, count in parts:
-                for h, dst, src, n in both_halves(start, count, half):
-                    packed[h, dst : dst + n, :] = grads[which][src : src + n, tile * LANES : (tile + 1) * LANES]
-            for v in range(2):
-                line = jnp.sum(dv[v * 8 : v * 8 + 8, :], axis=0, keepdims=True)
-                for tile in range(line.shape[1] // LANES):
-                    row = at - half
-                    packed[1, row : row + 1, :] = line[:, tile * LANES : (tile + 1) * LANES]
-                    at += 1
-            tail = at - half
-            packed[1, tail:, :] = jnp.zeros((half - tail, LANES), F32)
-            mine[...] = packed[info[0]]
-            send[...] = packed[1 - info[0]]
-
-
-def backward_call(plan, step, chips, scalars, saved, avail, tgt, weights, nb, counts, tables, pieces, bstate, before):
+            b_out[0, at, :] = coeff[:waves]
+            b_out[1, at, :] = coeff[waves:]
+            yield
+
+    stagger([row_chain(rr) for rr in range(rows_blk)])
+
+
+def backward_call(plan, step, scalars, saved, avail, tgt, weights, nb, counts, tables, pieces, bstate):
     group, rows, waves, degrees, steps, fields, chans, hidden, lons = plan
     first, last = step == steps - 1, step == 0
     rows_blk = pair_rows(plan)
-    blk = rows_blk * lons
     links, lt, ffw_t, inv = tables
-    ins = [*saved, avail, tgt, *weights, nb, *counts]
+    ins = [*saved, avail, tgt, *weights[1:], nb, *counts]
     if not first:
         ins += [links, lt, ffw_t, *pieces]
         if step != steps - 2:
             ins.append(bstate)
+    if not last:
+        ins += [weights[0], inv]
+    sums = (2, rows * waves, chans)
+    shapes = [VM((rows * lons, 2 * hidden + chans), BF16)]
+    if not last:
+        shapes.append(VM(sums, BF16))
+        if not first:
+            shapes.append(VM((2, waves * degrees, chans), F32))
+    if first:
+        shapes.append(VM((8, LANES), F32))
+    flops = 2 * hidden * (2 * chans + hidden)
+    return step_call(
+        partial(backward_kernel, plan, step),
+        f"backward_{step}",
+        rows // rows_blk,
+        shapes,
+        ins,
+        scalars,
+        (rows * lons, flops),
+        [VM(sums, BF16), VM((2 * fields, chans), BF16)],
+    )
+
+
+def grads_kernel(plan, step, info, *refs):
+    _, rows, _, _, steps, _, chans, hidden, lons = plan
+    first, last = step == steps - 1, step == 0
+    refs = list(refs)
+    take = lambda: refs.pop(0)
+    units, dzs, nb = [take() for _ in range(3)]
+    before = None if first else [take() for _ in range(4)]
+    if last:
+        weights = [take() for _ in range(3)]
+        mine, send = take(), take()
+    grads = [take() for _ in range(4)]
+    gains, _ = splits(nb, chans, hidden)
+    ins = ((0, chans), (chans, hidden), (chans + hidden, hidden))
+    outs = ((0, hidden), (hidden, hidden), (2 * hidden, chans))
+    for k in range(3):
+        a, b = ins[k][0], outs[k][0]
+        unit = slice(a, a + ins[k][1])
+        slot = slice(b, b + outs[k][1])
+        low = [(units[c : c + CHUNK, unit] * gains[k]).astype(BF16) for c in range(0, rows * lons, CHUNK)]
+        new = dot(jnp.concatenate(low, axis=0), dzs[:, slot], ((0,), (0,)))
+        bias = fold(dzs[0:CHUNK, slot].astype(F32))
+        for c in range(CHUNK, rows * lons, CHUNK):
+            bias = bias + fold(dzs[c : c + CHUNK, slot].astype(F32))
+        if not first:
+            new = before[k][...] + new
+            bias = before[3][:, slot] + bias
+        grads[k][...] = new
+        grads[3][:, slot] = bias
+    if not last:
+        return
+    packed = refs.pop(0)
+    half = packed.shape[1]
+    parts, at = packed_parts(plan)
+    for which, tile, start, count in parts:
+        for h, dst, src, n in both_halves(start, count, half):
+            packed[h, dst : dst + n, :] = grads[which][src : src + n, tile * LANES : (tile + 1) * LANES]
+    lines = []
+    for k in range(3):
+        prod = grads[k][...] * weights[k][...].astype(F32)
+        thin = prod[:, 0:LANES]
+        for tile in range(1, prod.shape[1] // LANES):
+            thin = thin + prod[:, tile * LANES : (tile + 1) * LANES]
+        lines.append(jnp.sum(thin.T, axis=0, keepdims=True) / gains[k])
+    for line in (jnp.concatenate(lines, axis=1), jnp.sum(grads[3][...], axis=0, keepdims=True)):
+        for tile in range(line.shape[1] // LANES):
+            packed[1, at - half : at - half + 1, :] = line[:, tile * LANES : (tile + 1) * LANES]
+            at += 1
+    packed[1, at - half :, :] = jnp.zeros((2 * half - at, LANES), F32)
+    mine[...] = packed[info[0]]
+    send[...] = packed[1 - info[0]]
+
+
+def grads_call(plan, step, chips, info, units, dzs, nb, before, weights):
+    _, rows, _, _, steps, _, chans, hidden, lons = plan
+    first, last = step == steps - 1, step == 0
+    ins = [units, dzs, nb]
+    aliases = {}
+    if not first:
         ins += before
-    if not last:
-        ins.append(inv)
-    specs = [whole(a) for a in ins]
-    for n in range(3):
-        specs[n] = pl.BlockSpec(memory_space=VM)
-    specs[3] = pl.BlockSpec((rows_blk, fields, lons), lambda i, *_: (i, 0, 0))
-    sums = [((chans, hidden), F32), ((hidden, hidden), F32), ((hidden, chans), F32), ((16, chans + 2 * hidden), F32)]
-    scratch = [VM((2, rows * waves, chans), BF16), VM((2 * fields, chans), BF16)]
+    sums = [VM(s, F32) for s in ((chans, hidden), (hidden, hidden), (hidden, chans), (8, 2 * hidden + chans))]
     if last:
+        ins += weights
         half = chips * packed_block(plan, chips)
-        scratch += [VM(*s) for s in sums] + [VM((2, half, LANES), F32)]
-        shapes = [jax.ShapeDtypeStruct((half, LANES), F32)] * 2
-        ospecs = [whole(a) for a in shapes]
+        shapes, scratch = [VM((half, LANES), F32)] * 2, [*sums, VM((2, half, LANES), F32)]
     else:
-        shapes = [jax.ShapeDtypeStruct(*s) for s in sums]
-        ospecs = [whole(a) for a in shapes]
-        shapes.append(jax.ShapeDtypeStruct((2, rows * waves, chans), BF16))
-        ospecs.append(pl.BlockSpec((2, rows_blk * waves, chans), lambda i, *_: (0, i, 0)))
+        shapes, scratch = sums, []
         if not first:
-            shapes.append(jax.ShapeDtypeStruct((2, waves * degrees, chans), F32))
-            ospecs.append(whole(shapes[-1]))
-    if first:
-        shapes.append(jax.ShapeDtypeStruct((8, LANES), F32))
-        ospecs.append(whole(shapes[-1]))
-    return pl.pallas_call(
-        partial(backward_kernel, plan, step),
-        out_shape=shapes,
-        grid_spec=pltpu.PrefetchScalarGridSpec(
-            num_scalar_prefetch=3,
-            grid=(rows // rows_blk,),
-            in_specs=specs,
-            out_specs=ospecs,
-            scratch_shapes=scratch,
-        ),
-        compiler_params=kernel_params(),
-        name=f"backward_{step}",
-    )(*scalars, *ins)
+            aliases = {4 + n: n for n in range(4)}
+    flops = 2 * hidden * (2 * chans + hidden)
+    return step_call(
+        partial(grads_kernel, plan, step), f"grads_{step}", 1, shapes, ins, (info,), (rows * lons, flops), scratch, aliases
+    )
 
 
 def pairs_kernel(chips, group, mine, got, loss, out):
@@ -829,13 +939,15 @@
     swap = [(0, 1), (1, 0)]
     across = lambda a: lax.ppermute(a, "tm", swap)
 
-    def to_members(a):
+    def to_members(a, fill):
         out = [a]
         bit = 1
         while bit < group:
             out += [lax.ppermute(v, "lat", [(n, n ^ bit) for n in range(waves)]) for v in out]
             bit *= 2
-        return out + [across(v) for v in out]
+        away, filled = lax.optimization_barrier((out[1:], fill()))
+        out = [a, *away]
+        return out + [across(v) for v in out], filled
 
     half = fields // 2
     pad = -(2 * degrees + half + 1) % 8
@@ -873,28 +985,34 @@
 
     saved, pieces = [], None
     for s in range(steps):
-        units, slopes, scales, nums, *rest = forward_call(
+        units, inners, scales, *rest = forward_call(
             plan, s, scalars, state, avail, nums, inv_t, ffw, lt, weights, nb, links, pieces
         )
+        fill = lambda: slopes_call(plan, s, inners, scales)
+        if s < steps - 1:
+            pieces, slopes = to_members(rest[2], fill)
+            nums = counts_call(plan, s, scalars, [rest[0], rest[1], avail, nums, inv_t])
+            pieces, nums = lax.optimization_barrier((pieces, nums))
+            if s:
+                state = rest[3]
+        else:
+            counts, slopes = to_members(rest[0], fill)
         saved.append((units, slopes, scales))
-        if s < steps - 1:
-            pieces = to_members(rest[0])
-        if 0 < s < steps - 1:
-            state = rest[1]
-    counts = to_members(nums)
-    before, bstate, loss = None, None, None
+    before, bstate = None, None
     for s in reversed(range(steps)):
-        out = backward_call(
-            plan, s, chips, scalars, saved[s], avail, tgt, weights, nb, counts, (links, lt, ffw_t, inv), pieces, bstate, before
+        dzs, *rest = backward_call(
+            plan, s, scalars, saved[s], avail, tgt, weights, nb, counts, (links, lt, ffw_t, inv), pieces, bstate
         )
-        if s > 0:
-            before = out[:4]
-            pieces = to_members(out[4])
+        fill = lambda: grads_call(plan, s, chips, info, saved[s][0], dzs, nb, before, weights)
+        if s == 0:
+            before = fill()
+        else:
+            pieces, before = to_members(rest[0], fill)
             if s == steps - 1:
-                loss = out[5]
+                loss = rest[1]
             else:
-                bstate = out[5]
-    mine, send = out
+                bstate = rest[1]
+    mine, send = before
     blk = mine.shape[0] // chips
     groups = [[c * chips + n for n in range(chips)] for c in range(copies)]
     exchange = lambda a: lax.all_to_all(a, "lat", split_axis=0, concat_axis=0, tiled=True, axis_index_groups=groups)

time: 159 us -> 135 us (0.85)
  waiting for transfers between devices: 46.3 us -> 32.5 us
  Pallas kernels: 66.4 us -> 57.7 us
  other arithmetic: 7.18 us -> 5.43 us
    ppermute x7, waiting for transfers between devices: 25.4 us -> 13.4 us  [to_members(): lax.ppermute(v, 'lat', [(n, n ^ bit) for n in range(waves)])]
    pallas_call x8 -> x19, Pallas kernels: 61.4 us -> 52.9 us  [step_call(): pl.pallas_call(kernel, out_shape=shapes, grid_spec=pltpu.PrefetchScalarGr...]
    ppermute x19, waiting for transfers between devices: 13.3 us -> 10.4 us  [grouped_device(): across = lambda a: lax.ppermute(a, 'tm', swap)]
  transfers between devices with their start and end apart: 27 -> 27, of which waited for: 19 -> 19; matrix products, arithmetic and copies ran while one was open for 6% -> 6% of each run, Pallas kernels for 0% -> 12%
where the time goes in v3:
time: 135 us
  Pallas kernels  57.7 us (43%)
  waiting for transfers between devices  32.5 us (24%)
  blocking collectives  21.1 us (16%)
  starting transfers between devices  14.1 us (10%)
  other arithmetic  5.43 us (4%)
  local copies, waits for them, and re-layouts  2.86 us (2%)
    pallas_call x19, Pallas kernels, step_call(): pl.pallas_call(kernel, out_shape=shapes, grid_spec=pltpu.PrefetchScalarGr...  52.9 us
    all_to_all x2, blocking collectives, grouped_device(): lax.all_to_all(a, 'lat', split_axis=0, concat_axis=0, tiled=True, axis_in...  21.1 us
    ppermute x7, waiting for transfers between devices, to_members(): lax.ppermute(v, 'lat', [(n, n ^ bit) for n in range(waves)])  13.4 us
    ppermute x19, waiting for transfers between devices, grouped_device(): across = lambda a: lax.ppermute(a, 'tm', swap)  10.4 us
    all_to_all x1, waiting for transfers between devices, grouped_device(): lax.all_to_all(spread.reshape(waves, *times.shape[1:]), 'lat', split_axis...  8.69 us
    all_to_all x1, starting transfers between devices, grouped_device(): lax.all_to_all(spread.reshape(waves, *times.shape[1:]), 'lat', split_axis...  8.01 us
    ppermute x7, starting transfers between devices, to_members(): lax.ppermute(v, 'lat', [(n, n ^ bit) for n in range(waves)])  4.14 us
    pallas_call x3, Pallas kernels, small_call(): pl.pallas_call(kernel, out_shape=shapes, grid_spec=pltpu.PrefetchScalarGr...  3.69 us
  transfers between devices with their start and end apart: 27, of which 19 were waited for; matrix products, arithmetic and copies ran while one was open for 6% of the time, Pallas kernels for 12%

profile of v3, /device:TPU:0, one launch (start us, length us, event | category | flops | bytes accessed | tf_op | source)
XLA Modules:
  0.0 134.7 jit_solution(12919790276555134165)
XLA Ops:
  5.8 8.0 %all-to-all-start = ((bf16[16,40,256]{2,1,0:T(8,128)(2,1)}), bf16[16,40,256]{2,1,0:T(8,128)(2,1)S(1)}, u32[]{:S(2)}, u32[]{:S(2)}) async-start(bf16[16,40,256]{2,1,0:T(8,128)(2,1)} %bitcast.5), calls=%async_computation | async-start | bytes 655360 | tf_op jit(solution)/shard_map/all_to_all | solution.py:963
  17.0 8.7 %all-to-all-done.got = bf16[16,40,256]{2,1,0:T(8,128)(2,1)S(1)} async-done(((bf16[16,40,256]{2,1,0:T(8,128)(2,1)}), bf16[16,40,256]{2,1,0:T(8,128)(2,1)S(1)}, u32[]{:S(2)}, u32[]{:S(2)}) %all-to-all-start) | async-done | bytes 327712 | tf_op jit(solution)/shard_map/all_to_all | solution.py:963
  25.8 1.5 %collective-permute-done.1.got_o = bf16[16,40,256]{2,1,0:T(8,128)(2,1)S(1)} collective-permute-done((bf16[16,40,256]{2,1,0:T(8,128)(2,1)S(1)}, bf16[16,40,256]{2,1,0:T(8,128)(2,1)S(1)}, u32[]{:S(2)}, u32[]{:S(2)}) %collective-permute-start.1) | collective-permute-done | bytes 327712 | tf_op jit(solution)/shard_map/ppermute | solution.py:940
  28.5 4.5 %forward_0.1 = (f32[1024,1024]{1,0:T(8,128)S(1)}, f32[1024,768]{1,0:T(8,128)S(1)}, f32[1024,384]{1,0:T(8,128)S(1)}, bf16[2,64,256]{2,1,0:T(8,128)(2,1)S(1)}, f32...) custom-call(s32[2]{0:T(128)S(1)} %pad_add_fusion.info, s32[16]{0:T(128)S(1)} %copy-done.10, f32[16]{0:T(128)S(1)} %copy-done.11, ...), custom_call_target="tpu_custom_call" | custom-call | flops 704643072 | bytes 8388608 | tf_op jit(solution)/shard_map/forward_0/pallas_call | solution.py:518
  33.6 1.5 %slopes_0.1.refs_1_ = f32[1024,768]{1,0:T(8,128)S(1)} custom-call(f32[1024,768]{1,0:T(8,128)S(1)} %get-tuple-element.135.inners, f32[1024,384]{1,0:T(8,128)S(1)} %get-tuple-element.136.scales.refs_2_), custom_call_target="tpu_custom_call", output_to_operand_aliasing={{}: (0, {})} | custom-call | flops 6291456 | bytes 8388608 | tf_op jit(solution)/shard_map/slopes_0/pallas_call | solution.py:518
  35.1 2.2 %collective-permute-done.3.refs_10_ = bf16[2,64,256]{2,1,0:T(8,128)(2,1)S(1)} collective-permute-done((bf16[2,64,256]{2,1,0:T(8,128)(2,1)S(1)}, bf16[2,64,256]{2,1,0:T(8,128)(2,1)S(1)}, u32[]{:S(2)}, u32[]{:S(2)}) %collective-permute-start.3) | collective-permute-done | bytes 65568 | tf_op jit(solution)/shard_map/ppermute | solution.py:946
  38.5 4.9 %forward_1.1 = (f32[1024,1024]{1,0:T(8,128)S(1)}, f32[1024,768]{1,0:T(8,128)S(1)}, f32[1024,384]{1,0:T(8,128)S(1)}, bf16[2,64,256]{2,1,0:T(8,128)(2,1)S(1)}, f32...) custom-call(s32[2]{0:T(128)S(1)} %pad_add_fusion.info, s32[16]{0:T(128)S(1)} %copy-done.10, ...), custom_call_target="tpu_custom_call" | custom-call | flops 704643072 | bytes 8388608 | tf_op jit(solution)/shard_map/forward_1/pallas_call | solution.py:518
  44.2 1.5 %slopes_1.1.refs_1_ = f32[1024,768]{1,0:T(8,128)S(1)} custom-call(f32[1024,768]{1,0:T(8,128)S(1)} %get-tuple-element.151.inners, f32[1024,384]{1,0:T(8,128)S(1)} %get-tuple-element.152.scales.refs_2_), custom_call_target="tpu_custom_call", output_to_operand_aliasing={{}: (0, {})} | custom-call | flops 6291456 | bytes 8388608 | tf_op jit(solution)/shard_map/slopes_1/pallas_call | solution.py:518
  45.7 2.2 %collective-permute-done.6.refs_10_ = bf16[2,64,256]{2,1,0:T(8,128)(2,1)S(1)} collective-permute-done((bf16[2,64,256]{2,1,0:T(8,128)(2,1)S(1)}, bf16[2,64,256]{2,1,0:T(8,128)(2,1)S(1)}, u32[]{:S(2)}, u32[]{:S(2)}) %collective-permute-start.6) | collective-permute-done | bytes 65568 | tf_op jit(solution)/shard_map/ppermute | solution.py:946
  49.2 4.9 %forward_2.1 = (f32[1024,1024]{1,0:T(8,128)S(1)}, f32[1024,768]{1,0:T(8,128)S(1)}, f32[1024,384]{1,0:T(8,128)S(1)}, bf16[2,64,256]{2,1,0:T(8,128)(2,1)S(1)}, f32...) custom-call(s32[2]{0:T(128)S(1)} %pad_add_fusion.info, s32[16]{0:T(128)S(1)} %copy-done.10, ...), custom_call_target="tpu_custom_call" | custom-call | flops 704643072 | bytes 8388608 | tf_op jit(solution)/shard_map/forward_2/pallas_call | solution.py:518
  54.8 1.5 %slopes_2.1.refs_1_ = f32[1024,768]{1,0:T(8,128)S(1)} custom-call(f32[1024,768]{1,0:T(8,128)S(1)} %get-tuple-element.163.inners, f32[1024,384]{1,0:T(8,128)S(1)} %get-tuple-element.164.scales.refs_2_), custom_call_target="tpu_custom_call", output_to_operand_aliasing={{}: (0, {})} | custom-call | flops 6291456 | bytes 8388608 | tf_op jit(solution)/shard_map/slopes_2/pallas_call | solution.py:518
  56.4 2.2 %collective-permute-done.9.refs_12_ = bf16[2,64,256]{2,1,0:T(8,128)(2,1)S(1)} collective-permute-done((bf16[2,64,256]{2,1,0:T(8,128)(2,1)S(1)}, bf16[2,64,256]{2,1,0:T(8,128)(2,1)S(1)}, u32[]{:S(2)}, u32[]{:S(2)}) %collective-permute-start.9) | collective-permute-done | bytes 65568 | tf_op jit(solution)/shard_map/ppermute | solution.py:946
  59.8 5.1 %forward_3.1 = (f32[1024,1024]{1,0:T(8,128)S(1)}, f32[1024,768]{1,0:T(8,128)S(1)}, f32[1024,384]{1,0:T(8,128)S(1)}, f32[40,128]{1,0:T(8,128)S(1)}) custom-call(s32[2]{0:T(128)S(1)} %pad_add_fusion.info, s32[16]{0:T(128)S(1)} %copy-done.10, f32[16]{0:T(128)S(1)} %copy-done.11, f32[2,256,256]{2,1,0:T(8,128)S(1)} %get-tuple-element.161.refs_0_, ...), custom_call_target="tpu_custom_call" | custom-call | flops 704643072 | bytes 8388608 | tf_op jit(solution)/shard_map/forward_3/pallas_call | solution.py:518
  65.7 1.5 %slopes_3.1.refs_1_ = f32[1024,768]{1,0:T(8,128)S(1)} custom-call(f32[1024,768]{1,0:T(8,128)S(1)} %get-tuple-element.175.inners, f32[1024,384]{1,0:T(8,128)S(1)} %get-tuple-element.176.scales.refs_2_), custom_call_target="tpu_custom_call", output_to_operand_aliasing={{}: (0, {})} | custom-call | flops 6291456 | bytes 8388608 | tf_op jit(solution)/shard_map/slopes_3/pallas_call | solution.py:518
  67.2 1.5 %collective-permute-done.12.refs_9_ = f32[40,128]{1,0:T(8,128)S(1)} collective-permute-done((f32[40,128]{1,0:T(8,128)S(1)}, f32[40,128]{1,0:T(8,128)S(1)}, u32[]{:S(2)}, u32[]{:S(2)}) %collective-permute-start.12) | collective-permute-done | bytes 20512 | tf_op jit(solution)/shard_map/ppermute | solution.py:946
  69.9 3.9 %backward_3.1 = (bf16[1024,1024]{1,0:T(8,128)(2,1)S(1)}, bf16[2,64,256]{2,1,0:T(8,128)(2,1)S(1)}, f32[8,128]{1,0:T(8,128)S(1)}) custom-call(s32[2]{0:T(128)S(1)} %pad_add_fusion.info, s32[16]{0:T(128)S(1)} %copy-done.10, f32[16]{0:T(128)S(1)} %copy-done.11, f32[1024,1024]{1,0:T(8,128)S(1)} %get-tuple-element.183.refs_0_, f32[1024,768]{1,0:T(8,128)S(1)} %slopes_3.1.refs_1_, ...), custom_call_target="tpu_custom_call" | custom-call | flops 704643072 | bytes 8388608 | tf_op jit(solution)/shard_map/backward_3/pallas_call | solution.py:518
  74.5 1.9 %grads_3.1 = (f32[256,384]{1,0:T(8,128)S(1)}, f32[384,384]{1,0:T(8,128)S(1)}, f32[384,256]{1,0:T(8,128)S(1)}, f32[8,1024]{1,0:T(8,128)S(1)}) custom-call(s32[2]{0:T(128)S(1)} %pad_add_fusion.info, f32[1024,1024]{1,0:T(8,128)S(1)} %get-tuple-element.183.refs_0_, bf16[1024,1024]{1,0:T(8,128)(2,1)S(1)} %get-tuple-element.186.refs_1_, f32[2,1024]{1,0:T(2,128)S(1)} %copy-done.3), custom_call_target="tpu_custom_call" | custom-call | flops 704643072 | bytes 8388608 | tf_op jit(solution)/shard_map/grads_3/pallas_call | solution.py:518
  76.4 1.9 %collective-permute-done.15.refs_16_ = bf16[2,64,256]{2,1,0:T(8,128)(2,1)S(1)} collective-permute-done((bf16[2,64,256]{2,1,0:T(8,128)(2,1)S(1)}, bf16[2,64,256]{2,1,0:T(8,128)(2,1)S(1)}, u32[]{:S(2)}, u32[]{:S(2)}) %collective-permute-start.15) | collective-permute-done | bytes 65568 | tf_op jit(solution)/shard_map/ppermute | solution.py:946
  79.6 4.2 %backward_2.1 = (bf16[1024,1024]{1,0:T(8,128)(2,1)S(1)}, bf16[2,64,256]{2,1,0:T(8,128)(2,1)S(1)}, f32[2,256,256]{2,1,0:T(8,128)S(1)}) custom-call(s32[2]{0:T(128)S(1)} %pad_add_fusion.info, s32[16]{0:T(128)S(1)} %copy-done.10, f32[16]{0:T(128)S(1)} %copy-done.11, f32[1024,1024]{1,0:T(8,128)S(1)} %get-tuple-element.181.refs_0_, ...), custom_call_target="tpu_custom_call" | custom-call | flops 704643072 | bytes 8388608 | tf_op jit(solution)/shard_map/backward_2/pallas_call | solution.py:518
  84.5 2.0 %grads_2.1 = (f32[256,384]{1,0:T(8,128)S(1)}, f32[384,384]{1,0:T(8,128)S(1)}, f32[384,256]{1,0:T(8,128)S(1)}, f32[8,1024]{1,0:T(8,128)S(1)}) custom-call(s32[2]{0:T(128)S(1)} %pad_add_fusion.info, f32[1024,1024]{1,0:T(8,128)S(1)} %get-tuple-element.181.refs_0_, ...), custom_call_target="tpu_custom_call", output_to_operand_aliasing={{0}: (4, {}), {1}: (5, {}), {2}: (6, {}), {3}: (7, {})} | custom-call | flops 704643072 | bytes 8388608 | tf_op jit(solution)/shard_map/grads_2/pallas_call | solution.py:518
  86.5 1.8 %collective-permute-done.18.refs_16_ = bf16[2,64,256]{2,1,0:T(8,128)(2,1)S(1)} collective-permute-done((bf16[2,64,256]{2,1,0:T(8,128)(2,1)S(1)}, bf16[2,64,256]{2,1,0:T(8,128)(2,1)S(1)}, u32[]{:S(2)}, u32[]{:S(2)}) %collective-permute-start.18) | collective-permute-done | bytes 65568 | tf_op jit(solution)/shard_map/ppermute | solution.py:946
  88.3 1.2 collective-permute-done.20.refs_18_
  89.5 4.2 %backward_1.1 = (bf16[1024,1024]{1,0:T(8,128)(2,1)S(1)}, bf16[2,64,256]{2,1,0:T(8,128)(2,1)S(1)}, f32[2,256,256]{2,1,0:T(8,128)S(1)}) custom-call(s32[2]{0:T(128)S(1)} %pad_add_fusion.info, s32[16]{0:T(128)S(1)} %copy-done.10, f32[16]{0:T(128)S(1)} %copy-done.11, f32[1024,1024]{1,0:T(8,128)S(1)} %get-tuple-element.179.refs_0_, ...), custom_call_target="tpu_custom_call" | custom-call | flops 704643072 | bytes 8388608 | tf_op jit(solution)/shard_map/backward_1/pallas_call | solution.py:518
  94.5 2.0 %grads_1.1 = (f32[256,384]{1,0:T(8,128)S(1)}, f32[384,384]{1,0:T(8,128)S(1)}, f32[384,256]{1,0:T(8,128)S(1)}, f32[8,1024]{1,0:T(8,128)S(1)}) custom-call(s32[2]{0:T(128)S(1)} %pad_add_fusion.info, f32[1024,1024]{1,0:T(8,128)S(1)} %get-tuple-element.179.refs_0_, ...), custom_call_target="tpu_custom_call", output_to_operand_aliasing={{0}: (4, {}), {1}: (5, {}), {2}: (6, {}), {3}: (7, {})} | custom-call | flops 704643072 | bytes 8388608 | tf_op jit(solution)/shard_map/grads_1/pallas_call | solution.py:518
  96.5 1.7 %collective-permute-done.21.refs_16_ = bf16[2,64,256]{2,1,0:T(8,128)(2,1)S(1)} collective-permute-done((bf16[2,64,256]{2,1,0:T(8,128)(2,1)S(1)}, bf16[2,64,256]{2,1,0:T(8,128)(2,1)S(1)}, u32[]{:S(2)}, u32[]{:S(2)}) %collective-permute-start.21) | collective-permute-done | bytes 65568 | tf_op jit(solution)/shard_map/ppermute | solution.py:946
  98.3 1.2 collective-permute-done.23.refs_18_
  99.5 3.4 %backward_0.1.refs_1_ = bf16[1024,1024]{1,0:T(8,128)(2,1)S(1)} custom-call(s32[2]{0:T(128)S(1)} %pad_add_fusion.info, s32[16]{0:T(128)S(1)} %copy-done.10, f32[16]{0:T(128)S(1)} %copy-done.11, f32[1024,1024]{1,0:T(8,128)S(1)} %get-tuple-element.133.refs_0_, f32[1024,768]{1,0:T(8,128)S(1)} %slopes_0.1.refs_1_, ...), custom_call_target="tpu_custom_call" | custom-call | flops 704643072 | bytes 8388608 | tf_op jit(solution)/shard_map/backward_0/pallas_call | solution.py:518
  102.9 2.4 %grads_0.1 = (f32[1408,128]{1,0:T(8,128)S(1)}, f32[1408,128]{1,0:T(8,128)S(1)}) custom-call(s32[2]{0:T(128)S(1)} %pad_add_fusion.info, f32[1024,1024]{1,0:T(8,128)S(1)} %get-tuple-element.133.refs_0_, bf16[1024,1024]{1,0:T(8,128)(2,1)S(1)} %backward_0.1.refs_1_, f32[2,1024]{1,0:T(2,128)S(1)} %copy-done.3, f32[256,384]{1,0:T(8,128)S(1)} %get-tuple-element.216.refs_3_, ...), custom_call_target="tpu_custom_call" | custom-call | flops 704643072 | bytes 8388608 | tf_op jit(solution)/shard_map/grads_0/pallas_call | solution.py:518
  105.7 2.0 %collective-permute-done.24.got = f32[1408,128]{1,0:T(8,128)S(1)} collective-permute-done((f32[1408,128]{1,0:T(8,128)S(1)}, f32[1408,128]{1,0:T(8,128)S(1)}, u32[]{:S(2)}, u32[]{:S(2)}) %collective-permute-start.24) | collective-permute-done | bytes 720928 | tf_op jit(solution)/shard_map/ppermute | solution.py:940
  107.8 11.2 %all_to_all.15.got = bf16[8,192,128]{2,1,0:T(8,128)(2,1)S(1)} all-to-all(bf16[8,192,128]{2,1,0:T(8,128)(2,1)S(1)} %pairs.1), channel_id=1, replica_groups={{0,1,2,3,4,5,6,7},{8,9,10,11,12,13,14,15},{16,17,18,19,20,21,22,23},{24..., dimensions={0} | all-to-all | bytes 786432 | tf_op jit(solution)/shard_map/all_to_all | solution.py:1018
  119.1 9.9 %all_to_all.16 = bf16[8,176,128]{2,1,0:T(8,128)(2,1)S(1)} all-to-all(bf16[8,176,128]{2,1,0:T(8,128)(2,1)S(1)} %get-tuple-element.224), channel_id=1, replica_groups={{0,1,2,3,4,5,6,7},{8,9,10,11,12,13,14,15},{16,17,18,19,20,21,22,23},{24..., dimensions={0} | all-to-all | bytes 720896 | tf_op jit(solution)/shard_map/all_to_all | solution.py:1018
  130.7 3.5 %update.1 = (f32[8,128]{1,0:T(8,128)S(1)}, f32[256,384]{1,0:T(8,128)}, f32[384,384]{1,0:T(8,128)}, f32[384,256]{1,0:T(8,128)}, f32[2,1024]{1,0:T(2,128)}, /*inde...) custom-call(s32[2]{0:T(128)S(1)} %pad_add_fusion.info, ...), custom_call_target="tpu_custom_call" | custom-call | tf_op jit(solution)/shard_map/update/pallas_call | solution.py:902
  (105 shorter events, 23.5 us)
Async XLA Ops:
  0.7 26.7 %copy-start.14 = (s32[16]{0:T(128)S(1)}, s32[16]{0:T(128)}, u32[]{:S(2)}) copy-start(s32[16]{0:T(128)} %slots.1) | copy-start | bytes 196
  0.7 26.7 %copy-start.11 = (f32[16]{0:T(128)S(1)}, f32[16]{0:T(128)}, u32[]{:S(2)}) copy-start(f32[16]{0:T(128)} %quad.23) | copy-start | bytes 196
  0.7 26.7 %copy-start.10 = (s32[16]{0:T(128)S(1)}, s32[16]{0:T(128)}, u32[]{:S(2)}) copy-start(s32[16]{0:T(128)} %order.23) | copy-start | bytes 196
  0.7 27.7 %copy-start.3 = (f32[2,1024]{1,0:T(2,128)S(1)}, f32[2,1024]{1,0:T(2,128)}, u32[]{:S(2)}) copy-start(f32[2,1024]{1,0:T(2,128)} %refs_3_.1) | copy-start | bytes 24580
  0.7 25.0 %collective-permute-start.2 = (f32[2,4,8]{2,1,0:T(4,128)}, f32[2,4,8]{2,1,0:T(4,128)S(1)}, u32[]{:S(2)}, u32[]{:S(2)}) collective-permute-start(f32[2,4,8]{2,1,0:T(4,128)} %param.25), channel_id=1, source_target_pairs={{0,16},{16,0},{1,17},{17,1},{2,18},{18,2},{3,19},{19,3},{4,20},{20... | collective-permute-start | bytes 776 | tf_op jit(solution)/shard_map/ppermute | solution.py:940
  3.8 1.3 collective-permute-start
  5.8 19.8 %all-to-all-start = ((bf16[16,40,256]{2,1,0:T(8,128)(2,1)}), bf16[16,40,256]{2,1,0:T(8,128)(2,1)S(1)}, u32[]{:S(2)}, u32[]{:S(2)}) async-start(bf16[16,40,256]{2,1,0:T(8,128)(2,1)} %bitcast.5), calls=%async_computation | async-start | bytes 655360 | tf_op jit(solution)/shard_map/all_to_all | solution.py:963
  25.7 1.6 %collective-permute-start.1 = (bf16[16,40,256]{2,1,0:T(8,128)(2,1)S(1)}, bf16[16,40,256]{2,1,0:T(8,128)(2,1)S(1)}, u32[]{:S(2)}, u32[]{:S(2)}) collective-permute-start(bf16[16,40,256]{2,1,0:T(8,128)(2,1)S(1)} %all-to-all-done.got), channel_id=1, source_target_pairs={{0,16},{16,0},{1,17},{17,1},{2,18},{18,2},{3,19},{19,3},{4,20},{20... | collective-permute-start | bytes 983048 | tf_op jit(solution)/shard_map/ppermute | solution.py:940
  32.9 4.3 %collective-permute-start.3 = (bf16[2,64,256]{2,1,0:T(8,128)(2,1)S(1)}, bf16[2,64,256]{2,1,0:T(8,128)(2,1)S(1)}, u32[]{:S(2)}, u32[]{:S(2)}) collective-permute-start(bf16[2,64,256]{2,1,0:T(8,128)(2,1)S(1)} %get-tuple-element.145.refs_9_), channel_id=1, source_target_pairs={{0,1},{1,0},{2,3},{3,2},{4,5},{5,4},{6,7},{7,6},{8,9},{9,8},{10,11... | collective-permute-start | bytes 196616 | tf_op jit(solution)/shard_map/ppermute | solution.py:946
  33.6 4.9 %collective-permute-start.4 = (bf16[2,64,256]{2,1,0:T(8,128)(2,1)S(1)}, bf16[2,64,256]{2,1,0:T(8,128)(2,1)S(1)}, u32[]{:S(2)}, u32[]{:S(2)}) collective-permute-start(bf16[2,64,256]{2,1,0:T(8,128)(2,1)S(1)} %get-tuple-element.145.refs_9_), channel_id=1, source_target_pairs={{0,16},{16,0},{1,17},{17,1},{2,18},{18,2},{3,19},{19,3},{4,20},{20... | collective-permute-start | bytes 196616 | tf_op jit(solution)/shard_map/ppermute | solution.py:940
  37.3 1.3 collective-permute-start.5
  43.4 4.5 %collective-permute-start.6 = (bf16[2,64,256]{2,1,0:T(8,128)(2,1)S(1)}, bf16[2,64,256]{2,1,0:T(8,128)(2,1)S(1)}, u32[]{:S(2)}, u32[]{:S(2)}) collective-permute-start(bf16[2,64,256]{2,1,0:T(8,128)(2,1)S(1)} %get-tuple-element.157.refs_9_), channel_id=1, source_target_pairs={{0,1},{1,0},{2,3},{3,2},{4,5},{5,4},{6,7},{7,6},{8,9},{9,8},{10,11... | collective-permute-start | bytes 196616 | tf_op jit(solution)/shard_map/ppermute | solution.py:946
  44.0 5.0 %collective-permute-start.7 = (bf16[2,64,256]{2,1,0:T(8,128)(2,1)S(1)}, bf16[2,64,256]{2,1,0:T(8,128)(2,1)S(1)}, u32[]{:S(2)}, u32[]{:S(2)}) collective-permute-start(bf16[2,64,256]{2,1,0:T(8,128)(2,1)S(1)} %get-tuple-element.157.refs_9_), channel_id=1, source_target_pairs={{0,16},{16,0},{1,17},{17,1},{2,18},{18,2},{3,19},{19,3},{4,20},{20... | collective-permute-start | bytes 196616 | tf_op jit(solution)/shard_map/ppermute | solution.py:940
  47.9 1.3 collective-permute-start.8
  54.0 4.5 %collective-permute-start.9 = (bf16[2,64,256]{2,1,0:T(8,128)(2,1)S(1)}, bf16[2,64,256]{2,1,0:T(8,128)(2,1)S(1)}, u32[]{:S(2)}, u32[]{:S(2)}) collective-permute-start(bf16[2,64,256]{2,1,0:T(8,128)(2,1)S(1)} %get-tuple-element.170.refs_11_), channel_id=1, source_target_pairs={{0,1},{1,0},{2,3},{3,2},{4,5},{5,4},{6,7},{7,6},{8,9},{9,8},{10,11... | collective-permute-start | bytes 196616 | tf_op jit(solution)/shard_map/ppermute | solution.py:946
  54.7 5.0 %collective-permute-start.10 = (bf16[2,64,256]{2,1,0:T(8,128)(2,1)S(1)}, bf16[2,64,256]{2,1,0:T(8,128)(2,1)S(1)}, u32[]{:S(2)}, u32[]{:S(2)}) collective-permute-start(bf16[2,64,256]{2,1,0:T(8,128)(2,1)S(1)} %get-tuple-element.170.refs_11_), channel_id=1, source_target_pairs={{0,16},{16,0},{1,17},{17,1},{2,18},{18,2},{3,19},{19,3},{4,20},{20... | collective-permute-start | bytes 196616 | tf_op jit(solution)/shard_map/ppermute | solution.py:940
  58.5 1.3 collective-permute-start.11
  64.9 3.8 %collective-permute-start.12 = (f32[40,128]{1,0:T(8,128)S(1)}, f32[40,128]{1,0:T(8,128)S(1)}, u32[]{:S(2)}, u32[]{:S(2)}) collective-permute-start(f32[40,128]{1,0:T(8,128)S(1)} %get-tuple-element.174.refs_8_), channel_id=1, source_target_pairs={{0,1},{1,0},{2,3},{3,2},{4,5},{5,4},{6,7},{7,6},{8,9},{9,8},{10,11... | collective-permute-start | bytes 61448 | tf_op jit(solution)/shard_map/ppermute | solution.py:946
  65.5 3.2 %collective-permute-start.13 = (f32[40,128]{1,0:T(8,128)S(1)}, f32[40,128]{1,0:T(8,128)S(1)}, u32[]{:S(2)}, u32[]{:S(2)}) collective-permute-start(f32[40,128]{1,0:T(8,128)S(1)} %get-tuple-element.174.refs_8_), channel_id=1, source_target_pairs={{0,16},{16,0},{1,17},{17,1},{2,18},{18,2},{3,19},{19,3},{4,20},{20... | collective-permute-start | bytes 61448 | tf_op jit(solution)/shard_map/ppermute | solution.py:940
  68.7 1.2 collective-permute-start.14
  73.8 4.5 %collective-permute-start.16 = (bf16[2,64,256]{2,1,0:T(8,128)(2,1)S(1)}, bf16[2,64,256]{2,1,0:T(8,128)(2,1)S(1)}, u32[]{:S(2)}, u32[]{:S(2)}) collective-permute-start(bf16[2,64,256]{2,1,0:T(8,128)(2,1)S(1)} %get-tuple-element.185.refs_15_), channel_id=1, source_target_pairs={{0,16},{16,0},{1,17},{17,1},{2,18},{18,2},{3,19},{19,3},{4,20},{20... | collective-permute-start | bytes 196616 | tf_op jit(solution)/shard_map/ppermute | solution.py:940
  74.0 4.3 %collective-permute-start.15 = (bf16[2,64,256]{2,1,0:T(8,128)(2,1)S(1)}, bf16[2,64,256]{2,1,0:T(8,128)(2,1)S(1)}, u32[]{:S(2)}, u32[]{:S(2)}) collective-permute-start(bf16[2,64,256]{2,1,0:T(8,128)(2,1)S(1)} %get-tuple-element.185.refs_15_), channel_id=1, source_target_pairs={{0,1},{1,0},{2,3},{3,2},{4,5},{5,4},{6,7},{7,6},{8,9},{9,8},{10,11... | collective-permute-start | bytes 196616 | tf_op jit(solution)/shard_map/ppermute | solution.py:946
  78.3 1.3 collective-permute-start.17
  83.7 4.5 %collective-permute-start.19 = (bf16[2,64,256]{2,1,0:T(8,128)(2,1)S(1)}, bf16[2,64,256]{2,1,0:T(8,128)(2,1)S(1)}, u32[]{:S(2)}, u32[]{:S(2)}) collective-permute-start(bf16[2,64,256]{2,1,0:T(8,128)(2,1)S(1)} %get-tuple-element.192.refs_15_), channel_id=1, source_target_pairs={{0,16},{16,0},{1,17},{17,1},{2,18},{18,2},{3,19},{19,3},{4,20},{20... | collective-permute-start | bytes 196616 | tf_op jit(solution)/shard_map/ppermute | solution.py:940
  83.9 4.4 %collective-permute-start.18 = (bf16[2,64,256]{2,1,0:T(8,128)(2,1)S(1)}, bf16[2,64,256]{2,1,0:T(8,128)(2,1)S(1)}, u32[]{:S(2)}, u32[]{:S(2)}) collective-permute-start(bf16[2,64,256]{2,1,0:T(8,128)(2,1)S(1)} %get-tuple-element.192.refs_15_), channel_id=1, source_target_pairs={{0,1},{1,0},{2,3},{3,2},{4,5},{5,4},{6,7},{7,6},{8,9},{9,8},{10,11... | collective-permute-start | bytes 196616 | tf_op jit(solution)/shard_map/ppermute | solution.py:946
  88.3 1.3 collective-permute-start.20
  93.7 4.5 %collective-permute-start.22 = (bf16[2,64,256]{2,1,0:T(8,128)(2,1)S(1)}, bf16[2,64,256]{2,1,0:T(8,128)(2,1)S(1)}, u32[]{:S(2)}, u32[]{:S(2)}) collective-permute-start(bf16[2,64,256]{2,1,0:T(8,128)(2,1)S(1)} %get-tuple-element.204.refs_15_), channel_id=1, source_target_pairs={{0,16},{16,0},{1,17},{17,1},{2,18},{18,2},{3,19},{19,3},{4,20},{20... | collective-permute-start | bytes 196616 | tf_op jit(solution)/shard_map/ppermute | solution.py:940
  93.9 4.4 %collective-permute-start.21 = (bf16[2,64,256]{2,1,0:T(8,128)(2,1)S(1)}, bf16[2,64,256]{2,1,0:T(8,128)(2,1)S(1)}, u32[]{:S(2)}, u32[]{:S(2)}) collective-permute-start(bf16[2,64,256]{2,1,0:T(8,128)(2,1)S(1)} %get-tuple-element.204.refs_15_), channel_id=1, source_target_pairs={{0,1},{1,0},{2,3},{3,2},{4,5},{5,4},{6,7},{7,6},{8,9},{9,8},{10,11... | collective-permute-start | bytes 196616 | tf_op jit(solution)/shard_map/ppermute | solution.py:946
  98.3 1.3 collective-permute-start.23
  105.3 25.3 %copy-start.1 = (f32[256,384]{1,0:T(8,128)S(1)}, f32[256,384]{1,0:T(8,128)}, u32[]{:S(2)}) copy-start(f32[256,384]{1,0:T(8,128)} %refs_0_.1) | copy-start | bytes 1179652
  105.4 2.3 %collective-permute-start.24 = (f32[1408,128]{1,0:T(8,128)S(1)}, f32[1408,128]{1,0:T(8,128)S(1)}, u32[]{:S(2)}, u32[]{:S(2)}) collective-permute-start(f32[1408,128]{1,0:T(8,128)S(1)} %get-tuple-element.221), channel_id=1, source_target_pairs={{0,16},{16,0},{1,17},{17,1},{2,18},{18,2},{3,19},{19,3},{4,20},{20... | collective-permute-start | bytes 2162696 | tf_op jit(solution)/shard_map/ppermute | solution.py:940
  128.9 1.7 %collective-permute-start.25 = (bf16[1408,128]{1,0:T(8,128)(2,1)S(1)}, bf16[1408,128]{1,0:T(8,128)(2,1)S(1)}, u32[]{:S(2)}, u32[]{:S(2)}) collective-permute-start(bf16[1408,128]{1,0:T(8,128)(2,1)S(1)} %bitcast.21), channel_id=1, source_target_pairs={{0,16},{16,0},{1,17},{17,1},{2,18},{18,2},{3,19},{19,3},{4,20},{20... | collective-permute-start | bytes 1081352 | tf_op jit(solution)/shard_map/ppermute | solution.py:940
  (11 other events, 268.8 us)

commit v4 on v3

--- a/solution.py
+++ b/solution.py
@@ -247,7 +247,7 @@
 GROUP = 2
 SUB = 256
 CHUNK = 32
-ROWS_BLOCK = 2
+ROWS_BLOCK = 4
 VMEM_LIMIT = 10 << 20
 SAVED_LIMIT = 96 << 20
 

time: 135 us -> 130 us (0.963)
  Pallas kernels: 57.7 us -> 53.1 us
    pallas_call x19, Pallas kernels: 52.9 us -> 48.4 us  [step_call(): pl.pallas_call(kernel, out_shape=shapes, grid_spec=pltpu.PrefetchScalarGr...]
where the time goes in v4:
time: 130 us
  Pallas kernels  53.1 us (41%)
  waiting for transfers between devices  32 us (25%)
  blocking collectives  21.1 us (16%)
  starting transfers between devices  14.1 us (11%)
  other arithmetic  5.43 us (4%)
  local copies, waits for them, and re-layouts  2.86 us (2%)
    pallas_call x19, Pallas kernels, step_call(): pl.pallas_call(kernel, out_shape=shapes, grid_spec=pltpu.PrefetchScalarGr...  48.4 us
    all_to_all x2, blocking collectives, grouped_device(): lax.all_to_all(a, 'lat', split_axis=0, concat_axis=0, tiled=True, axis_in...  21.1 us
    ppermute x7, waiting for transfers between devices, to_members(): lax.ppermute(v, 'lat', [(n, n ^ bit) for n in range(waves)])  12.9 us
    ppermute x19, waiting for transfers between devices, grouped_device(): across = lambda a: lax.ppermute(a, 'tm', swap)  10.4 us
    all_to_all x1, waiting for transfers between devices, grouped_device(): lax.all_to_all(spread.reshape(waves, *times.shape[1:]), 'lat', split_axis...  8.69 us
    all_to_all x1, starting transfers between devices, grouped_device(): lax.all_to_all(spread.reshape(waves, *times.shape[1:]), 'lat', split_axis...  8.01 us
    ppermute x7, starting transfers between devices, to_members(): lax.ppermute(v, 'lat', [(n, n ^ bit) for n in range(waves)])  4.12 us
    pallas_call x3, Pallas kernels, small_call(): pl.pallas_call(kernel, out_shape=shapes, grid_spec=pltpu.PrefetchScalarGr...  3.69 us
  transfers between devices with their start and end apart: 27, of which 19 were waited for; matrix products, arithmetic and copies ran while one was open for 6% of the time, Pallas kernels for 12%

profile of v4, /device:TPU:0, one launch (start us, length us, event | category | flops | bytes accessed | tf_op | source)
XLA Modules:
  0.0 129.6 jit_solution(219103606270915820)
XLA Ops:
  5.8 8.0 %all-to-all-start = ((bf16[16,40,256]{2,1,0:T(8,128)(2,1)}), bf16[16,40,256]{2,1,0:T(8,128)(2,1)S(1)}, u32[]{:S(2)}, u32[]{:S(2)}) async-start(bf16[16,40,256]{2,1,0:T(8,128)(2,1)} %bitcast.5), calls=%async_computation | async-start | bytes 655360 | tf_op jit(solution)/shard_map/all_to_all | solution.py:963
  17.0 8.7 %all-to-all-done.got = bf16[16,40,256]{2,1,0:T(8,128)(2,1)S(1)} async-done(((bf16[16,40,256]{2,1,0:T(8,128)(2,1)}), bf16[16,40,256]{2,1,0:T(8,128)(2,1)S(1)}, u32[]{:S(2)}, u32[]{:S(2)}) %all-to-all-start) | async-done | bytes 327712 | tf_op jit(solution)/shard_map/all_to_all | solution.py:963
  25.8 1.5 %collective-permute-done.1.got_o = bf16[16,40,256]{2,1,0:T(8,128)(2,1)S(1)} collective-permute-done((bf16[16,40,256]{2,1,0:T(8,128)(2,1)S(1)}, bf16[16,40,256]{2,1,0:T(8,128)(2,1)S(1)}, u32[]{:S(2)}, u32[]{:S(2)}) %collective-permute-start.1) | collective-permute-done | bytes 327712 | tf_op jit(solution)/shard_map/ppermute | solution.py:940
  28.5 3.6 %forward_0.1 = (f32[1024,1024]{1,0:T(8,128)S(1)}, f32[1024,768]{1,0:T(8,128)S(1)}, f32[1024,384]{1,0:T(8,128)S(1)}, bf16[2,64,256]{2,1,0:T(8,128)(2,1)S(1)}, f32...) custom-call(s32[2]{0:T(128)S(1)} %pad_add_fusion.info, s32[16]{0:T(128)S(1)} %copy-done.10, f32[16]{0:T(128)S(1)} %copy-done.11, ...), custom_call_target="tpu_custom_call" | custom-call | flops 704643072 | bytes 8388608 | tf_op jit(solution)/shard_map/forward_0/pallas_call | solution.py:518
  32.7 1.5 %slopes_0.1.refs_1_ = f32[1024,768]{1,0:T(8,128)S(1)} custom-call(f32[1024,768]{1,0:T(8,128)S(1)} %get-tuple-element.135.inners, f32[1024,384]{1,0:T(8,128)S(1)} %get-tuple-element.136.scales.refs_2_), custom_call_target="tpu_custom_call", output_to_operand_aliasing={{}: (0, {})} | custom-call | flops 6291456 | bytes 8388608 | tf_op jit(solution)/shard_map/slopes_0/pallas_call | solution.py:518
  34.2 2.1 %collective-permute-done.3.refs_10_ = bf16[2,64,256]{2,1,0:T(8,128)(2,1)S(1)} collective-permute-done((bf16[2,64,256]{2,1,0:T(8,128)(2,1)S(1)}, bf16[2,64,256]{2,1,0:T(8,128)(2,1)S(1)}, u32[]{:S(2)}, u32[]{:S(2)}) %collective-permute-start.3) | collective-permute-done | bytes 65568 | tf_op jit(solution)/shard_map/ppermute | solution.py:946
  37.6 4.0 %forward_1.1 = (f32[1024,1024]{1,0:T(8,128)S(1)}, f32[1024,768]{1,0:T(8,128)S(1)}, f32[1024,384]{1,0:T(8,128)S(1)}, bf16[2,64,256]{2,1,0:T(8,128)(2,1)S(1)}, f32...) custom-call(s32[2]{0:T(128)S(1)} %pad_add_fusion.info, s32[16]{0:T(128)S(1)} %copy-done.10, ...), custom_call_target="tpu_custom_call" | custom-call | flops 704643072 | bytes 8388608 | tf_op jit(solution)/shard_map/forward_1/pallas_call | solution.py:518
  42.3 1.5 %slopes_1.1.refs_1_ = f32[1024,768]{1,0:T(8,128)S(1)} custom-call(f32[1024,768]{1,0:T(8,128)S(1)} %get-tuple-element.151.inners, f32[1024,384]{1,0:T(8,128)S(1)} %get-tuple-element.152.scales.refs_2_), custom_call_target="tpu_custom_call", output_to_operand_aliasing={{}: (0, {})} | custom-call | flops 6291456 | bytes 8388608 | tf_op jit(solution)/shard_map/slopes_1/pallas_call | solution.py:518
  43.9 2.2 %collective-permute-done.6.refs_10_ = bf16[2,64,256]{2,1,0:T(8,128)(2,1)S(1)} collective-permute-done((bf16[2,64,256]{2,1,0:T(8,128)(2,1)S(1)}, bf16[2,64,256]{2,1,0:T(8,128)(2,1)S(1)}, u32[]{:S(2)}, u32[]{:S(2)}) %collective-permute-start.6) | collective-permute-done | bytes 65568 | tf_op jit(solution)/shard_map/ppermute | solution.py:946
  47.3 4.0 %forward_2.1 = (f32[1024,1024]{1,0:T(8,128)S(1)}, f32[1024,768]{1,0:T(8,128)S(1)}, f32[1024,384]{1,0:T(8,128)S(1)}, bf16[2,64,256]{2,1,0:T(8,128)(2,1)S(1)}, f32...) custom-call(s32[2]{0:T(128)S(1)} %pad_add_fusion.info, s32[16]{0:T(128)S(1)} %copy-done.10, ...), custom_call_target="tpu_custom_call" | custom-call | flops 704643072 | bytes 8388608 | tf_op jit(solution)/shard_map/forward_2/pallas_call | solution.py:518
  52.0 1.7 %slopes_2.1.refs_1_ = f32[1024,768]{1,0:T(8,128)S(1)} custom-call(f32[1024,768]{1,0:T(8,128)S(1)} %get-tuple-element.163.inners, f32[1024,384]{1,0:T(8,128)S(1)} %get-tuple-element.164.scales.refs_2_), custom_call_target="tpu_custom_call", output_to_operand_aliasing={{}: (0, {})} | custom-call | flops 6291456 | bytes 8388608 | tf_op jit(solution)/shard_map/slopes_2/pallas_call | solution.py:518
  53.8 2.0 %collective-permute-done.9.refs_12_ = bf16[2,64,256]{2,1,0:T(8,128)(2,1)S(1)} collective-permute-done((bf16[2,64,256]{2,1,0:T(8,128)(2,1)S(1)}, bf16[2,64,256]{2,1,0:T(8,128)(2,1)S(1)}, u32[]{:S(2)}, u32[]{:S(2)}) %collective-permute-start.9) | collective-permute-done | bytes 65568 | tf_op jit(solution)/shard_map/ppermute | solution.py:946
  57.0 4.4 %forward_3.1 = (f32[1024,1024]{1,0:T(8,128)S(1)}, f32[1024,768]{1,0:T(8,128)S(1)}, f32[1024,384]{1,0:T(8,128)S(1)}, f32[40,128]{1,0:T(8,128)S(1)}) custom-call(s32[2]{0:T(128)S(1)} %pad_add_fusion.info, s32[16]{0:T(128)S(1)} %copy-done.10, f32[16]{0:T(128)S(1)} %copy-done.11, f32[2,256,256]{2,1,0:T(8,128)S(1)} %get-tuple-element.161.refs_0_, ...), custom_call_target="tpu_custom_call" | custom-call | flops 704643072 | bytes 8388608 | tf_op jit(solution)/shard_map/forward_3/pallas_call | solution.py:518
  62.1 1.5 %slopes_3.1.refs_1_ = f32[1024,768]{1,0:T(8,128)S(1)} custom-call(f32[1024,768]{1,0:T(8,128)S(1)} %get-tuple-element.175.inners, f32[1024,384]{1,0:T(8,128)S(1)} %get-tuple-element.176.scales.refs_2_), custom_call_target="tpu_custom_call", output_to_operand_aliasing={{}: (0, {})} | custom-call | flops 6291456 | bytes 8388608 | tf_op jit(solution)/shard_map/slopes_3/pallas_call | solution.py:518
  63.7 1.5 %collective-permute-done.12.refs_9_ = f32[40,128]{1,0:T(8,128)S(1)} collective-permute-done((f32[40,128]{1,0:T(8,128)S(1)}, f32[40,128]{1,0:T(8,128)S(1)}, u32[]{:S(2)}, u32[]{:S(2)}) %collective-permute-start.12) | collective-permute-done | bytes 20512 | tf_op jit(solution)/shard_map/ppermute | solution.py:946
  66.4 3.3 %backward_3.1 = (bf16[1024,1024]{1,0:T(8,128)(2,1)S(1)}, bf16[2,64,256]{2,1,0:T(8,128)(2,1)S(1)}, f32[8,128]{1,0:T(8,128)S(1)}) custom-call(s32[2]{0:T(128)S(1)} %pad_add_fusion.info, s32[16]{0:T(128)S(1)} %copy-done.10, f32[16]{0:T(128)S(1)} %copy-done.11, f32[1024,1024]{1,0:T(8,128)S(1)} %get-tuple-element.183.refs_0_, f32[1024,768]{1,0:T(8,128)S(1)} %slopes_3.1.refs_1_, ...), custom_call_target="tpu_custom_call" | custom-call | flops 704643072 | bytes 8388608 | tf_op jit(solution)/shard_map/backward_3/pallas_call | solution.py:518
  70.4 1.9 %grads_3.1 = (f32[256,384]{1,0:T(8,128)S(1)}, f32[384,384]{1,0:T(8,128)S(1)}, f32[384,256]{1,0:T(8,128)S(1)}, f32[8,1024]{1,0:T(8,128)S(1)}) custom-call(s32[2]{0:T(128)S(1)} %pad_add_fusion.info, f32[1024,1024]{1,0:T(8,128)S(1)} %get-tuple-element.183.refs_0_, bf16[1024,1024]{1,0:T(8,128)(2,1)S(1)} %get-tuple-element.186.refs_1_, f32[2,1024]{1,0:T(2,128)S(1)} %copy-done.3), custom_call_target="tpu_custom_call" | custom-call | flops 704643072 | bytes 8388608 | tf_op jit(solution)/shard_map/grads_3/pallas_call | solution.py:518
  72.3 1.9 %collective-permute-done.15.refs_16_ = bf16[2,64,256]{2,1,0:T(8,128)(2,1)S(1)} collective-permute-done((bf16[2,64,256]{2,1,0:T(8,128)(2,1)S(1)}, bf16[2,64,256]{2,1,0:T(8,128)(2,1)S(1)}, u32[]{:S(2)}, u32[]{:S(2)}) %collective-permute-start.15) | collective-permute-done | bytes 65568 | tf_op jit(solution)/shard_map/ppermute | solution.py:946
  74.2 1.2 collective-permute-done.17.refs_18_
  75.4 3.9 %backward_2.1 = (bf16[1024,1024]{1,0:T(8,128)(2,1)S(1)}, bf16[2,64,256]{2,1,0:T(8,128)(2,1)S(1)}, f32[2,256,256]{2,1,0:T(8,128)S(1)}) custom-call(s32[2]{0:T(128)S(1)} %pad_add_fusion.info, s32[16]{0:T(128)S(1)} %copy-done.10, f32[16]{0:T(128)S(1)} %copy-done.11, f32[1024,1024]{1,0:T(8,128)S(1)} %get-tuple-element.181.refs_0_, ...), custom_call_target="tpu_custom_call" | custom-call | flops 704643072 | bytes 8388608 | tf_op jit(solution)/shard_map/backward_2/pallas_call | solution.py:518
  80.1 2.0 %grads_2.1 = (f32[256,384]{1,0:T(8,128)S(1)}, f32[384,384]{1,0:T(8,128)S(1)}, f32[384,256]{1,0:T(8,128)S(1)}, f32[8,1024]{1,0:T(8,128)S(1)}) custom-call(s32[2]{0:T(128)S(1)} %pad_add_fusion.info, f32[1024,1024]{1,0:T(8,128)S(1)} %get-tuple-element.181.refs_0_, ...), custom_call_target="tpu_custom_call", output_to_operand_aliasing={{0}: (4, {}), {1}: (5, {}), {2}: (6, {}), {3}: (7, {})} | custom-call | flops 704643072 | bytes 8388608 | tf_op jit(solution)/shard_map/grads_2/pallas_call | solution.py:518
  82.1 1.7 %collective-permute-done.18.refs_16_ = bf16[2,64,256]{2,1,0:T(8,128)(2,1)S(1)} collective-permute-done((bf16[2,64,256]{2,1,0:T(8,128)(2,1)S(1)}, bf16[2,64,256]{2,1,0:T(8,128)(2,1)S(1)}, u32[]{:S(2)}, u32[]{:S(2)}) %collective-permute-start.18) | collective-permute-done | bytes 65568 | tf_op jit(solution)/shard_map/ppermute | solution.py:946
  83.9 1.2 collective-permute-done.20.refs_18_
  85.1 3.9 %backward_1.1 = (bf16[1024,1024]{1,0:T(8,128)(2,1)S(1)}, bf16[2,64,256]{2,1,0:T(8,128)(2,1)S(1)}, f32[2,256,256]{2,1,0:T(8,128)S(1)}) custom-call(s32[2]{0:T(128)S(1)} %pad_add_fusion.info, s32[16]{0:T(128)S(1)} %copy-done.10, f32[16]{0:T(128)S(1)} %copy-done.11, f32[1024,1024]{1,0:T(8,128)S(1)} %get-tuple-element.179.refs_0_, ...), custom_call_target="tpu_custom_call" | custom-call | flops 704643072 | bytes 8388608 | tf_op jit(solution)/shard_map/backward_1/pallas_call | solution.py:518
  89.7 2.2 %grads_1.1 = (f32[256,384]{1,0:T(8,128)S(1)}, f32[384,384]{1,0:T(8,128)S(1)}, f32[384,256]{1,0:T(8,128)S(1)}, f32[8,1024]{1,0:T(8,128)S(1)}) custom-call(s32[2]{0:T(128)S(1)} %pad_add_fusion.info, f32[1024,1024]{1,0:T(8,128)S(1)} %get-tuple-element.179.refs_0_, ...), custom_call_target="tpu_custom_call", output_to_operand_aliasing={{0}: (4, {}), {1}: (5, {}), {2}: (6, {}), {3}: (7, {})} | custom-call | flops 704643072 | bytes 8388608 | tf_op jit(solution)/shard_map/grads_1/pallas_call | solution.py:518
  92.0 1.5 %collective-permute-done.21.refs_16_ = bf16[2,64,256]{2,1,0:T(8,128)(2,1)S(1)} collective-permute-done((bf16[2,64,256]{2,1,0:T(8,128)(2,1)S(1)}, bf16[2,64,256]{2,1,0:T(8,128)(2,1)S(1)}, u32[]{:S(2)}, u32[]{:S(2)}) %collective-permute-start.21) | collective-permute-done | bytes 65568 | tf_op jit(solution)/shard_map/ppermute | solution.py:946
  94.8 2.9 %backward_0.1.refs_1_ = bf16[1024,1024]{1,0:T(8,128)(2,1)S(1)} custom-call(s32[2]{0:T(128)S(1)} %pad_add_fusion.info, s32[16]{0:T(128)S(1)} %copy-done.10, f32[16]{0:T(128)S(1)} %copy-done.11, f32[1024,1024]{1,0:T(8,128)S(1)} %get-tuple-element.133.refs_0_, f32[1024,768]{1,0:T(8,128)S(1)} %slopes_0.1.refs_1_, ...), custom_call_target="tpu_custom_call" | custom-call | flops 704643072 | bytes 8388608 | tf_op jit(solution)/shard_map/backward_0/pallas_call | solution.py:518
  97.7 2.4 %grads_0.1 = (f32[1408,128]{1,0:T(8,128)S(1)}, f32[1408,128]{1,0:T(8,128)S(1)}) custom-call(s32[2]{0:T(128)S(1)} %pad_add_fusion.info, f32[1024,1024]{1,0:T(8,128)S(1)} %get-tuple-element.133.refs_0_, bf16[1024,1024]{1,0:T(8,128)(2,1)S(1)} %backward_0.1.refs_1_, f32[2,1024]{1,0:T(2,128)S(1)} %copy-done.3, f32[256,384]{1,0:T(8,128)S(1)} %get-tuple-element.216.refs_3_, ...), custom_call_target="tpu_custom_call" | custom-call | flops 704643072 | bytes 8388608 | tf_op jit(solution)/shard_map/grads_0/pallas_call | solution.py:518
  100.5 2.0 %collective-permute-done.24.got = f32[1408,128]{1,0:T(8,128)S(1)} collective-permute-done((f32[1408,128]{1,0:T(8,128)S(1)}, f32[1408,128]{1,0:T(8,128)S(1)}, u32[]{:S(2)}, u32[]{:S(2)}) %collective-permute-start.24) | collective-permute-done | bytes 720928 | tf_op jit(solution)/shard_map/ppermute | solution.py:940
  102.7 11.2 %all_to_all.15.got = bf16[8,192,128]{2,1,0:T(8,128)(2,1)S(1)} all-to-all(bf16[8,192,128]{2,1,0:T(8,128)(2,1)S(1)} %pairs.1), channel_id=1, replica_groups={{0,1,2,3,4,5,6,7},{8,9,10,11,12,13,14,15},{16,17,18,19,20,21,22,23},{24..., dimensions={0} | all-to-all | bytes 786432 | tf_op jit(solution)/shard_map/all_to_all | solution.py:1018
  113.9 9.9 %all_to_all.16 = bf16[8,176,128]{2,1,0:T(8,128)(2,1)S(1)} all-to-all(bf16[8,176,128]{2,1,0:T(8,128)(2,1)S(1)} %get-tuple-element.224), channel_id=1, replica_groups={{0,1,2,3,4,5,6,7},{8,9,10,11,12,13,14,15},{16,17,18,19,20,21,22,23},{24..., dimensions={0} | all-to-all | bytes 720896 | tf_op jit(solution)/shard_map/all_to_all | solution.py:1018
  125.6 3.5 %update.1 = (f32[8,128]{1,0:T(8,128)S(1)}, f32[256,384]{1,0:T(8,128)}, f32[384,384]{1,0:T(8,128)}, f32[384,256]{1,0:T(8,128)}, f32[2,1024]{1,0:T(2,128)}, /*inde...) custom-call(s32[2]{0:T(128)S(1)} %pad_add_fusion.info, ...), custom_call_target="tpu_custom_call" | custom-call | tf_op jit(solution)/shard_map/update/pallas_call | solution.py:902
  (105 shorter events, 23.4 us)
Async XLA Ops:
  0.7 26.7 %copy-start.14 = (s32[16]{0:T(128)S(1)}, s32[16]{0:T(128)}, u32[]{:S(2)}) copy-start(s32[16]{0:T(128)} %slots.1) | copy-start | bytes 196
  0.7 26.7 %copy-start.11 = (f32[16]{0:T(128)S(1)}, f32[16]{0:T(128)}, u32[]{:S(2)}) copy-start(f32[16]{0:T(128)} %quad.23) | copy-start | bytes 196
  0.7 26.7 %copy-start.10 = (s32[16]{0:T(128)S(1)}, s32[16]{0:T(128)}, u32[]{:S(2)}) copy-start(s32[16]{0:T(128)} %order.23) | copy-start | bytes 196
  0.7 27.7 %copy-start.3 = (f32[2,1024]{1,0:T(2,128)S(1)}, f32[2,1024]{1,0:T(2,128)}, u32[]{:S(2)}) copy-start(f32[2,1024]{1,0:T(2,128)} %refs_3_.1) | copy-start | bytes 24580
  0.7 25.0 %collective-permute-start.2 = (f32[2,4,8]{2,1,0:T(4,128)}, f32[2,4,8]{2,1,0:T(4,128)S(1)}, u32[]{:S(2)}, u32[]{:S(2)}) collective-permute-start(f32[2,4,8]{2,1,0:T(4,128)} %param.25), channel_id=1, source_target_pairs={{0,16},{16,0},{1,17},{17,1},{2,18},{18,2},{3,19},{19,3},{4,20},{20... | collective-permute-start | bytes 776 | tf_op jit(solution)/shard_map/ppermute | solution.py:940
  3.8 1.3 collective-permute-start
  5.8 19.8 %all-to-all-start = ((bf16[16,40,256]{2,1,0:T(8,128)(2,1)}), bf16[16,40,256]{2,1,0:T(8,128)(2,1)S(1)}, u32[]{:S(2)}, u32[]{:S(2)}) async-start(bf16[16,40,256]{2,1,0:T(8,128)(2,1)} %bitcast.5), calls=%async_computation | async-start | bytes 655360 | tf_op jit(solution)/shard_map/all_to_all | solution.py:963
  25.7 1.6 %collective-permute-start.1 = (bf16[16,40,256]{2,1,0:T(8,128)(2,1)S(1)}, bf16[16,40,256]{2,1,0:T(8,128)(2,1)S(1)}, u32[]{:S(2)}, u32[]{:S(2)}) collective-permute-start(bf16[16,40,256]{2,1,0:T(8,128)(2,1)S(1)} %all-to-all-done.got), channel_id=1, source_target_pairs={{0,16},{16,0},{1,17},{17,1},{2,18},{18,2},{3,19},{19,3},{4,20},{20... | collective-permute-start | bytes 983048 | tf_op jit(solution)/shard_map/ppermute | solution.py:940
  32.1 4.3 %collective-permute-start.3 = (bf16[2,64,256]{2,1,0:T(8,128)(2,1)S(1)}, bf16[2,64,256]{2,1,0:T(8,128)(2,1)S(1)}, u32[]{:S(2)}, u32[]{:S(2)}) collective-permute-start(bf16[2,64,256]{2,1,0:T(8,128)(2,1)S(1)} %get-tuple-element.145.refs_9_), channel_id=1, source_target_pairs={{0,1},{1,0},{2,3},{3,2},{4,5},{5,4},{6,7},{7,6},{8,9},{9,8},{10,11... | collective-permute-start | bytes 196616 | tf_op jit(solution)/shard_map/ppermute | solution.py:946
  32.7 4.9 %collective-permute-start.4 = (bf16[2,64,256]{2,1,0:T(8,128)(2,1)S(1)}, bf16[2,64,256]{2,1,0:T(8,128)(2,1)S(1)}, u32[]{:S(2)}, u32[]{:S(2)}) collective-permute-start(bf16[2,64,256]{2,1,0:T(8,128)(2,1)S(1)} %get-tuple-element.145.refs_9_), channel_id=1, source_target_pairs={{0,16},{16,0},{1,17},{17,1},{2,18},{18,2},{3,19},{19,3},{4,20},{20... | collective-permute-start | bytes 196616 | tf_op jit(solution)/shard_map/ppermute | solution.py:940
  36.3 1.3 collective-permute-start.5
  41.6 4.5 %collective-permute-start.6 = (bf16[2,64,256]{2,1,0:T(8,128)(2,1)S(1)}, bf16[2,64,256]{2,1,0:T(8,128)(2,1)S(1)}, u32[]{:S(2)}, u32[]{:S(2)}) collective-permute-start(bf16[2,64,256]{2,1,0:T(8,128)(2,1)S(1)} %get-tuple-element.157.refs_9_), channel_id=1, source_target_pairs={{0,1},{1,0},{2,3},{3,2},{4,5},{5,4},{6,7},{7,6},{8,9},{9,8},{10,11... | collective-permute-start | bytes 196616 | tf_op jit(solution)/shard_map/ppermute | solution.py:946
  42.2 5.0 %collective-permute-start.7 = (bf16[2,64,256]{2,1,0:T(8,128)(2,1)S(1)}, bf16[2,64,256]{2,1,0:T(8,128)(2,1)S(1)}, u32[]{:S(2)}, u32[]{:S(2)}) collective-permute-start(bf16[2,64,256]{2,1,0:T(8,128)(2,1)S(1)} %get-tuple-element.157.refs_9_), channel_id=1, source_target_pairs={{0,16},{16,0},{1,17},{17,1},{2,18},{18,2},{3,19},{19,3},{4,20},{20... | collective-permute-start | bytes 196616 | tf_op jit(solution)/shard_map/ppermute | solution.py:940
  46.0 1.3 collective-permute-start.8
  51.3 4.5 %collective-permute-start.9 = (bf16[2,64,256]{2,1,0:T(8,128)(2,1)S(1)}, bf16[2,64,256]{2,1,0:T(8,128)(2,1)S(1)}, u32[]{:S(2)}, u32[]{:S(2)}) collective-permute-start(bf16[2,64,256]{2,1,0:T(8,128)(2,1)S(1)} %get-tuple-element.170.refs_11_), channel_id=1, source_target_pairs={{0,1},{1,0},{2,3},{3,2},{4,5},{5,4},{6,7},{7,6},{8,9},{9,8},{10,11... | collective-permute-start | bytes 196616 | tf_op jit(solution)/shard_map/ppermute | solution.py:946
  51.9 5.0 %collective-permute-start.10 = (bf16[2,64,256]{2,1,0:T(8,128)(2,1)S(1)}, bf16[2,64,256]{2,1,0:T(8,128)(2,1)S(1)}, u32[]{:S(2)}, u32[]{:S(2)}) collective-permute-start(bf16[2,64,256]{2,1,0:T(8,128)(2,1)S(1)} %get-tuple-element.170.refs_11_), channel_id=1, source_target_pairs={{0,16},{16,0},{1,17},{17,1},{2,18},{18,2},{3,19},{19,3},{4,20},{20... | collective-permute-start | bytes 196616 | tf_op jit(solution)/shard_map/ppermute | solution.py:940
  55.7 1.3 collective-permute-start.11
  61.4 3.8 %collective-permute-start.12 = (f32[40,128]{1,0:T(8,128)S(1)}, f32[40,128]{1,0:T(8,128)S(1)}, u32[]{:S(2)}, u32[]{:S(2)}) collective-permute-start(f32[40,128]{1,0:T(8,128)S(1)} %get-tuple-element.174.refs_8_), channel_id=1, source_target_pairs={{0,1},{1,0},{2,3},{3,2},{4,5},{5,4},{6,7},{7,6},{8,9},{9,8},{10,11... | collective-permute-start | bytes 61448 | tf_op jit(solution)/shard_map/ppermute | solution.py:946
  62.0 3.2 %collective-permute-start.13 = (f32[40,128]{1,0:T(8,128)S(1)}, f32[40,128]{1,0:T(8,128)S(1)}, u32[]{:S(2)}, u32[]{:S(2)}) collective-permute-start(f32[40,128]{1,0:T(8,128)S(1)} %get-tuple-element.174.refs_8_), channel_id=1, source_target_pairs={{0,16},{16,0},{1,17},{17,1},{2,18},{18,2},{3,19},{19,3},{4,20},{20... | collective-permute-start | bytes 61448 | tf_op jit(solution)/shard_map/ppermute | solution.py:940
  65.2 1.2 collective-permute-start.14
  69.7 4.5 %collective-permute-start.16 = (bf16[2,64,256]{2,1,0:T(8,128)(2,1)S(1)}, bf16[2,64,256]{2,1,0:T(8,128)(2,1)S(1)}, u32[]{:S(2)}, u32[]{:S(2)}) collective-permute-start(bf16[2,64,256]{2,1,0:T(8,128)(2,1)S(1)} %get-tuple-element.185.refs_15_), channel_id=1, source_target_pairs={{0,16},{16,0},{1,17},{17,1},{2,18},{18,2},{3,19},{19,3},{4,20},{20... | collective-permute-start | bytes 196616 | tf_op jit(solution)/shard_map/ppermute | solution.py:940
  69.8 4.3 %collective-permute-start.15 = (bf16[2,64,256]{2,1,0:T(8,128)(2,1)S(1)}, bf16[2,64,256]{2,1,0:T(8,128)(2,1)S(1)}, u32[]{:S(2)}, u32[]{:S(2)}) collective-permute-start(bf16[2,64,256]{2,1,0:T(8,128)(2,1)S(1)} %get-tuple-element.185.refs_15_), channel_id=1, source_target_pairs={{0,1},{1,0},{2,3},{3,2},{4,5},{5,4},{6,7},{7,6},{8,9},{9,8},{10,11... | collective-permute-start | bytes 196616 | tf_op jit(solution)/shard_map/ppermute | solution.py:946
  74.2 1.3 collective-permute-start.17
  79.3 4.5 %collective-permute-start.19 = (bf16[2,64,256]{2,1,0:T(8,128)(2,1)S(1)}, bf16[2,64,256]{2,1,0:T(8,128)(2,1)S(1)}, u32[]{:S(2)}, u32[]{:S(2)}) collective-permute-start(bf16[2,64,256]{2,1,0:T(8,128)(2,1)S(1)} %get-tuple-element.192.refs_15_), channel_id=1, source_target_pairs={{0,16},{16,0},{1,17},{17,1},{2,18},{18,2},{3,19},{19,3},{4,20},{20... | collective-permute-start | bytes 196616 | tf_op jit(solution)/shard_map/ppermute | solution.py:940
  79.5 4.3 %collective-permute-start.18 = (bf16[2,64,256]{2,1,0:T(8,128)(2,1)S(1)}, bf16[2,64,256]{2,1,0:T(8,128)(2,1)S(1)}, u32[]{:S(2)}, u32[]{:S(2)}) collective-permute-start(bf16[2,64,256]{2,1,0:T(8,128)(2,1)S(1)} %get-tuple-element.192.refs_15_), channel_id=1, source_target_pairs={{0,1},{1,0},{2,3},{3,2},{4,5},{5,4},{6,7},{7,6},{8,9},{9,8},{10,11... | collective-permute-start | bytes 196616 | tf_op jit(solution)/shard_map/ppermute | solution.py:946
  83.9 1.3 collective-permute-start.20
  89.0 4.5 %collective-permute-start.22 = (bf16[2,64,256]{2,1,0:T(8,128)(2,1)S(1)}, bf16[2,64,256]{2,1,0:T(8,128)(2,1)S(1)}, u32[]{:S(2)}, u32[]{:S(2)}) collective-permute-start(bf16[2,64,256]{2,1,0:T(8,128)(2,1)S(1)} %get-tuple-element.204.refs_15_), channel_id=1, source_target_pairs={{0,16},{16,0},{1,17},{17,1},{2,18},{18,2},{3,19},{19,3},{4,20},{20... | collective-permute-start | bytes 196616 | tf_op jit(solution)/shard_map/ppermute | solution.py:940
  89.2 4.4 %collective-permute-start.21 = (bf16[2,64,256]{2,1,0:T(8,128)(2,1)S(1)}, bf16[2,64,256]{2,1,0:T(8,128)(2,1)S(1)}, u32[]{:S(2)}, u32[]{:S(2)}) collective-permute-start(bf16[2,64,256]{2,1,0:T(8,128)(2,1)S(1)} %get-tuple-element.204.refs_15_), channel_id=1, source_target_pairs={{0,1},{1,0},{2,3},{3,2},{4,5},{5,4},{6,7},{7,6},{8,9},{9,8},{10,11... | collective-permute-start | bytes 196616 | tf_op jit(solution)/shard_map/ppermute | solution.py:946
  93.5 1.3 collective-permute-start.23
  100.2 25.3 %copy-start.1 = (f32[256,384]{1,0:T(8,128)S(1)}, f32[256,384]{1,0:T(8,128)}, u32[]{:S(2)}) copy-start(f32[256,384]{1,0:T(8,128)} %refs_0_.1) | copy-start | bytes 1179652
  100.3 2.3 %collective-permute-start.24 = (f32[1408,128]{1,0:T(8,128)S(1)}, f32[1408,128]{1,0:T(8,128)S(1)}, u32[]{:S(2)}, u32[]{:S(2)}) collective-permute-start(f32[1408,128]{1,0:T(8,128)S(1)} %get-tuple-element.221), channel_id=1, source_target_pairs={{0,16},{16,0},{1,17},{17,1},{2,18},{18,2},{3,19},{19,3},{4,20},{20... | collective-permute-start | bytes 2162696 | tf_op jit(solution)/shard_map/ppermute | solution.py:940
  123.8 1.7 %collective-permute-start.25 = (bf16[1408,128]{1,0:T(8,128)(2,1)S(1)}, bf16[1408,128]{1,0:T(8,128)(2,1)S(1)}, u32[]{:S(2)}, u32[]{:S(2)}) collective-permute-start(bf16[1408,128]{1,0:T(8,128)(2,1)S(1)} %bitcast.21), channel_id=1, source_target_pairs={{0,16},{16,0},{1,17},{17,1},{2,18},{18,2},{3,19},{19,3},{4,20},{20... | collective-permute-start | bytes 1081352 | tf_op jit(solution)/shard_map/ppermute | solution.py:940
  (11 other events, 268.8 us)

commit v5 on v4

--- a/solution.py
+++ b/solution.py
@@ -248,6 +248,7 @@
 SUB = 256
 CHUNK = 32
 ROWS_BLOCK = 4
+UPDATE_ROWS = 32
 VMEM_LIMIT = 10 << 20
 SAVED_LIMIT = 96 << 20
 
@@ -315,6 +316,53 @@
 
 def row_weight(plan, info, order, quad, row):
     return quad[order[(info[1] * 2 + info[0]) * plan.rows + row]]
+
+
+def pack_kernel(info, state_in, seen_in, legendre_in, keep, send, state, seen, legendre, sems):
+    pairs = ((state_in, state), (seen_in, seen), (legendre_in, legendre))
+    loads = [pltpu.make_async_copy(a, b, sems.at[n]) for n, (a, b) in enumerate(pairs)]
+    for load in loads:
+        load.start()
+    for load in loads:
+        load.wait()
+    times, _, parts, degrees, chans = state.shape
+    fields = seen.shape[1]
+    lats = legendre.shape[2]
+    iota = lambda d, s: lax.broadcasted_iota(jnp.int32, s, d)
+    repeat = (iota(1, (lats, chans)) % lats == iota(0, (lats, chans))).astype(F32).astype(BF16)
+    line = dot(legendre[0], repeat)
+    line = jnp.where(iota(1, (degrees, chans)) // lats == iota(0, (degrees, chans)), line, 0.0)
+    line = jnp.sum(line, axis=0, keepdims=True)
+    half = fields // parts
+    blank = jnp.zeros((keep.shape[1] - 2 * degrees - half - 1, chans), F32)
+    mine = info[0] == 0
+    for t in range(times):
+        rows = []
+        for p in range(parts):
+            x = state[t, 0, p]
+            hi = x.astype(BF16).astype(F32)
+            there = [seen[t, f].astype(F32) for f in range(p * half, (p + 1) * half)]
+            rows.append(jnp.concatenate([hi, x - hi, *there, line, blank], axis=0))
+        keep[t] = jnp.where(mine, rows[0], rows[1]).astype(BF16)
+        send[t] = jnp.where(mine, rows[1], rows[0]).astype(BF16)
+
+
+def pack_call(info, state, seen, legendre, deep):
+    times, _, _, _, chans = state.shape
+    ins = [pltpu.with_memory_space_constraint(a, pltpu.HBM) for a in (state, seen, legendre)]
+    return pl.pallas_call(
+        pack_kernel,
+        out_shape=[VM((times, deep, chans), BF16)] * 2,
+        grid_spec=pltpu.PrefetchScalarGridSpec(
+            num_scalar_prefetch=1,
+            grid=(1,),
+            in_specs=[pl.BlockSpec(memory_space=pltpu.HBM)] * 3,
+            out_specs=[pl.BlockSpec(memory_space=VM)] * 2,
+            scratch_shapes=[VM(a.shape, a.dtype) for a in ins] + [pltpu.SemaphoreType.DMA((3,))],
+        ),
+        compiler_params=kernel_params(),
+        name="pack",
+    )(info, *ins)
 
 
 def prepare_kernel(
@@ -379,29 +427,18 @@
 def prepare_call(plan, info, slots, order, quad, got, got_o, inv, ffw, wanted):
     group, rows, waves, degrees, steps, fields, chans, _, lons = plan
     span, mine = waves * degrees, rows * waves
+    shapes = [
+        VM((2, span, chans), F32),
+        VM((span, 2 * group * mine), BF16),
+        VM((mine, span), BF16),
+        VM((rows, fields, lons), BF16),
+        VM(((steps + 1) * fields, LANES), F32),
+        VM((lons, 2 * waves), BF16),
+        VM((lons, 2 * waves), BF16),
+        VM(wanted.shape, F32),
+    ]
     ins = [got, got_o, inv, ffw, wanted]
-    shapes = [
-        jax.ShapeDtypeStruct((2, span, chans), F32),
-        jax.ShapeDtypeStruct((span, 2 * group * mine), BF16),
-        jax.ShapeDtypeStruct((mine, span), BF16),
-        jax.ShapeDtypeStruct((rows, fields, lons), BF16),
-        jax.ShapeDtypeStruct(((steps + 1) * fields, LANES), F32),
-        jax.ShapeDtypeStruct((lons, 2 * waves), BF16),
-        jax.ShapeDtypeStruct((lons, 2 * waves), BF16),
-        jax.ShapeDtypeStruct(wanted.shape, F32),
-    ]
-    return pl.pallas_call(
-        partial(prepare_kernel, plan),
-        out_shape=shapes,
-        grid_spec=pltpu.PrefetchScalarGridSpec(
-            num_scalar_prefetch=4,
-            grid=(1,),
-            in_specs=[whole(a) for a in ins],
-            out_specs=[whole(a) for a in shapes],
-        ),
-        compiler_params=kernel_params(),
-        name="prepare",
-    )(info, slots, order, quad, *ins)
+    return step_call(partial(prepare_kernel, plan), "prepare", 1, shapes, ins, (info, slots, order, quad), (span, 2 * span))
 
 
 def kernel_params():
@@ -618,6 +655,44 @@
     return out
 
 
+def shares(plan, step, counts, tgt):
+    steps, fields, chans = plan.steps, plan.fields, plan.chans
+    levels = chans // fields
+
+    def total(s):
+        acc = [c[s * fields : (s + 1) * fields, :] for c in counts]
+        while len(acc) > 1:
+            acc = [a + b for a, b in zip(acc[::2], acc[1::2])]
+        return acc[0]
+
+    den = total(steps)
+    bias_of = lambda s: total(s) / (levels * den) - tgt[s * fields : (s + 1) * fields, :]
+    gb = 2.0 * bias_of(step) / (steps * levels * den)
+    gb = jnp.where(field_mask(fields, chans), wide(gb, chans), 0.0)
+    hi = gb.astype(BF16).astype(F32)
+    return jnp.concatenate([hi, gb - hi], axis=0).astype(BF16), bias_of
+
+
+def spread_share(avail, gmask, row):
+    av2 = jnp.concatenate([avail[row].astype(F32)] * 2, axis=0).astype(BF16)
+    return dot(av2, gmask, ((0,), (0,)))
+
+
+def masks_kernel(plan, step, info, order, quad, avail, tgt, *refs):
+    rows, lons = plan.rows, plan.lons
+    counts, out = refs[:-1], refs[-1]
+    gmask, _ = shares(plan, step, counts, tgt)
+    for row in range(rows):
+        out[row * lons : (row + 1) * lons, :] = row_weight(plan, info, order, quad, row) * spread_share(avail, gmask, row)
+
+
+def masks_call(plan, step, scalars, avail, tgt, counts):
+    cols = plan.rows * plan.lons
+    shapes = [VM((cols, plan.chans), F32)]
+    work = (cols, 32 * plan.chans)
+    return step_call(partial(masks_kernel, plan, step), f"masks_{step}", 1, shapes, [avail, tgt, *counts], scalars, work)[0]
+
+
 def backward_kernel(plan, step, info, order, quad, *refs):
     group, rows, waves, _, steps, fields, chans, hidden, lons = plan
     first, last = step == steps - 1, step == 0
@@ -627,9 +702,12 @@
     levels = chans // fields
     refs = list(refs)
     take = lambda: refs.pop(0)
-    units, slopes, scales, avail, tgt, w2, w3, nb = [take() for _ in range(8)]
-    counts = [take() for _ in range(members)]
-    if not first:
+    units, slopes, scales, w2, w3, nb = [take() for _ in range(6)]
+    if first:
+        avail, tgt = take(), take()
+        counts = [take() for _ in range(members)]
+    else:
+        masks = take()
         links, lt, ffw_t = [take() for _ in range(3)]
         pieces = [take() for _ in range(members)]
         if not fresh:
@@ -642,25 +720,15 @@
         if not first:
             bstate_out = take()
     if first:
-        loss = take()
-    coef, gmask = take(), take()
+        loss, gmask = take(), take()
+    else:
+        coef = take()
     i = pl.program_id(0)
 
     @pl.when(i == 0)
     def _():
-        def total(s):
-            acc = [c[s * fields : (s + 1) * fields, :] for c in counts]
-            while len(acc) > 1:
-                acc = [a + b for a, b in zip(acc[::2], acc[1::2])]
-            return acc[0]
-
-        den = total(steps)
-        bias_of = lambda s: total(s) / (levels * den) - tgt[s * fields : (s + 1) * fields, :]
-        gb = 2.0 * bias_of(step) / (steps * levels * den)
-        gb = jnp.where(field_mask(fields, chans), wide(gb, chans), 0.0)
-        hi = gb.astype(BF16).astype(F32)
-        gmask[...] = jnp.concatenate([hi, gb - hi], axis=0).astype(BF16)
         if first:
+            gmask[...], bias_of = shares(plan, step, counts, tgt)
             sq = bias_of(0) * bias_of(0)
             for s in range(1, steps):
                 sq = sq + bias_of(s) * bias_of(s)
@@ -688,18 +756,19 @@
         q = row_weight(plan, info, order, quad, row)
         chunks = [pl.ds(pl.multiple_of(row * lons + c, CHUNK), CHUNK) for c in range(0, lons, CHUNK)]
         cut = lambda v: [v[c : c + CHUNK] for c in range(0, lons, CHUNK)]
-        av2 = jnp.concatenate([avail[row].astype(F32)] * 2, axis=0).astype(BF16)
-        mask = dot(av2, gmask[...], ((0,), (0,)))
-        if not first:
+        if first:
+            mask = cut(spread_share(avail, gmask[...], row))
+        else:
             tend = dot(ffw_t[...], jnp.concatenate([coef[0, at, :], coef[1, at, :]], axis=0))
         yield
         dpreds, low = [], []
-        for n, (cs, part) in enumerate(zip(chunks, cut(mask))):
-            dpred = q * part
+        for n, cs in enumerate(chunks):
+            dpred = q * mask[n] if first else masks[cs, :]
             dout = STEP_SCALE * dpred
-            if not first:
+            if first:
+                dpreds.append(dpred)
+            else:
                 dout = dout + q * cut(tend)[n]
-            dpreds.append(dpred)
             low.append(dout.astype(BF16))
             dzs[cs, 2 * hidden :] = low[-1]
         yield
@@ -720,7 +789,8 @@
             grids = []
             for n, (cs, part) in enumerate(zip(chunks, cut(back))):
                 dx = norm_back(part, gains[0], units[cs, 0:chans])
-                grids.append((dpreds[n] + dx * wide(scales[cs, 0:LANES], chans)).astype(BF16))
+                dpred = dpreds[n] if first else masks[cs, :]
+                grids.append((dpred + dx * wide(scales[cs, 0:LANES], chans)).astype(BF16))
             yield
             coeff = dot(inv[...], jnp.concatenate(grids, axis=0)).astype(BF16)
             b_out[0, at, :] = coeff[:waves]
@@ -730,12 +800,12 @@
     stagger([row_chain(rr) for rr in range(rows_blk)])
 
 
-def backward_call(plan, step, scalars, saved, avail, tgt, weights, nb, counts, tables, pieces, bstate):
+def backward_call(plan, step, scalars, saved, wanted, weights, nb, tables, pieces, bstate):
     group, rows, waves, degrees, steps, fields, chans, hidden, lons = plan
     first, last = step == steps - 1, step == 0
     rows_blk = pair_rows(plan)
     links, lt, ffw_t, inv = tables
-    ins = [*saved, avail, tgt, *weights[1:], nb, *counts]
+    ins = [*saved, *weights[1:], nb, *wanted]
     if not first:
         ins += [links, lt, ffw_t, *pieces]
         if step != steps - 2:
@@ -759,7 +829,7 @@
         ins,
         scalars,
         (rows * lons, flops),
-        [VM(sums, BF16), VM((2 * fields, chans), BF16)],
+        [VM((2 * fields, chans), BF16) if first else VM(sums, BF16)],
     )
 
 
@@ -863,11 +933,13 @@
     loss[...] = jnp.broadcast_to(jnp.sum(total[blk:], axis=0, keepdims=True), loss.shape)
 
 
-def update_kernel(plan, info, part, part_o, *refs):
+def update_kernel(plan, info, part, part_o, loss, *refs):
     params, means, squares = refs[0:4], refs[4:8], refs[8:12]
-    norm = refs[12]
-    masters, new_means, new_squares, halves = refs[13:17], refs[17:21], refs[21:25], refs[25:29]
-    packed = refs[29]
+    scalars = refs[12:14]
+    outs = [refs[14 + 4 * k : 18 + 4 * k] for k in range(4)]
+    packed, sems = refs[30], refs[31]
+    stage = [refs[32 + 4 * k : 36 + 4 * k] for k in range(4)]
+    ones = refs[48:50]
     packed[info[0]] = part[...]
     packed[1 - info[0]] = part_o[...]
     half = packed.shape[1]
@@ -876,26 +948,72 @@
         g = packed[h].astype(F32)
         acc = acc + jnp.sum((g * g).reshape(half // 16, 16, LANES), axis=0)
     total = jnp.sum(jnp.sum(acc, axis=0, keepdims=True), axis=1, keepdims=True)
-    root = jnp.sqrt(jnp.broadcast_to(total, (8, LANES)))
-    norm[...] = root
-    factor = (CLIP_NORM / jnp.maximum(root, CLIP_NORM))[0:1, :]
+    root = jnp.sqrt(total)
+    ones[0][...] = loss[0:1, 0:1]
+    ones[1][...] = root
+    singles = [pltpu.make_async_copy(ones[n], scalars[n], sems.at[16 + n]) for n in range(2)]
+    for copy in singles:
+        copy.start()
+    factor = jnp.broadcast_to(CLIP_NORM / jnp.maximum(root, CLIP_NORM), (1, LANES))
 
     def apply(which, rs, cs, g):
-        w, a, b = adamw(params[which][rs, cs], means[which][rs, cs], squares[which][rs, cs], g * factor)
-        masters[which][rs, cs] = w
-        new_means[which][rs, cs] = a
-        new_squares[which][rs, cs] = b
-        halves[which][rs, cs] = w.astype(BF16)
+        g = g * factor
+        w = params[which][rs, cs]
+        a = BETA_ONE * means[which][rs, cs] + (1.0 - BETA_ONE) * g
+        b = BETA_TWO * squares[which][rs, cs] + (1.0 - BETA_TWO) * g * g
+        w = w - LEARN_RATE * (a / (b * lax.rsqrt(b) + EPS_ADAM) + DECAY * w)
+        for k, value in enumerate((w, a, b, w.astype(BF16))):
+            stage[k][which][rs, cs] = value
+
+    def copies(which):
+        return [
+            pltpu.make_async_copy(stage[k][which], outs[k][which], sems.at[4 * which + k]) for k in range(4)
+        ]
 
     parts, at = packed_parts(plan)
-    for which, tile, start, count in parts:
-        for h, src, dst, n in both_halves(start, count, half):
-            apply(which, slice(dst, dst + n), slice(tile * LANES, (tile + 1) * LANES), packed[h, src : src + n, :].astype(F32))
+    for n, (which, tile, start, count) in enumerate(parts):
+        cs = slice(tile * LANES, (tile + 1) * LANES)
+        for h, src, dst, size in both_halves(start, count, half):
+            for c in range(0, size, UPDATE_ROWS):
+                n_rows = min(UPDATE_ROWS, size - c)
+                g = packed[h, src + c : src + c + n_rows, :].astype(F32)
+                apply(which, slice(dst + c, dst + c + n_rows), cs, g)
+        if n + 1 == len(parts) or parts[n + 1][0] != which:
+            for copy in copies(which):
+                copy.start()
     tiles = (plan.chans + 2 * plan.hidden) // LANES
     rows = packed[1, at - half : at - half + 2 * tiles, :].astype(F32)
     for tile in range(tiles):
         g = jnp.concatenate([rows[tile : tile + 1], rows[tiles + tile : tiles + tile + 1]], axis=0)
         apply(3, slice(0, 2), slice(tile * LANES, (tile + 1) * LANES), g)
+    for copy in copies(3):
+        copy.start()
+    for copy in singles:
+        copy.wait()
+    for which in range(4):
+        for copy in copies(which):
+            copy.wait()
+
+
+def update_call(plan, info, part, part_o, loss, params, means, squares):
+    kinds = (F32, F32, F32, BF16)
+    hbm = pl.BlockSpec(memory_space=pl.ANY)
+    vmem = pl.BlockSpec(memory_space=VM)
+    return pl.pallas_call(
+        partial(update_kernel, plan),
+        out_shape=[jax.ShapeDtypeStruct((1, 1), F32)] * 2 + [jax.ShapeDtypeStruct(w.shape, kind) for kind in kinds for w in params],
+        grid_spec=pltpu.PrefetchScalarGridSpec(
+            num_scalar_prefetch=1,
+            grid=(1,),
+            in_specs=[vmem] * 15,
+            out_specs=[hbm] * 18,
+            scratch_shapes=[VM((2, *part.shape), BF16), pltpu.SemaphoreType.DMA((18,))]
+            + [VM(w.shape, kind) for kind in kinds for w in params]
+            + [VM((1, 1), F32)] * 2,
+        ),
+        compiler_params=kernel_params(),
+        name="update",
+    )(info, part, part_o, loss, *params, *means, *squares)
 
 
 def small_call(kernel, name, shapes, ins, scalars=(), scratch=()):
@@ -949,15 +1067,21 @@
         out = [a, *away]
         return out + [across(v) for v in out], filled
 
-    half = fields // 2
-    pad = -(2 * degrees + half + 1) % 8
-    high = spectral_state[:, 0].astype(BF16)
-    low = (spectral_state[:, 0] - high.astype(F32)).astype(BF16)
-    seen = available[:, :, 0].reshape(tdev, 2, half, lons).astype(BF16)
-    leg = jnp.broadcast_to(legendre.reshape(1, 1, 1, chans), (tdev, 2, 1, chans))
-    pack = jnp.concatenate([high, low, seen, leg, jnp.zeros((tdev, 2, pad, chans), BF16)], axis=2)
-    keep = lax.dynamic_index_in_dim(pack, core, axis=1, keepdims=False)
-    other = across(lax.dynamic_index_in_dim(pack, 1 - core, axis=1, keepdims=False))
+    def to_each(a, fill):
+        places = [(c, n) for c in range(2) for n in range(waves)]
+        out = []
+        for other, m in [(c, n) for c in range(2) for n in range(group)][1:]:
+            if other and not m:
+                out.append(across(a))
+            else:
+                pairs = [(c * waves + n, (c ^ other) * waves + (n ^ m)) for c, n in places]
+                out.append(lax.ppermute(a, ("tm", "lat"), pairs))
+        out, filled = lax.optimization_barrier((out, fill()))
+        return [a, *out], filled
+
+    deep = -(-(2 * degrees + fields // 2 + 1) // 8) * 8
+    keep, send = pack_call(info, spectral_state, available, legendre, deep)
+    other = across(send)
     times = jnp.concatenate([jnp.where(core == 0, keep, other), jnp.where(core == 0, other, keep)], axis=0)
     spread = jnp.broadcast_to(times[None, :, None], (copies, 2 * tdev, group, *times.shape[1:]))
     got = lax.all_to_all(spread.reshape(waves, *times.shape[1:]), "lat", split_axis=0, concat_axis=0, tiled=True)
@@ -996,18 +1120,18 @@
             if s:
                 state = rest[3]
         else:
-            counts, slopes = to_members(rest[0], fill)
+            counts, slopes = to_each(rest[0], fill)
         saved.append((units, slopes, scales))
     before, bstate = None, None
+    wanted = [avail, tgt, *counts]
     for s in reversed(range(steps)):
-        dzs, *rest = backward_call(
-            plan, s, scalars, saved[s], avail, tgt, weights, nb, counts, (links, lt, ffw_t, inv), pieces, bstate
-        )
-        fill = lambda: grads_call(plan, s, chips, info, saved[s][0], dzs, nb, before, weights)
+        dzs, *rest = backward_call(plan, s, scalars, saved[s], wanted, weights, nb, (links, lt, ffw_t, inv), pieces, bstate)
+        grads = lambda: grads_call(plan, s, chips, info, saved[s][0], dzs, nb, before, weights)
         if s == 0:
-            before = fill()
+            before = grads()
         else:
-            pieces, before = to_members(rest[0], fill)
+            fill = lambda: (grads(), [masks_call(plan, s - 1, scalars, avail, tgt, counts)])
+            pieces, (before, wanted) = to_members(rest[0], fill)
             if s == steps - 1:
                 loss = rest[1]
             else:
@@ -1029,18 +1153,8 @@
         [exchange(parts)],
     )
     part = exchange(reduced).reshape(chips * blk, LANES)
-    shapes = [jax.ShapeDtypeStruct((8, LANES), F32)]
-    for kind in (F32, F32, F32, BF16):
-        shapes += [jax.ShapeDtypeStruct(w.shape, kind) for w in params]
-    norm, *results = small_call(
-        partial(update_kernel, plan),
-        "update",
-        shapes,
-        [part, across(part), *params, *means, *squares],
-        (info,),
-        [VM((2, chips * blk, LANES), BF16)],
-    )
-    return (loss[0, 0], norm[0, 0], *results)
+    loss, norm, *results = update_call(plan, info, part, across(part), loss, params, means, squares)
+    return (loss.reshape(()), norm.reshape(()), *results)
 
 
 def make_plan(mesh, args):

time: 130 us -> 128 us (0.985)
  waiting for transfers between devices: 32 us -> 24.9 us
  starting transfers between devices: 14.1 us -> 18.2 us
  Pallas kernels: 53.1 us -> 56.7 us
  local copies, waits for them, and re-layouts: 2.86 us -> 0.99 us
  other arithmetic: 5.43 us -> 3.82 us
    ppermute x7 -> x6, waiting for transfers between devices: 12.9 us -> 7.97 us  [to_members(): lax.ppermute(v, 'lat', [(n, n ^ bit) for n in range(waves)])]
    pallas_call x1 -> x2, Pallas kernels: 1.05 us -> 4.94 us  [the longest x1 3.4 us: update_call(): pl.pallas_call(partial(update_kernel, plan), out_shape=[jax.ShapeDtypeStr...]
    pallas_call x3 -> x2, Pallas kernels: 3.69 us -> 0.19 us  [small_call(): pl.pallas_call(kernel, out_shape=shapes, grid_spec=pltpu.PrefetchScalarGr...]
    pallas_call x19 -> x23, Pallas kernels: 48.4 us -> 51.6 us  [step_call(): pl.pallas_call(kernel, out_shape=shapes, grid_spec=pltpu.PrefetchScalarGr...]
    ppermute x19 -> x18, waiting for transfers between devices: 10.4 us -> 8.21 us  [grouped_device(): across = lambda a: lax.ppermute(a, 'tm', swap)]
    ppermute x7 -> x6, starting transfers between devices: 4.12 us -> 6.21 us  [to_members(): lax.ppermute(v, 'lat', [(n, n ^ bit) for n in range(waves)])]
    ppermute x0 -> x2, starting transfers between devices: none -> 2.09 us  [to_each(): out.append(lax.ppermute(a, ('tm', 'lat'), pairs))]
    convert_element_type x2 -> x0, other arithmetic: 1.62 us -> none  [the longest x1 0.85 us: grouped_device(): low = (spectral_state[:, 0] - high.astype(F32)).astype(BF16)]
  transfers between devices with their start and end apart: 27 -> 27, of which waited for: 19 -> 18; matrix products, arithmetic and copies ran while one was open for 6% -> 4% of each run, Pallas kernels for 12% -> 15%
where the time goes in v5:
time: 128 us; the launch traced here: 127 us
  Pallas kernels  56.7 us (44%)
  waiting for transfers between devices  24.9 us (19%)
  blocking collectives  21.4 us (17%)
  starting transfers between devices  18.2 us (14%)
  other arithmetic  3.82 us (3%)
  between operations  1.28 us (1%)
    pallas_call x23, Pallas kernels, step_call(): pl.pallas_call(kernel, out_shape=shapes, grid_spec=pltpu.PrefetchScalarGr...  51.6 us
    all_to_all x2, blocking collectives, grouped_device(): lax.all_to_all(a, 'lat', split_axis=0, concat_axis=0, tiled=True, axis_in...  21.4 us
    ppermute x18, waiting for transfers between devices, grouped_device(): across = lambda a: lax.ppermute(a, 'tm', swap)  8.21 us
    all_to_all x1, starting transfers between devices, grouped_device(): lax.all_to_all(spread.reshape(waves, *times.shape[1:]), 'lat', split_axis...  8.2 us
    ppermute x6, waiting for transfers between devices, to_members(): lax.ppermute(v, 'lat', [(n, n ^ bit) for n in range(waves)])  7.97 us
    all_to_all x1, waiting for transfers between devices, grouped_device(): lax.all_to_all(spread.reshape(waves, *times.shape[1:]), 'lat', split_axis...  7.93 us
    ppermute x6, starting transfers between devices, to_members(): lax.ppermute(v, 'lat', [(n, n ^ bit) for n in range(waves)])  6.21 us
    pallas_call x1, Pallas kernels, update_call(): pl.pallas_call(partial(update_kernel, plan), out_shape=[jax.ShapeDtypeStr...  3.4 us
  transfers between devices with their start and end apart: 27, of which 18 were waited for; matrix products, arithmetic and copies ran while one was open for 4% of the time, Pallas kernels for 15%

profile of v5, /device:TPU:0, one launch (start us, length us, event | category | flops | bytes accessed | tf_op | source)
XLA Modules:
  0.0 127.2 jit_solution(13078248413643490153)
XLA Ops:
  0.8 1.5 %pack.1 = (bf16[2,40,256]{2,1,0:T(8,128)(2,1)S(1)}, bf16[2,40,256]{2,1,0:T(8,128)(2,1)S(1)}) custom-call(s32[2]{0:T(128)S(1)} %pad_add_fusion.info, f32[2,1,2,16,256]{4,3,2,1,0:T(8,128)} %state_in.1, s32[2,8,1,256]{3,2,1,0:T(1,128)} %seen_in.1, bf16[1,16,16]{2,1,0:T(8,128)(2,1)} %legendre_in.1), custom_call_target="tpu_custom_call" | custom-call | tf_op jit(solution)/shard_map/pack/pallas_call | solution.py:353
  4.6 8.2 %all-to-all-start = ((bf16[16,40,256]{2,1,0:T(8,128)(2,1)}), bf16[16,40,256]{2,1,0:T(8,128)(2,1)S(1)}, u32[]{:S(2)}, u32[]{:S(2)}) async-start(bf16[16,40,256]{2,1,0:T(8,128)(2,1)} %bitcast.2), calls=%async_computation | async-start | bytes 655360 | tf_op jit(solution)/shard_map/all_to_all | solution.py:1087
  16.5 7.9 %all-to-all-done.got = bf16[16,40,256]{2,1,0:T(8,128)(2,1)S(1)} async-done(((bf16[16,40,256]{2,1,0:T(8,128)(2,1)}), bf16[16,40,256]{2,1,0:T(8,128)(2,1)S(1)}, u32[]{:S(2)}, u32[]{:S(2)}) %all-to-all-start) | async-done | bytes 327712 | tf_op jit(solution)/shard_map/all_to_all | solution.py:1087
  24.5 1.5 %collective-permute-done.1.got_o = bf16[16,40,256]{2,1,0:T(8,128)(2,1)S(1)} collective-permute-done((bf16[16,40,256]{2,1,0:T(8,128)(2,1)S(1)}, bf16[16,40,256]{2,1,0:T(8,128)(2,1)S(1)}, u32[]{:S(2)}, u32[]{:S(2)}) %collective-permute-start.1) | collective-permute-done | bytes 327712 | tf_op jit(solution)/shard_map/ppermute | solution.py:1058
  27.2 3.6 %forward_0.1 = (f32[1024,1024]{1,0:T(8,128)S(1)}, f32[1024,768]{1,0:T(8,128)S(1)}, f32[1024,384]{1,0:T(8,128)S(1)}, bf16[2,64,256]{2,1,0:T(8,128)(2,1)S(1)}, f32...) custom-call(s32[2]{0:T(128)S(1)} %pad_add_fusion.info, s32[16]{0:T(128)S(1)} %copy-done.10, f32[16]{0:T(128)S(1)} %copy-done.11, ...), custom_call_target="tpu_custom_call" | custom-call | flops 704643072 | bytes 8388608 | tf_op jit(solution)/shard_map/forward_0/pallas_call | solution.py:555
  31.4 1.5 %slopes_0.1.refs_1_ = f32[1024,768]{1,0:T(8,128)S(1)} custom-call(f32[1024,768]{1,0:T(8,128)S(1)} %get-tuple-element.145.inners, f32[1024,384]{1,0:T(8,128)S(1)} %get-tuple-element.146.scales.refs_2_), custom_call_target="tpu_custom_call", output_to_operand_aliasing={{}: (0, {})} | custom-call | flops 6291456 | bytes 8388608 | tf_op jit(solution)/shard_map/slopes_0/pallas_call | solution.py:555
  32.9 2.2 %collective-permute-done.3.refs_10_ = bf16[2,64,256]{2,1,0:T(8,128)(2,1)S(1)} collective-permute-done((bf16[2,64,256]{2,1,0:T(8,128)(2,1)S(1)}, bf16[2,64,256]{2,1,0:T(8,128)(2,1)S(1)}, u32[]{:S(2)}, u32[]{:S(2)}) %collective-permute-start.3) | collective-permute-done | bytes 65568 | tf_op jit(solution)/shard_map/ppermute | solution.py:1064
  36.4 4.0 %forward_1.1 = (f32[1024,1024]{1,0:T(8,128)S(1)}, f32[1024,768]{1,0:T(8,128)S(1)}, f32[1024,384]{1,0:T(8,128)S(1)}, bf16[2,64,256]{2,1,0:T(8,128)(2,1)S(1)}, f32...) custom-call(s32[2]{0:T(128)S(1)} %pad_add_fusion.info, s32[16]{0:T(128)S(1)} %copy-done.10, ...), custom_call_target="tpu_custom_call" | custom-call | flops 704643072 | bytes 8388608 | tf_op jit(solution)/shard_map/forward_1/pallas_call | solution.py:555
  41.1 1.5 %slopes_1.1.refs_1_ = f32[1024,768]{1,0:T(8,128)S(1)} custom-call(f32[1024,768]{1,0:T(8,128)S(1)} %get-tuple-element.160.inners, f32[1024,384]{1,0:T(8,128)S(1)} %get-tuple-element.161.scales.refs_2_), custom_call_target="tpu_custom_call", output_to_operand_aliasing={{}: (0, {})} | custom-call | flops 6291456 | bytes 8388608 | tf_op jit(solution)/shard_map/slopes_1/pallas_call | solution.py:555
  42.6 2.2 %collective-permute-done.6.refs_10_ = bf16[2,64,256]{2,1,0:T(8,128)(2,1)S(1)} collective-permute-done((bf16[2,64,256]{2,1,0:T(8,128)(2,1)S(1)}, bf16[2,64,256]{2,1,0:T(8,128)(2,1)S(1)}, u32[]{:S(2)}, u32[]{:S(2)}) %collective-permute-start.6) | collective-permute-done | bytes 65568 | tf_op jit(solution)/shard_map/ppermute | solution.py:1064
  46.1 4.0 %forward_2.1 = (f32[1024,1024]{1,0:T(8,128)S(1)}, f32[1024,768]{1,0:T(8,128)S(1)}, f32[1024,384]{1,0:T(8,128)S(1)}, bf16[2,64,256]{2,1,0:T(8,128)(2,1)S(1)}, f32...) custom-call(s32[2]{0:T(128)S(1)} %pad_add_fusion.info, s32[16]{0:T(128)S(1)} %copy-done.10, ...), custom_call_target="tpu_custom_call" | custom-call | flops 704643072 | bytes 8388608 | tf_op jit(solution)/shard_map/forward_2/pallas_call | solution.py:555
  50.8 1.7 %slopes_2.1.refs_1_ = f32[1024,768]{1,0:T(8,128)S(1)} custom-call(f32[1024,768]{1,0:T(8,128)S(1)} %get-tuple-element.174.inners, f32[1024,384]{1,0:T(8,128)S(1)} %get-tuple-element.175.scales.refs_2_), custom_call_target="tpu_custom_call", output_to_operand_aliasing={{}: (0, {})} | custom-call | flops 6291456 | bytes 8388608 | tf_op jit(solution)/shard_map/slopes_2/pallas_call | solution.py:555
  52.5 2.0 %collective-permute-done.9.refs_12_ = bf16[2,64,256]{2,1,0:T(8,128)(2,1)S(1)} collective-permute-done((bf16[2,64,256]{2,1,0:T(8,128)(2,1)S(1)}, bf16[2,64,256]{2,1,0:T(8,128)(2,1)S(1)}, u32[]{:S(2)}, u32[]{:S(2)}) %collective-permute-start.9) | collective-permute-done | bytes 65568 | tf_op jit(solution)/shard_map/ppermute | solution.py:1064
  55.7 4.4 %forward_3.1 = (f32[1024,1024]{1,0:T(8,128)S(1)}, f32[1024,768]{1,0:T(8,128)S(1)}, f32[1024,384]{1,0:T(8,128)S(1)}, f32[40,128]{1,0:T(8,128)S(1)}) custom-call(s32[2]{0:T(128)S(1)} %pad_add_fusion.info, s32[16]{0:T(128)S(1)} %copy-done.10, f32[16]{0:T(128)S(1)} %copy-done.11, f32[2,256,256]{2,1,0:T(8,128)S(1)} %get-tuple-element.177.refs_0_, ...), custom_call_target="tpu_custom_call" | custom-call | flops 704643072 | bytes 8388608 | tf_op jit(solution)/shard_map/forward_3/pallas_call | solution.py:555
  60.8 1.5 %collective-permute-start.12 = (f32[40,128]{1,0:T(8,128)S(1)}, f32[40,128]{1,0:T(8,128)S(1)}, u32[]{:S(2)}, u32[]{:S(2)}) collective-permute-start(f32[40,128]{1,0:T(8,128)S(1)} %get-tuple-element.188.refs_8_.refs_0_), channel_id=1, source_target_pairs={{0,1},{1,0},{2,3},{3,2},{4,5},{5,4},{6,7},{7,6},{8,9},{9,8},{10,11... | collective-permute-start | bytes 61448 | tf_op jit(solution)/shard_map/ppermute | solution.py:1078
  62.3 1.5 %slopes_3.1.refs_1_ = f32[1024,768]{1,0:T(8,128)S(1)} custom-call(f32[1024,768]{1,0:T(8,128)S(1)} %get-tuple-element.189.inners, f32[1024,384]{1,0:T(8,128)S(1)} %get-tuple-element.190.scales.refs_2_), custom_call_target="tpu_custom_call", output_to_operand_aliasing={{}: (0, {})} | custom-call | flops 6291456 | bytes 8388608 | tf_op jit(solution)/shard_map/slopes_3/pallas_call | solution.py:555
  64.6 3.3 %backward_3.1 = (bf16[1024,1024]{1,0:T(8,128)(2,1)S(1)}, bf16[2,64,256]{2,1,0:T(8,128)(2,1)S(1)}, f32[8,128]{1,0:T(8,128)S(1)}) custom-call(s32[2]{0:T(128)S(1)} %pad_add_fusion.info, s32[16]{0:T(128)S(1)} %copy-done.10, f32[16]{0:T(128)S(1)} %copy-done.11, f32[1024,1024]{1,0:T(8,128)S(1)} %get-tuple-element.187.refs_0_, f32[1024,768]{1,0:T(8,128)S(1)} %slopes_3.1.refs_1_, ...), custom_call_target="tpu_custom_call" | custom-call | flops 704643072 | bytes 8388608 | tf_op jit(solution)/shard_map/backward_3/pallas_call | solution.py:555
  67.9 1.5 %collective-permute-start.15 = (bf16[2,64,256]{2,1,0:T(8,128)(2,1)S(1)}, bf16[2,64,256]{2,1,0:T(8,128)(2,1)S(1)}, u32[]{:S(2)}, u32[]{:S(2)}) collective-permute-start(bf16[2,64,256]{2,1,0:T(8,128)(2,1)S(1)} %get-tuple-element.196.refs_10_), channel_id=1, source_target_pairs={{0,1},{1,0},{2,3},{3,2},{4,5},{5,4},{6,7},{7,6},{8,9},{9,8},{10,11... | collective-permute-start | bytes 196616 | tf_op jit(solution)/shard_map/ppermute | solution.py:1064
  70.3 1.9 %grads_3.1 = (f32[256,384]{1,0:T(8,128)S(1)}, f32[384,384]{1,0:T(8,128)S(1)}, f32[384,256]{1,0:T(8,128)S(1)}, f32[8,1024]{1,0:T(8,128)S(1)}) custom-call(s32[2]{0:T(128)S(1)} %pad_add_fusion.info, f32[1024,1024]{1,0:T(8,128)S(1)} %get-tuple-element.187.refs_0_, bf16[1024,1024]{1,0:T(8,128)(2,1)S(1)} %get-tuple-element.197.refs_1_, f32[2,1024]{1,0:T(2,128)S(1)} %copy-done.3), custom_call_target="tpu_custom_call" | custom-call | flops 704643072 | bytes 8388608 | tf_op jit(solution)/shard_map/grads_3/pallas_call | solution.py:555
  73.7 3.7 %backward_2.1 = (bf16[1024,1024]{1,0:T(8,128)(2,1)S(1)}, bf16[2,64,256]{2,1,0:T(8,128)(2,1)S(1)}, f32[2,256,256]{2,1,0:T(8,128)S(1)}) custom-call(s32[2]{0:T(128)S(1)} %pad_add_fusion.info, s32[16]{0:T(128)S(1)} %copy-done.10, f32[16]{0:T(128)S(1)} %copy-done.11, f32[1024,1024]{1,0:T(8,128)S(1)} %get-tuple-element.172.refs_0_, ...), custom_call_target="tpu_custom_call" | custom-call | flops 704643072 | bytes 8388608 | tf_op jit(solution)/shard_map/backward_2/pallas_call | solution.py:555
  77.5 1.5 %collective-permute-start.18 = (bf16[2,64,256]{2,1,0:T(8,128)(2,1)S(1)}, bf16[2,64,256]{2,1,0:T(8,128)(2,1)S(1)}, u32[]{:S(2)}, u32[]{:S(2)}) collective-permute-start(bf16[2,64,256]{2,1,0:T(8,128)(2,1)S(1)} %get-tuple-element.205.refs_10_), channel_id=1, source_target_pairs={{0,1},{1,0},{2,3},{3,2},{4,5},{5,4},{6,7},{7,6},{8,9},{9,8},{10,11... | collective-permute-start | bytes 196616 | tf_op jit(solution)/shard_map/ppermute | solution.py:1064
  79.0 2.0 %grads_2.1 = (f32[256,384]{1,0:T(8,128)S(1)}, f32[384,384]{1,0:T(8,128)S(1)}, f32[384,256]{1,0:T(8,128)S(1)}, f32[8,1024]{1,0:T(8,128)S(1)}) custom-call(s32[2]{0:T(128)S(1)} %pad_add_fusion.info, f32[1024,1024]{1,0:T(8,128)S(1)} %get-tuple-element.172.refs_0_, ...), custom_call_target="tpu_custom_call", output_to_operand_aliasing={{0}: (4, {}), {1}: (5, {}), {2}: (6, {}), {3}: (7, {})} | custom-call | flops 704643072 | bytes 8388608 | tf_op jit(solution)/shard_map/grads_2/pallas_call | solution.py:555
  83.1 3.7 %backward_1.1 = (bf16[1024,1024]{1,0:T(8,128)(2,1)S(1)}, bf16[2,64,256]{2,1,0:T(8,128)(2,1)S(1)}, f32[2,256,256]{2,1,0:T(8,128)S(1)}) custom-call(s32[2]{0:T(128)S(1)} %pad_add_fusion.info, s32[16]{0:T(128)S(1)} %copy-done.10, f32[16]{0:T(128)S(1)} %copy-done.11, f32[1024,1024]{1,0:T(8,128)S(1)} %get-tuple-element.158.refs_0_, ...), custom_call_target="tpu_custom_call" | custom-call | flops 704643072 | bytes 8388608 | tf_op jit(solution)/shard_map/backward_1/pallas_call | solution.py:555
  87.0 1.5 %collective-permute-start.21 = (bf16[2,64,256]{2,1,0:T(8,128)(2,1)S(1)}, bf16[2,64,256]{2,1,0:T(8,128)(2,1)S(1)}, u32[]{:S(2)}, u32[]{:S(2)}) collective-permute-start(bf16[2,64,256]{2,1,0:T(8,128)(2,1)S(1)} %get-tuple-element.218.refs_10_), channel_id=1, source_target_pairs={{0,1},{1,0},{2,3},{3,2},{4,5},{5,4},{6,7},{7,6},{8,9},{9,8},{10,11... | collective-permute-start | bytes 196616 | tf_op jit(solution)/shard_map/ppermute | solution.py:1064
  88.4 2.3 %grads_1.1 = (f32[256,384]{1,0:T(8,128)S(1)}, f32[384,384]{1,0:T(8,128)S(1)}, f32[384,256]{1,0:T(8,128)S(1)}, f32[8,1024]{1,0:T(8,128)S(1)}) custom-call(s32[2]{0:T(128)S(1)} %pad_add_fusion.info, f32[1024,1024]{1,0:T(8,128)S(1)} %get-tuple-element.158.refs_0_, ...), custom_call_target="tpu_custom_call", output_to_operand_aliasing={{0}: (4, {}), {1}: (5, {}), {2}: (6, {}), {3}: (7, {})} | custom-call | flops 704643072 | bytes 8388608 | tf_op jit(solution)/shard_map/grads_1/pallas_call | solution.py:555
  92.6 2.9 %backward_0.1.refs_1_ = bf16[1024,1024]{1,0:T(8,128)(2,1)S(1)} custom-call(s32[2]{0:T(128)S(1)} %pad_add_fusion.info, s32[16]{0:T(128)S(1)} %copy-done.10, f32[16]{0:T(128)S(1)} %copy-done.11, f32[1024,1024]{1,0:T(8,128)S(1)} %get-tuple-element.143.refs_0_, f32[1024,768]{1,0:T(8,128)S(1)} %slopes_0.1.refs_1_, ...), custom_call_target="tpu_custom_call" | custom-call | flops 704643072 | bytes 8388608 | tf_op jit(solution)/shard_map/backward_0/pallas_call | solution.py:555
  95.4 2.4 %grads_0.1 = (f32[1408,128]{1,0:T(8,128)S(1)}, f32[1408,128]{1,0:T(8,128)S(1)}) custom-call(s32[2]{0:T(128)S(1)} %pad_add_fusion.info, f32[1024,1024]{1,0:T(8,128)S(1)} %get-tuple-element.143.refs_0_, bf16[1024,1024]{1,0:T(8,128)(2,1)S(1)} %backward_0.1.refs_1_, f32[2,1024]{1,0:T(2,128)S(1)} %copy-done.3, f32[256,384]{1,0:T(8,128)S(1)} %get-tuple-element.231.refs_3_, ...), custom_call_target="tpu_custom_call" | custom-call | flops 704643072 | bytes 8388608 | tf_op jit(solution)/shard_map/grads_0/pallas_call | solution.py:555
  98.2 2.0 %collective-permute-done.24.got = f32[1408,128]{1,0:T(8,128)S(1)} collective-permute-done((f32[1408,128]{1,0:T(8,128)S(1)}, f32[1408,128]{1,0:T(8,128)S(1)}, u32[]{:S(2)}, u32[]{:S(2)}) %collective-permute-start.24) | collective-permute-done | bytes 720928 | tf_op jit(solution)/shard_map/ppermute | solution.py:1058
  100.4 11.7 %all_to_all.15.got = bf16[8,192,128]{2,1,0:T(8,128)(2,1)S(1)} all-to-all(bf16[8,192,128]{2,1,0:T(8,128)(2,1)S(1)} %pairs.1), channel_id=1, replica_groups={{0,1,2,3,4,5,6,7},{8,9,10,11,12,13,14,15},{16,17,18,19,20,21,22,23},{24..., dimensions={0} | all-to-all | bytes 786432 | tf_op jit(solution)/shard_map/all_to_all | solution.py:1142
  112.1 9.8 %all_to_all.16 = bf16[8,176,128]{2,1,0:T(8,128)(2,1)S(1)} all-to-all(bf16[8,176,128]{2,1,0:T(8,128)(2,1)S(1)} %get-tuple-element.238), channel_id=1, replica_groups={{0,1,2,3,4,5,6,7},{8,9,10,11,12,13,14,15},{16,17,18,19,20,21,22,23},{24..., dimensions={0} | all-to-all | bytes 720896 | tf_op jit(solution)/shard_map/all_to_all | solution.py:1142
  121.9 1.7 %collective-permute-done.25.part_o = bf16[1408,128]{1,0:T(8,128)(2,1)S(1)} collective-permute-done((bf16[1408,128]{1,0:T(8,128)(2,1)S(1)}, bf16[1408,128]{1,0:T(8,128)(2,1)S(1)}, u32[]{:S(2)}, u32[]{:S(2)}) %collective-permute-start.25) | collective-permute-done | bytes 360480 | tf_op jit(solution)/shard_map/ppermute | solution.py:1058
  123.6 3.4 %update.1 = (f32[1,1]{1,0:T(1,128)}, f32[1,1]{1,0:T(1,128)}, f32[256,384]{1,0:T(8,128)}, f32[384,384]{1,0:T(8,128)}, f32[384,256]{1,0:T(8,128)}, /*index=5*/f32[...) custom-call(s32[2]{0:T(128)S(1)} %pad_add_fusion.info, ...), custom_call_target="tpu_custom_call" | custom-call | tf_op jit(solution)/shard_map/update/pallas_call | solution.py:1002
  (99 shorter events, 21.6 us)
Async XLA Ops:
  0.7 26.5 %copy-start.3 = (f32[2,1024]{1,0:T(2,128)S(1)}, f32[2,1024]{1,0:T(2,128)}, u32[]{:S(2)}) copy-start(f32[2,1024]{1,0:T(2,128)} %refs_3_.1) | copy-start | bytes 24580
  2.4 1.4 %collective-permute-start = (bf16[2,40,256]{2,1,0:T(8,128)(2,1)S(1)}, bf16[2,40,256]{2,1,0:T(8,128)(2,1)S(1)}, u32[]{:S(2)}, u32[]{:S(2)}) collective-permute-start(bf16[2,40,256]{2,1,0:T(8,128)(2,1)S(1)} %get-tuple-element.139), channel_id=1, source_target_pairs={{0,16},{16,0},{1,17},{17,1},{2,18},{18,2},{3,19},{19,3},{4,20},{20... | collective-permute-start | bytes 122888 | tf_op jit(solution)/shard_map/ppermute | solution.py:1058
  2.9 21.5 %collective-permute-start.2 = (f32[2,4,8]{2,1,0:T(4,128)}, f32[2,4,8]{2,1,0:T(4,128)S(1)}, u32[]{:S(2)}, u32[]{:S(2)}) collective-permute-start(f32[2,4,8]{2,1,0:T(4,128)} %param.25), channel_id=1, source_target_pairs={{0,16},{16,0},{1,17},{17,1},{2,18},{18,2},{3,19},{19,3},{4,20},{20... | collective-permute-start | bytes 776 | tf_op jit(solution)/shard_map/ppermute | solution.py:1058
  4.6 19.8 %all-to-all-start = ((bf16[16,40,256]{2,1,0:T(8,128)(2,1)}), bf16[16,40,256]{2,1,0:T(8,128)(2,1)S(1)}, u32[]{:S(2)}, u32[]{:S(2)}) async-start(bf16[16,40,256]{2,1,0:T(8,128)(2,1)} %bitcast.2), calls=%async_computation | async-start | bytes 655360 | tf_op jit(solution)/shard_map/all_to_all | solution.py:1087
  24.4 1.6 %collective-permute-start.1 = (bf16[16,40,256]{2,1,0:T(8,128)(2,1)S(1)}, bf16[16,40,256]{2,1,0:T(8,128)(2,1)S(1)}, u32[]{:S(2)}, u32[]{:S(2)}) collective-permute-start(bf16[16,40,256]{2,1,0:T(8,128)(2,1)S(1)} %all-to-all-done.got), channel_id=1, source_target_pairs={{0,16},{16,0},{1,17},{17,1},{2,18},{18,2},{3,19},{19,3},{4,20},{20... | collective-permute-start | bytes 983048 | tf_op jit(solution)/shard_map/ppermute | solution.py:1058
  30.8 4.3 %collective-permute-start.3 = (bf16[2,64,256]{2,1,0:T(8,128)(2,1)S(1)}, bf16[2,64,256]{2,1,0:T(8,128)(2,1)S(1)}, u32[]{:S(2)}, u32[]{:S(2)}) collective-permute-start(bf16[2,64,256]{2,1,0:T(8,128)(2,1)S(1)} %get-tuple-element.154.refs_9_), channel_id=1, source_target_pairs={{0,1},{1,0},{2,3},{3,2},{4,5},{5,4},{6,7},{7,6},{8,9},{9,8},{10,11... | collective-permute-start | bytes 196616 | tf_op jit(solution)/shard_map/ppermute | solution.py:1064
  31.4 4.9 %collective-permute-start.4 = (bf16[2,64,256]{2,1,0:T(8,128)(2,1)S(1)}, bf16[2,64,256]{2,1,0:T(8,128)(2,1)S(1)}, u32[]{:S(2)}, u32[]{:S(2)}) collective-permute-start(bf16[2,64,256]{2,1,0:T(8,128)(2,1)S(1)} %get-tuple-element.154.refs_9_), channel_id=1, source_target_pairs={{0,16},{16,0},{1,17},{17,1},{2,18},{18,2},{3,19},{19,3},{4,20},{20... | collective-permute-start | bytes 196616 | tf_op jit(solution)/shard_map/ppermute | solution.py:1058
  35.1 1.3 collective-permute-start.5
  40.3 4.5 %collective-permute-start.6 = (bf16[2,64,256]{2,1,0:T(8,128)(2,1)S(1)}, bf16[2,64,256]{2,1,0:T(8,128)(2,1)S(1)}, u32[]{:S(2)}, u32[]{:S(2)}) collective-permute-start(bf16[2,64,256]{2,1,0:T(8,128)(2,1)S(1)} %get-tuple-element.168.refs_9_), channel_id=1, source_target_pairs={{0,1},{1,0},{2,3},{3,2},{4,5},{5,4},{6,7},{7,6},{8,9},{9,8},{10,11... | collective-permute-start | bytes 196616 | tf_op jit(solution)/shard_map/ppermute | solution.py:1064
  40.9 5.0 %collective-permute-start.7 = (bf16[2,64,256]{2,1,0:T(8,128)(2,1)S(1)}, bf16[2,64,256]{2,1,0:T(8,128)(2,1)S(1)}, u32[]{:S(2)}, u32[]{:S(2)}) collective-permute-start(bf16[2,64,256]{2,1,0:T(8,128)(2,1)S(1)} %get-tuple-element.168.refs_9_), channel_id=1, source_target_pairs={{0,16},{16,0},{1,17},{17,1},{2,18},{18,2},{3,19},{19,3},{4,20},{20... | collective-permute-start | bytes 196616 | tf_op jit(solution)/shard_map/ppermute | solution.py:1058
  44.8 1.3 collective-permute-start.8
  50.0 4.5 %collective-permute-start.9 = (bf16[2,64,256]{2,1,0:T(8,128)(2,1)S(1)}, bf16[2,64,256]{2,1,0:T(8,128)(2,1)S(1)}, u32[]{:S(2)}, u32[]{:S(2)}) collective-permute-start(bf16[2,64,256]{2,1,0:T(8,128)(2,1)S(1)} %get-tuple-element.183.refs_11_), channel_id=1, source_target_pairs={{0,1},{1,0},{2,3},{3,2},{4,5},{5,4},{6,7},{7,6},{8,9},{9,8},{10,11... | collective-permute-start | bytes 196616 | tf_op jit(solution)/shard_map/ppermute | solution.py:1064
  50.6 5.0 %collective-permute-start.10 = (bf16[2,64,256]{2,1,0:T(8,128)(2,1)S(1)}, bf16[2,64,256]{2,1,0:T(8,128)(2,1)S(1)}, u32[]{:S(2)}, u32[]{:S(2)}) collective-permute-start(bf16[2,64,256]{2,1,0:T(8,128)(2,1)S(1)} %get-tuple-element.183.refs_11_), channel_id=1, source_target_pairs={{0,16},{16,0},{1,17},{17,1},{2,18},{18,2},{3,19},{19,3},{4,20},{20... | collective-permute-start | bytes 196616 | tf_op jit(solution)/shard_map/ppermute | solution.py:1058
  54.5 1.3 collective-permute-start.11
  60.1 3.7 %collective-permute-start.14 = (f32[40,128]{1,0:T(8,128)S(1)}, f32[40,128]{1,0:T(8,128)S(1)}, u32[]{:S(2)}, u32[]{:S(2)}) collective-permute-start(f32[40,128]{1,0:T(8,128)S(1)} %get-tuple-element.188.refs_8_.refs_0_), channel_id=1, source_target_pairs={{0,17},{1,16},{2,19},{3,18},{4,21},{5,20},{6,23},{7,22},{8,25},{9,... | collective-permute-start | bytes 61448 | tf_op jit(solution)/shard_map/ppermute | solution.py:1078
  60.8 3.1 %collective-permute-start.13 = (f32[40,128]{1,0:T(8,128)S(1)}, f32[40,128]{1,0:T(8,128)S(1)}, u32[]{:S(2)}, u32[]{:S(2)}) collective-permute-start(f32[40,128]{1,0:T(8,128)S(1)} %get-tuple-element.188.refs_8_.refs_0_), channel_id=1, source_target_pairs={{0,16},{16,0},{1,17},{17,1},{2,18},{18,2},{3,19},{19,3},{4,20},{20... | collective-permute-start | bytes 61448 | tf_op jit(solution)/shard_map/ppermute | solution.py:1058
  60.8 3.8 %collective-permute-start.12 = (f32[40,128]{1,0:T(8,128)S(1)}, f32[40,128]{1,0:T(8,128)S(1)}, u32[]{:S(2)}, u32[]{:S(2)}) collective-permute-start(f32[40,128]{1,0:T(8,128)S(1)} %get-tuple-element.188.refs_8_.refs_0_), channel_id=1, source_target_pairs={{0,1},{1,0},{2,3},{3,2},{4,5},{5,4},{6,7},{7,6},{8,9},{9,8},{10,11... | collective-permute-start | bytes 61448 | tf_op jit(solution)/shard_map/ppermute | solution.py:1078
  67.9 5.4 %collective-permute-start.16 = (bf16[2,64,256]{2,1,0:T(8,128)(2,1)S(1)}, bf16[2,64,256]{2,1,0:T(8,128)(2,1)S(1)}, u32[]{:S(2)}, u32[]{:S(2)}) collective-permute-start(bf16[2,64,256]{2,1,0:T(8,128)(2,1)S(1)} %get-tuple-element.196.refs_10_), channel_id=1, source_target_pairs={{0,16},{16,0},{1,17},{17,1},{2,18},{18,2},{3,19},{19,3},{4,20},{20... | collective-permute-start | bytes 196616 | tf_op jit(solution)/shard_map/ppermute | solution.py:1058
  67.9 4.5 %collective-permute-start.15 = (bf16[2,64,256]{2,1,0:T(8,128)(2,1)S(1)}, bf16[2,64,256]{2,1,0:T(8,128)(2,1)S(1)}, u32[]{:S(2)}, u32[]{:S(2)}) collective-permute-start(bf16[2,64,256]{2,1,0:T(8,128)(2,1)S(1)} %get-tuple-element.196.refs_10_), channel_id=1, source_target_pairs={{0,1},{1,0},{2,3},{3,2},{4,5},{5,4},{6,7},{7,6},{8,9},{9,8},{10,11... | collective-permute-start | bytes 196616 | tf_op jit(solution)/shard_map/ppermute | solution.py:1064
  72.4 1.3 collective-permute-start.17
  77.3 5.4 %collective-permute-start.19 = (bf16[2,64,256]{2,1,0:T(8,128)(2,1)S(1)}, bf16[2,64,256]{2,1,0:T(8,128)(2,1)S(1)}, u32[]{:S(2)}, u32[]{:S(2)}) collective-permute-start(bf16[2,64,256]{2,1,0:T(8,128)(2,1)S(1)} %get-tuple-element.205.refs_10_), channel_id=1, source_target_pairs={{0,16},{16,0},{1,17},{17,1},{2,18},{18,2},{3,19},{19,3},{4,20},{20... | collective-permute-start | bytes 196616 | tf_op jit(solution)/shard_map/ppermute | solution.py:1058
  77.5 4.3 %collective-permute-start.18 = (bf16[2,64,256]{2,1,0:T(8,128)(2,1)S(1)}, bf16[2,64,256]{2,1,0:T(8,128)(2,1)S(1)}, u32[]{:S(2)}, u32[]{:S(2)}) collective-permute-start(bf16[2,64,256]{2,1,0:T(8,128)(2,1)S(1)} %get-tuple-element.205.refs_10_), channel_id=1, source_target_pairs={{0,1},{1,0},{2,3},{3,2},{4,5},{5,4},{6,7},{7,6},{8,9},{9,8},{10,11... | collective-permute-start | bytes 196616 | tf_op jit(solution)/shard_map/ppermute | solution.py:1064
  81.9 1.3 collective-permute-start.20
  86.8 4.5 %collective-permute-start.22 = (bf16[2,64,256]{2,1,0:T(8,128)(2,1)S(1)}, bf16[2,64,256]{2,1,0:T(8,128)(2,1)S(1)}, u32[]{:S(2)}, u32[]{:S(2)}) collective-permute-start(bf16[2,64,256]{2,1,0:T(8,128)(2,1)S(1)} %get-tuple-element.218.refs_10_), channel_id=1, source_target_pairs={{0,16},{16,0},{1,17},{17,1},{2,18},{18,2},{3,19},{19,3},{4,20},{20... | collective-permute-start | bytes 196616 | tf_op jit(solution)/shard_map/ppermute | solution.py:1058
  87.0 4.3 %collective-permute-start.21 = (bf16[2,64,256]{2,1,0:T(8,128)(2,1)S(1)}, bf16[2,64,256]{2,1,0:T(8,128)(2,1)S(1)}, u32[]{:S(2)}, u32[]{:S(2)}) collective-permute-start(bf16[2,64,256]{2,1,0:T(8,128)(2,1)S(1)} %get-tuple-element.218.refs_10_), channel_id=1, source_target_pairs={{0,1},{1,0},{2,3},{3,2},{4,5},{5,4},{6,7},{7,6},{8,9},{9,8},{10,11... | collective-permute-start | bytes 196616 | tf_op jit(solution)/shard_map/ppermute | solution.py:1064
  91.3 1.3 collective-permute-start.23
  97.9 25.7 %copy-start.1 = (f32[256,384]{1,0:T(8,128)S(1)}, f32[256,384]{1,0:T(8,128)}, u32[]{:S(2)}) copy-start(f32[256,384]{1,0:T(8,128)} %refs_0_.1) | copy-start | bytes 1179652
  97.9 25.7 %copy-start.2 = (f32[384,256]{1,0:T(8,128)S(1)}, f32[384,256]{1,0:T(8,128)}, u32[]{:S(2)}) copy-start(f32[384,256]{1,0:T(8,128)} %refs_2_.9) | copy-start | bytes 1179652
  97.9 25.7 %copy-start.4 = (f32[384,384]{1,0:T(8,128)S(1)}, f32[384,384]{1,0:T(8,128)}, u32[]{:S(2)}) copy-start(f32[384,384]{1,0:T(8,128)} %refs_5_.9) | copy-start | bytes 1769476
  97.9 25.7 %copy-start.5 = (f32[384,384]{1,0:T(8,128)S(1)}, f32[384,384]{1,0:T(8,128)}, u32[]{:S(2)}) copy-start(f32[384,384]{1,0:T(8,128)} %refs_9_.1) | copy-start | bytes 1769476
  98.0 2.3 %collective-permute-start.24 = (f32[1408,128]{1,0:T(8,128)S(1)}, f32[1408,128]{1,0:T(8,128)S(1)}, u32[]{:S(2)}, u32[]{:S(2)}) collective-permute-start(f32[1408,128]{1,0:T(8,128)S(1)} %get-tuple-element.236), channel_id=1, source_target_pairs={{0,16},{16,0},{1,17},{17,1},{2,18},{18,2},{3,19},{19,3},{4,20},{20... | collective-permute-start | bytes 2162696 | tf_op jit(solution)/shard_map/ppermute | solution.py:1058
  121.9 1.7 %collective-permute-start.25 = (bf16[1408,128]{1,0:T(8,128)(2,1)S(1)}, bf16[1408,128]{1,0:T(8,128)(2,1)S(1)}, u32[]{:S(2)}, u32[]{:S(2)}) collective-permute-start(bf16[1408,128]{1,0:T(8,128)(2,1)S(1)} %bitcast.10), channel_id=1, source_target_pairs={{0,16},{16,0},{1,17},{17,1},{2,18},{18,2},{3,19},{19,3},{4,20},{20... | collective-permute-start | bytes 1081352 | tf_op jit(solution)/shard_map/ppermute | solution.py:1058
  (11 other events, 269.7 us)

commit v6 on v5

--- a/solution.py
+++ b/solution.py
@@ -365,10 +365,15 @@
     )(info, *ins)
 
 
-def prepare_kernel(
-    plan, info, slots, order, quad, got, got_o, inv, ffw, wanted, state, links, lt, avail, nums, table, ffw_t, tgt
-):
-    group, rows, waves, degrees, steps, fields, chans, _, _ = plan
+def unpack_state(plan, ref, p, state):
+    waves, degrees = plan.waves, plan.degrees
+    for j in range(waves):
+        high = ref[j, 0:degrees, :].astype(F32)
+        state[p, pl.ds(j * degrees, degrees), :] = high + ref[j, degrees : 2 * degrees, :].astype(F32)
+
+
+def links_kernel(plan, info, slots, order, got, inv, ffw, wanted, state, links, lt, table, ffw_t, tgt):
+    group, rows, waves, degrees, _, fields, chans, _, _ = plan
     members = 2 * group
     core, member = info[0], info[1]
     span = waves * degrees
@@ -378,11 +383,8 @@
     leg = jnp.zeros((waves, chans), F32)
     row_of = lax.broadcasted_iota(jnp.int32, (waves, chans), 0)
     pick = lax.broadcasted_iota(jnp.int32, (8, chans), 0) == half
+    unpack_state(plan, got, core, state)
     for j in range(waves):
-        at = pl.ds(j * degrees, degrees)
-        for ref, p in ((got, core), (got_o, 1 - core)):
-            hi = ref[j, 0:degrees, :].astype(F32)
-            state[p, at, :] = hi + ref[j, degrees : 2 * degrees, :].astype(F32)
         tail = got[j, 2 * degrees : 2 * degrees + 8, :].astype(F32)
         line = jnp.sum(jnp.where(pick, tail, 0.0), axis=0, keepdims=True)
         leg = jnp.where(row_of == j, line, leg)
@@ -406,6 +408,16 @@
     plg = jnp.where((r0 // degrees == r1 % waves) & (r0 % degrees >= wave_row), plg, 0.0)
     links[...] = plg.astype(BF16)
     lt[...] = plg[:, 0:mine].T.astype(BF16)
+    table[...] = inv[...].T.astype(BF16)
+    ffw_t[...] = ffw[...].T.astype(BF16)
+    tgt[...] = wanted[...]
+
+
+def fields_kernel(plan, info, order, quad, held, got, got_o, state, avail, nums):
+    _, rows, _, degrees, steps, fields, chans, _, _ = plan
+    core, member = info[0], info[1]
+    half = fields // 2
+    unpack_state(plan, got_o, 1 - core, state)
     spot = member * 2 + core
     den = jnp.zeros((fields, chans), F32)
     for r in range(rows):
@@ -419,26 +431,32 @@
         den += quad[order[src]] * both
     nums[...] = jnp.zeros_like(nums)
     nums[steps * fields :, :] = jnp.broadcast_to(jnp.sum(den, axis=1, keepdims=True), (fields, nums.shape[1]))
-    table[...] = inv[...].T.astype(BF16)
-    ffw_t[...] = ffw[...].T.astype(BF16)
-    tgt[...] = wanted[...]
-
-
-def prepare_call(plan, info, slots, order, quad, got, got_o, inv, ffw, wanted):
-    group, rows, waves, degrees, steps, fields, chans, _, lons = plan
+
+
+def links_call(plan, info, slots, order, got, inv, ffw, wanted):
+    group, rows, waves, degrees, _, _, chans, _, lons = plan
     span, mine = waves * degrees, rows * waves
     shapes = [
         VM((2, span, chans), F32),
         VM((span, 2 * group * mine), BF16),
         VM((mine, span), BF16),
-        VM((rows, fields, lons), BF16),
-        VM(((steps + 1) * fields, LANES), F32),
         VM((lons, 2 * waves), BF16),
         VM((lons, 2 * waves), BF16),
         VM(wanted.shape, F32),
     ]
-    ins = [got, got_o, inv, ffw, wanted]
-    return step_call(partial(prepare_kernel, plan), "prepare", 1, shapes, ins, (info, slots, order, quad), (span, 2 * span))
+    return step_call(
+        partial(links_kernel, plan), "links", 1, shapes, [got, inv, ffw, wanted], (info, slots, order), (span, 2 * span)
+    )
+
+
+def fields_call(plan, scalars, state, got, got_o):
+    shapes = [
+        VM(state.shape, F32),
+        VM((plan.rows, plan.fields, plan.lons), BF16),
+        VM(((plan.steps + 1) * plan.fields, LANES), F32),
+    ]
+    work = (plan.waves * plan.degrees, 8)
+    return step_call(partial(fields_kernel, plan), "fields", 1, shapes, [state, got, got_o], scalars, work, (), {3: 0})
 
 
 def kernel_params():
@@ -863,12 +881,8 @@
         grads[3][:, slot] = bias
     if not last:
         return
-    packed = refs.pop(0)
-    half = packed.shape[1]
+    half = mine.shape[0]
     parts, at = packed_parts(plan)
-    for which, tile, start, count in parts:
-        for h, dst, src, n in both_halves(start, count, half):
-            packed[h, dst : dst + n, :] = grads[which][src : src + n, tile * LANES : (tile + 1) * LANES]
     lines = []
     for k in range(3):
         prod = grads[k][...] * weights[k][...].astype(F32)
@@ -876,13 +890,20 @@
         for tile in range(1, prod.shape[1] // LANES):
             thin = thin + prod[:, tile * LANES : (tile + 1) * LANES]
         lines.append(jnp.sum(thin.T, axis=0, keepdims=True) / gains[k])
+    tail = []
     for line in (jnp.concatenate(lines, axis=1), jnp.sum(grads[3][...], axis=0, keepdims=True)):
-        for tile in range(line.shape[1] // LANES):
-            packed[1, at - half : at - half + 1, :] = line[:, tile * LANES : (tile + 1) * LANES]
-            at += 1
-    packed[1, at - half :, :] = jnp.zeros((2 * half - at, LANES), F32)
-    mine[...] = packed[info[0]]
-    send[...] = packed[1 - info[0]]
+        tail += [line[:, c : c + LANES] for c in range(0, line.shape[1], LANES)]
+    tail = jnp.concatenate([*tail, jnp.zeros((2 * half - at - len(tail), LANES), F32)], axis=0)
+
+    def pack(halves):
+        for which, tile, start, count in parts:
+            for h, dst, src, n in both_halves(start, count, half):
+                part = grads[which][src : src + n, tile * LANES : (tile + 1) * LANES]
+                halves[h][dst : dst + n, :] = part.astype(halves[h].dtype)
+        halves[1][at - half :, :] = tail.astype(halves[1].dtype)
+
+    pl.when(info[0] == 0)(lambda: pack((mine, send)))
+    pl.when(info[0] == 1)(lambda: pack((send, mine)))
 
 
 def grads_call(plan, step, chips, info, units, dzs, nb, before, weights):
@@ -896,7 +917,7 @@
     if last:
         ins += weights
         half = chips * packed_block(plan, chips)
-        shapes, scratch = [VM((half, LANES), F32)] * 2, [*sums, VM((2, half, LANES), F32)]
+        shapes, scratch = [VM((half, LANES), F32), VM((half, LANES), BF16)], sums
     else:
         shapes, scratch = sums, []
         if not first:
@@ -918,7 +939,7 @@
     lines = jnp.concatenate([lines, jnp.zeros_like(lines)], axis=0).astype(BF16)
     for c in range(chips):
         at = slice(c * blk, (c + 1) * blk)
-        out[c, 0:blk, :] = (mine[at, :] + got[at, :]).astype(BF16)
+        out[c, 0:blk, :] = (mine[at, :] + got[at, :].astype(F32)).astype(BF16)
         out[c, blk:, :] = lines
 
 
@@ -1102,10 +1123,10 @@
     tgt_all = jnp.concatenate([jnp.where(core == 0, targets, theirs), jnp.where(core == 0, theirs, targets)], axis=0)
     tgt = lax.dynamic_index_in_dim(tgt_all, (chip // group) % (2 * tdev), axis=0, keepdims=False)
     tgt = jnp.broadcast_to(tgt.reshape(steps * fields, 1), (steps * fields, LANES))
-    state, links, lt, avail, nums, inv_t, ffw_t, tgt = prepare_call(
-        plan, info, wave_slots, lat_order, quad_weights, got, got_o, inv32, ffw32, tgt
-    )
+    made = links_call(plan, info, wave_slots, lat_order, got, inv32, ffw32, tgt)
+    got_o, (state, links, lt, inv_t, ffw_t, tgt) = lax.optimization_barrier((got_o, made))
     scalars = (info, lat_order, quad_weights)
+    state, avail, nums = fields_call(plan, scalars, state, got, got_o)
 
     saved, pieces = [], None
     for s in range(steps):

time: 128 us -> 127 us (level)
  waiting for transfers between devices: 24.9 us -> 23.3 us
    ppermute x18, waiting for transfers between devices: 8.21 us -> 6.62 us  [grouped_device(): across = lambda a: lax.ppermute(a, 'tm', swap)]
    pallas_call x23 -> x24, Pallas kernels: 51.6 us -> 51.9 us  [step_call(): pl.pallas_call(kernel, out_shape=shapes, grid_spec=pltpu.PrefetchScalarGr...]
  transfers between devices with their start and end apart: 27 -> 27, of which waited for: 18 -> 18; matrix products, arithmetic and copies ran while one was open for 4% -> 4% of each run, Pallas kernels for 15% -> 16%
where the time goes in v6:
time: 127 us; the launch traced here: 126 us
  Pallas kernels  57 us (45%)
  waiting for transfers between devices  23.3 us (18%)
  blocking collectives  21.6 us (17%)
  starting transfers between devices  18.2 us (14%)
  other arithmetic  3.82 us (3%)
  between operations  1.27 us (1%)
    pallas_call x24, Pallas kernels, step_call(): pl.pallas_call(kernel, out_shape=shapes, grid_spec=pltpu.PrefetchScalarGr...  51.9 us
    all_to_all x2, blocking collectives, grouped_device(): lax.all_to_all(a, 'lat', split_axis=0, concat_axis=0, tiled=True, axis_in...  21.6 us
    all_to_all x1, starting transfers between devices, grouped_device(): lax.all_to_all(spread.reshape(waves, *times.shape[1:]), 'lat', split_axis...  8.2 us
    ppermute x6, waiting for transfers between devices, to_members(): lax.ppermute(v, 'lat', [(n, n ^ bit) for n in range(waves)])  7.97 us
    all_to_all x1, waiting for transfers between devices, grouped_device(): lax.all_to_all(spread.reshape(waves, *times.shape[1:]), 'lat', split_axis...  7.93 us
    ppermute x18, waiting for transfers between devices, grouped_device(): across = lambda a: lax.ppermute(a, 'tm', swap)  6.62 us
    ppermute x6, starting transfers between devices, to_members(): lax.ppermute(v, 'lat', [(n, n ^ bit) for n in range(waves)])  6.21 us
    pallas_call x1, Pallas kernels, update_call(): pl.pallas_call(partial(update_kernel, plan), out_shape=[jax.ShapeDtypeStr...  3.4 us
  transfers between devices with their start and end apart: 27, of which 18 were waited for; matrix products, arithmetic and copies ran while one was open for 4% of the time, Pallas kernels for 16%

profile of v6, /device:TPU:0, one launch (start us, length us, event | category | flops | bytes accessed | tf_op | source)
XLA Modules:
  0.0 126.1 jit_solution(13447057527549116590)
XLA Ops:
  0.8 1.5 %pack.1 = (bf16[2,40,256]{2,1,0:T(8,128)(2,1)S(1)}, bf16[2,40,256]{2,1,0:T(8,128)(2,1)S(1)}) custom-call(s32[2]{0:T(128)S(1)} %pad_add_fusion.info, f32[2,1,2,16,256]{4,3,2,1,0:T(8,128)} %state_in.1, s32[2,8,1,256]{3,2,1,0:T(1,128)} %seen_in.1, bf16[1,16,16]{2,1,0:T(8,128)(2,1)} %legendre_in.1), custom_call_target="tpu_custom_call" | custom-call | tf_op jit(solution)/shard_map/pack/pallas_call | solution.py:353
  4.6 8.2 %all-to-all-start = ((bf16[16,40,256]{2,1,0:T(8,128)(2,1)}), bf16[16,40,256]{2,1,0:T(8,128)(2,1)S(1)}, u32[]{:S(2)}, u32[]{:S(2)}) async-start(bf16[16,40,256]{2,1,0:T(8,128)(2,1)} %bitcast.2), calls=%async_computation | async-start | bytes 655360 | tf_op jit(solution)/shard_map/all_to_all | solution.py:1108
  16.5 7.9 %all-to-all-done.got = bf16[16,40,256]{2,1,0:T(8,128)(2,1)S(1)} async-done(((bf16[16,40,256]{2,1,0:T(8,128)(2,1)}), bf16[16,40,256]{2,1,0:T(8,128)(2,1)S(1)}, u32[]{:S(2)}, u32[]{:S(2)}) %all-to-all-start) | async-done | bytes 327712 | tf_op jit(solution)/shard_map/all_to_all | solution.py:1108
  26.7 3.6 %forward_0.1 = (f32[1024,1024]{1,0:T(8,128)S(1)}, f32[1024,768]{1,0:T(8,128)S(1)}, f32[1024,384]{1,0:T(8,128)S(1)}, bf16[2,64,256]{2,1,0:T(8,128)(2,1)S(1)}, f32...) custom-call(s32[2]{0:T(128)S(1)} %pad_add_fusion.info, s32[16]{0:T(128)S(1)} %copy-done.10, f32[16]{0:T(128)S(1)} %copy-done.11, ...), custom_call_target="tpu_custom_call" | custom-call | flops 704643072 | bytes 8388608 | tf_op jit(solution)/shard_map/forward_0/pallas_call | solution.py:573
  30.9 1.5 %slopes_0.1.refs_1_ = f32[1024,768]{1,0:T(8,128)S(1)} custom-call(f32[1024,768]{1,0:T(8,128)S(1)} %get-tuple-element.161.inners, f32[1024,384]{1,0:T(8,128)S(1)} %get-tuple-element.162.scales.refs_2_), custom_call_target="tpu_custom_call", output_to_operand_aliasing={{}: (0, {})} | custom-call | flops 6291456 | bytes 8388608 | tf_op jit(solution)/shard_map/slopes_0/pallas_call | solution.py:573
  32.5 2.2 %collective-permute-done.3.refs_10_ = bf16[2,64,256]{2,1,0:T(8,128)(2,1)S(1)} collective-permute-done((bf16[2,64,256]{2,1,0:T(8,128)(2,1)S(1)}, bf16[2,64,256]{2,1,0:T(8,128)(2,1)S(1)}, u32[]{:S(2)}, u32[]{:S(2)}) %collective-permute-start.3) | collective-permute-done | bytes 65568 | tf_op jit(solution)/shard_map/ppermute | solution.py:1085
  35.9 4.0 %forward_1.1 = (f32[1024,1024]{1,0:T(8,128)S(1)}, f32[1024,768]{1,0:T(8,128)S(1)}, f32[1024,384]{1,0:T(8,128)S(1)}, bf16[2,64,256]{2,1,0:T(8,128)(2,1)S(1)}, f32...) custom-call(s32[2]{0:T(128)S(1)} %pad_add_fusion.info, s32[16]{0:T(128)S(1)} %copy-done.10, ...), custom_call_target="tpu_custom_call" | custom-call | flops 704643072 | bytes 8388608 | tf_op jit(solution)/shard_map/forward_1/pallas_call | solution.py:573
  40.6 1.5 %slopes_1.1.refs_1_ = f32[1024,768]{1,0:T(8,128)S(1)} custom-call(f32[1024,768]{1,0:T(8,128)S(1)} %get-tuple-element.176.inners, f32[1024,384]{1,0:T(8,128)S(1)} %get-tuple-element.177.scales.refs_2_), custom_call_target="tpu_custom_call", output_to_operand_aliasing={{}: (0, {})} | custom-call | flops 6291456 | bytes 8388608 | tf_op jit(solution)/shard_map/slopes_1/pallas_call | solution.py:573
  42.1 2.2 %collective-permute-done.6.refs_10_ = bf16[2,64,256]{2,1,0:T(8,128)(2,1)S(1)} collective-permute-done((bf16[2,64,256]{2,1,0:T(8,128)(2,1)S(1)}, bf16[2,64,256]{2,1,0:T(8,128)(2,1)S(1)}, u32[]{:S(2)}, u32[]{:S(2)}) %collective-permute-start.6) | collective-permute-done | bytes 65568 | tf_op jit(solution)/shard_map/ppermute | solution.py:1085
  45.6 4.0 %forward_2.1 = (f32[1024,1024]{1,0:T(8,128)S(1)}, f32[1024,768]{1,0:T(8,128)S(1)}, f32[1024,384]{1,0:T(8,128)S(1)}, bf16[2,64,256]{2,1,0:T(8,128)(2,1)S(1)}, f32...) custom-call(s32[2]{0:T(128)S(1)} %pad_add_fusion.info, s32[16]{0:T(128)S(1)} %copy-done.10, ...), custom_call_target="tpu_custom_call" | custom-call | flops 704643072 | bytes 8388608 | tf_op jit(solution)/shard_map/forward_2/pallas_call | solution.py:573
  50.3 1.7 %slopes_2.1.refs_1_ = f32[1024,768]{1,0:T(8,128)S(1)} custom-call(f32[1024,768]{1,0:T(8,128)S(1)} %get-tuple-element.190.inners, f32[1024,384]{1,0:T(8,128)S(1)} %get-tuple-element.191.scales.refs_2_), custom_call_target="tpu_custom_call", output_to_operand_aliasing={{}: (0, {})} | custom-call | flops 6291456 | bytes 8388608 | tf_op jit(solution)/shard_map/slopes_2/pallas_call | solution.py:573
  52.0 2.0 %collective-permute-done.9.refs_12_ = bf16[2,64,256]{2,1,0:T(8,128)(2,1)S(1)} collective-permute-done((bf16[2,64,256]{2,1,0:T(8,128)(2,1)S(1)}, bf16[2,64,256]{2,1,0:T(8,128)(2,1)S(1)}, u32[]{:S(2)}, u32[]{:S(2)}) %collective-permute-start.9) | collective-permute-done | bytes 65568 | tf_op jit(solution)/shard_map/ppermute | solution.py:1085
  55.3 4.4 %forward_3.1 = (f32[1024,1024]{1,0:T(8,128)S(1)}, f32[1024,768]{1,0:T(8,128)S(1)}, f32[1024,384]{1,0:T(8,128)S(1)}, f32[40,128]{1,0:T(8,128)S(1)}) custom-call(s32[2]{0:T(128)S(1)} %pad_add_fusion.info, s32[16]{0:T(128)S(1)} %copy-done.10, f32[16]{0:T(128)S(1)} %copy-done.11, f32[2,256,256]{2,1,0:T(8,128)S(1)} %get-tuple-element.193.refs_0_, ...), custom_call_target="tpu_custom_call" | custom-call | flops 704643072 | bytes 8388608 | tf_op jit(solution)/shard_map/forward_3/pallas_call | solution.py:573
  60.3 1.5 %collective-permute-start.12 = (f32[40,128]{1,0:T(8,128)S(1)}, f32[40,128]{1,0:T(8,128)S(1)}, u32[]{:S(2)}, u32[]{:S(2)}) collective-permute-start(f32[40,128]{1,0:T(8,128)S(1)} %get-tuple-element.204.refs_8_.refs_0_), channel_id=1, source_target_pairs={{0,1},{1,0},{2,3},{3,2},{4,5},{5,4},{6,7},{7,6},{8,9},{9,8},{10,11... | collective-permute-start | bytes 61448 | tf_op jit(solution)/shard_map/ppermute | solution.py:1099
  61.8 1.5 %slopes_3.1.refs_1_ = f32[1024,768]{1,0:T(8,128)S(1)} custom-call(f32[1024,768]{1,0:T(8,128)S(1)} %get-tuple-element.205.inners, f32[1024,384]{1,0:T(8,128)S(1)} %get-tuple-element.206.scales.refs_2_), custom_call_target="tpu_custom_call", output_to_operand_aliasing={{}: (0, {})} | custom-call | flops 6291456 | bytes 8388608 | tf_op jit(solution)/shard_map/slopes_3/pallas_call | solution.py:573
  64.1 3.3 %backward_3.1 = (bf16[1024,1024]{1,0:T(8,128)(2,1)S(1)}, bf16[2,64,256]{2,1,0:T(8,128)(2,1)S(1)}, f32[8,128]{1,0:T(8,128)S(1)}) custom-call(s32[2]{0:T(128)S(1)} %pad_add_fusion.info, s32[16]{0:T(128)S(1)} %copy-done.10, f32[16]{0:T(128)S(1)} %copy-done.11, f32[1024,1024]{1,0:T(8,128)S(1)} %get-tuple-element.203.refs_0_, f32[1024,768]{1,0:T(8,128)S(1)} %slopes_3.1.refs_1_, ...), custom_call_target="tpu_custom_call" | custom-call | flops 704643072 | bytes 8388608 | tf_op jit(solution)/shard_map/backward_3/pallas_call | solution.py:573
  67.4 1.5 %collective-permute-start.15 = (bf16[2,64,256]{2,1,0:T(8,128)(2,1)S(1)}, bf16[2,64,256]{2,1,0:T(8,128)(2,1)S(1)}, u32[]{:S(2)}, u32[]{:S(2)}) collective-permute-start(bf16[2,64,256]{2,1,0:T(8,128)(2,1)S(1)} %get-tuple-element.212.refs_10_), channel_id=1, source_target_pairs={{0,1},{1,0},{2,3},{3,2},{4,5},{5,4},{6,7},{7,6},{8,9},{9,8},{10,11... | collective-permute-start | bytes 196616 | tf_op jit(solution)/shard_map/ppermute | solution.py:1085
  69.9 1.9 %grads_3.1 = (f32[256,384]{1,0:T(8,128)S(1)}, f32[384,384]{1,0:T(8,128)S(1)}, f32[384,256]{1,0:T(8,128)S(1)}, f32[8,1024]{1,0:T(8,128)S(1)}) custom-call(s32[2]{0:T(128)S(1)} %pad_add_fusion.info, f32[1024,1024]{1,0:T(8,128)S(1)} %get-tuple-element.203.refs_0_, bf16[1024,1024]{1,0:T(8,128)(2,1)S(1)} %get-tuple-element.213.refs_1_, f32[2,1024]{1,0:T(2,128)S(1)} %copy-done.3), custom_call_target="tpu_custom_call" | custom-call | flops 704643072 | bytes 8388608 | tf_op jit(solution)/shard_map/grads_3/pallas_call | solution.py:573
  73.2 3.7 %backward_2.1 = (bf16[1024,1024]{1,0:T(8,128)(2,1)S(1)}, bf16[2,64,256]{2,1,0:T(8,128)(2,1)S(1)}, f32[2,256,256]{2,1,0:T(8,128)S(1)}) custom-call(s32[2]{0:T(128)S(1)} %pad_add_fusion.info, s32[16]{0:T(128)S(1)} %copy-done.10, f32[16]{0:T(128)S(1)} %copy-done.11, f32[1024,1024]{1,0:T(8,128)S(1)} %get-tuple-element.188.refs_0_, ...), custom_call_target="tpu_custom_call" | custom-call | flops 704643072 | bytes 8388608 | tf_op jit(solution)/shard_map/backward_2/pallas_call | solution.py:573
  77.0 1.5 %collective-permute-start.18 = (bf16[2,64,256]{2,1,0:T(8,128)(2,1)S(1)}, bf16[2,64,256]{2,1,0:T(8,128)(2,1)S(1)}, u32[]{:S(2)}, u32[]{:S(2)}) collective-permute-start(bf16[2,64,256]{2,1,0:T(8,128)(2,1)S(1)} %get-tuple-element.221.refs_10_), channel_id=1, source_target_pairs={{0,1},{1,0},{2,3},{3,2},{4,5},{5,4},{6,7},{7,6},{8,9},{9,8},{10,11... | collective-permute-start | bytes 196616 | tf_op jit(solution)/shard_map/ppermute | solution.py:1085
  78.5 2.0 %grads_2.1 = (f32[256,384]{1,0:T(8,128)S(1)}, f32[384,384]{1,0:T(8,128)S(1)}, f32[384,256]{1,0:T(8,128)S(1)}, f32[8,1024]{1,0:T(8,128)S(1)}) custom-call(s32[2]{0:T(128)S(1)} %pad_add_fusion.info, f32[1024,1024]{1,0:T(8,128)S(1)} %get-tuple-element.188.refs_0_, ...), custom_call_target="tpu_custom_call", output_to_operand_aliasing={{0}: (4, {}), {1}: (5, {}), {2}: (6, {}), {3}: (7, {})} | custom-call | flops 704643072 | bytes 8388608 | tf_op jit(solution)/shard_map/grads_2/pallas_call | solution.py:573
  82.6 3.6 %backward_1.1 = (bf16[1024,1024]{1,0:T(8,128)(2,1)S(1)}, bf16[2,64,256]{2,1,0:T(8,128)(2,1)S(1)}, f32[2,256,256]{2,1,0:T(8,128)S(1)}) custom-call(s32[2]{0:T(128)S(1)} %pad_add_fusion.info, s32[16]{0:T(128)S(1)} %copy-done.10, f32[16]{0:T(128)S(1)} %copy-done.11, f32[1024,1024]{1,0:T(8,128)S(1)} %get-tuple-element.174.refs_0_, ...), custom_call_target="tpu_custom_call" | custom-call | flops 704643072 | bytes 8388608 | tf_op jit(solution)/shard_map/backward_1/pallas_call | solution.py:573
  86.5 1.5 %collective-permute-start.21 = (bf16[2,64,256]{2,1,0:T(8,128)(2,1)S(1)}, bf16[2,64,256]{2,1,0:T(8,128)(2,1)S(1)}, u32[]{:S(2)}, u32[]{:S(2)}) collective-permute-start(bf16[2,64,256]{2,1,0:T(8,128)(2,1)S(1)} %get-tuple-element.234.refs_10_), channel_id=1, source_target_pairs={{0,1},{1,0},{2,3},{3,2},{4,5},{5,4},{6,7},{7,6},{8,9},{9,8},{10,11... | collective-permute-start | bytes 196616 | tf_op jit(solution)/shard_map/ppermute | solution.py:1085
  87.9 2.3 %grads_1.1 = (f32[256,384]{1,0:T(8,128)S(1)}, f32[384,384]{1,0:T(8,128)S(1)}, f32[384,256]{1,0:T(8,128)S(1)}, f32[8,1024]{1,0:T(8,128)S(1)}) custom-call(s32[2]{0:T(128)S(1)} %pad_add_fusion.info, f32[1024,1024]{1,0:T(8,128)S(1)} %get-tuple-element.174.refs_0_, ...), custom_call_target="tpu_custom_call", output_to_operand_aliasing={{0}: (4, {}), {1}: (5, {}), {2}: (6, {}), {3}: (7, {})} | custom-call | flops 704643072 | bytes 8388608 | tf_op jit(solution)/shard_map/grads_1/pallas_call | solution.py:573
  90.8 1.2 collective-permute-done.23.refs_13_
  92.1 2.9 %backward_0.1.refs_1_ = bf16[1024,1024]{1,0:T(8,128)(2,1)S(1)} custom-call(s32[2]{0:T(128)S(1)} %pad_add_fusion.info, s32[16]{0:T(128)S(1)} %copy-done.10, f32[16]{0:T(128)S(1)} %copy-done.11, f32[1024,1024]{1,0:T(8,128)S(1)} %get-tuple-element.159.refs_0_, f32[1024,768]{1,0:T(8,128)S(1)} %slopes_0.1.refs_1_, ...), custom_call_target="tpu_custom_call" | custom-call | flops 704643072 | bytes 8388608 | tf_op jit(solution)/shard_map/backward_0/pallas_call | solution.py:573
  95.0 2.2 %grads_0.1 = (f32[1408,128]{1,0:T(8,128)S(1)}, bf16[1408,128]{1,0:T(8,128)(2,1)S(1)}) custom-call(s32[2]{0:T(128)S(1)} %pad_add_fusion.info, f32[1024,1024]{1,0:T(8,128)S(1)} %get-tuple-element.159.refs_0_, bf16[1024,1024]{1,0:T(8,128)(2,1)S(1)} %backward_0.1.refs_1_, f32[2,1024]{1,0:T(2,128)S(1)} %copy-done.3, f32[256,384]{1,0:T(8,128)S(1)} %get-tuple-element.247.refs_3_, ...), custom_call_target="tpu_custom_call" | custom-call | flops 704643072 | bytes 8388608 | tf_op jit(solution)/shard_map/grads_0/pallas_call | solution.py:573
  97.6 1.5 %collective-permute-done.24.got = bf16[1408,128]{1,0:T(8,128)(2,1)S(1)} collective-permute-done((bf16[1408,128]{1,0:T(8,128)(2,1)S(1)}, bf16[1408,128]{1,0:T(8,128)(2,1)S(1)}, u32[]{:S(2)}, u32[]{:S(2)}) %collective-permute-start.24) | collective-permute-done | bytes 360480 | tf_op jit(solution)/shard_map/ppermute | solution.py:1079
  99.1 11.7 %all_to_all.15.got = bf16[8,192,128]{2,1,0:T(8,128)(2,1)S(1)} all-to-all(bf16[8,192,128]{2,1,0:T(8,128)(2,1)S(1)} %pairs.1), channel_id=1, replica_groups={{0,1,2,3,4,5,6,7},{8,9,10,11,12,13,14,15},{16,17,18,19,20,21,22,23},{24..., dimensions={0} | all-to-all | bytes 786432 | tf_op jit(solution)/shard_map/all_to_all | solution.py:1163
  110.9 9.9 %all_to_all.16 = bf16[8,176,128]{2,1,0:T(8,128)(2,1)S(1)} all-to-all(bf16[8,176,128]{2,1,0:T(8,128)(2,1)S(1)} %get-tuple-element.254), channel_id=1, replica_groups={{0,1,2,3,4,5,6,7},{8,9,10,11,12,13,14,15},{16,17,18,19,20,21,22,23},{24..., dimensions={0} | all-to-all | bytes 720896 | tf_op jit(solution)/shard_map/all_to_all | solution.py:1163
  120.8 1.7 %collective-permute-done.25.part_o = bf16[1408,128]{1,0:T(8,128)(2,1)S(1)} collective-permute-done((bf16[1408,128]{1,0:T(8,128)(2,1)S(1)}, bf16[1408,128]{1,0:T(8,128)(2,1)S(1)}, u32[]{:S(2)}, u32[]{:S(2)}) %collective-permute-start.25) | collective-permute-done | bytes 360480 | tf_op jit(solution)/shard_map/ppermute | solution.py:1079
  122.5 3.4 %update.1 = (f32[1,1]{1,0:T(1,128)}, f32[1,1]{1,0:T(1,128)}, f32[256,384]{1,0:T(8,128)}, f32[384,384]{1,0:T(8,128)}, f32[384,256]{1,0:T(8,128)}, /*index=5*/f32[...) custom-call(s32[2]{0:T(128)S(1)} %pad_add_fusion.info, ...), custom_call_target="tpu_custom_call" | custom-call | tf_op jit(solution)/shard_map/update/pallas_call | solution.py:1023
  (100 shorter events, 21.4 us)
Async XLA Ops:
  0.7 25.3 %copy-start.11 = (f32[16]{0:T(128)S(1)}, f32[16]{0:T(128)}, u32[]{:S(2)}) copy-start(f32[16]{0:T(128)} %quad.29) | copy-start | bytes 196
  0.7 26.0 %copy-start.3 = (f32[2,1024]{1,0:T(2,128)S(1)}, f32[2,1024]{1,0:T(2,128)}, u32[]{:S(2)}) copy-start(f32[2,1024]{1,0:T(2,128)} %refs_3_.1) | copy-start | bytes 24580
  2.4 1.4 %collective-permute-start = (bf16[2,40,256]{2,1,0:T(8,128)(2,1)S(1)}, bf16[2,40,256]{2,1,0:T(8,128)(2,1)S(1)}, u32[]{:S(2)}, u32[]{:S(2)}) collective-permute-start(bf16[2,40,256]{2,1,0:T(8,128)(2,1)S(1)} %get-tuple-element.147), channel_id=1, source_target_pairs={{0,16},{16,0},{1,17},{17,1},{2,18},{18,2},{3,19},{19,3},{4,20},{20... | collective-permute-start | bytes 122888 | tf_op jit(solution)/shard_map/ppermute | solution.py:1079
  2.9 21.5 %collective-permute-start.2 = (f32[2,4,8]{2,1,0:T(4,128)}, f32[2,4,8]{2,1,0:T(4,128)S(1)}, u32[]{:S(2)}, u32[]{:S(2)}) collective-permute-start(f32[2,4,8]{2,1,0:T(4,128)} %param.25), channel_id=1, source_target_pairs={{0,16},{16,0},{1,17},{17,1},{2,18},{18,2},{3,19},{19,3},{4,20},{20... | collective-permute-start | bytes 776 | tf_op jit(solution)/shard_map/ppermute | solution.py:1079
  4.6 19.8 %all-to-all-start = ((bf16[16,40,256]{2,1,0:T(8,128)(2,1)}), bf16[16,40,256]{2,1,0:T(8,128)(2,1)S(1)}, u32[]{:S(2)}, u32[]{:S(2)}) async-start(bf16[16,40,256]{2,1,0:T(8,128)(2,1)} %bitcast.2), calls=%async_computation | async-start | bytes 655360 | tf_op jit(solution)/shard_map/all_to_all | solution.py:1108
  24.4 1.6 %collective-permute-start.1 = (bf16[16,40,256]{2,1,0:T(8,128)(2,1)S(1)}, bf16[16,40,256]{2,1,0:T(8,128)(2,1)S(1)}, u32[]{:S(2)}, u32[]{:S(2)}) collective-permute-start(bf16[16,40,256]{2,1,0:T(8,128)(2,1)S(1)} %all-to-all-done.got), channel_id=1, source_target_pairs={{0,16},{16,0},{1,17},{17,1},{2,18},{18,2},{3,19},{19,3},{4,20},{20... | collective-permute-start | bytes 983048 | tf_op jit(solution)/shard_map/ppermute | solution.py:1079
  30.3 4.3 %collective-permute-start.3 = (bf16[2,64,256]{2,1,0:T(8,128)(2,1)S(1)}, bf16[2,64,256]{2,1,0:T(8,128)(2,1)S(1)}, u32[]{:S(2)}, u32[]{:S(2)}) collective-permute-start(bf16[2,64,256]{2,1,0:T(8,128)(2,1)S(1)} %get-tuple-element.170.refs_9_), channel_id=1, source_target_pairs={{0,1},{1,0},{2,3},{3,2},{4,5},{5,4},{6,7},{7,6},{8,9},{9,8},{10,11... | collective-permute-start | bytes 196616 | tf_op jit(solution)/shard_map/ppermute | solution.py:1085
  30.9 4.9 %collective-permute-start.4 = (bf16[2,64,256]{2,1,0:T(8,128)(2,1)S(1)}, bf16[2,64,256]{2,1,0:T(8,128)(2,1)S(1)}, u32[]{:S(2)}, u32[]{:S(2)}) collective-permute-start(bf16[2,64,256]{2,1,0:T(8,128)(2,1)S(1)} %get-tuple-element.170.refs_9_), channel_id=1, source_target_pairs={{0,16},{16,0},{1,17},{17,1},{2,18},{18,2},{3,19},{19,3},{4,20},{20... | collective-permute-start | bytes 196616 | tf_op jit(solution)/shard_map/ppermute | solution.py:1079
  34.6 1.3 collective-permute-start.5
  39.9 4.5 %collective-permute-start.6 = (bf16[2,64,256]{2,1,0:T(8,128)(2,1)S(1)}, bf16[2,64,256]{2,1,0:T(8,128)(2,1)S(1)}, u32[]{:S(2)}, u32[]{:S(2)}) collective-permute-start(bf16[2,64,256]{2,1,0:T(8,128)(2,1)S(1)} %get-tuple-element.184.refs_9_), channel_id=1, source_target_pairs={{0,1},{1,0},{2,3},{3,2},{4,5},{5,4},{6,7},{7,6},{8,9},{9,8},{10,11... | collective-permute-start | bytes 196616 | tf_op jit(solution)/shard_map/ppermute | solution.py:1085
  40.4 5.0 %collective-permute-start.7 = (bf16[2,64,256]{2,1,0:T(8,128)(2,1)S(1)}, bf16[2,64,256]{2,1,0:T(8,128)(2,1)S(1)}, u32[]{:S(2)}, u32[]{:S(2)}) collective-permute-start(bf16[2,64,256]{2,1,0:T(8,128)(2,1)S(1)} %get-tuple-element.184.refs_9_), channel_id=1, source_target_pairs={{0,16},{16,0},{1,17},{17,1},{2,18},{18,2},{3,19},{19,3},{4,20},{20... | collective-permute-start | bytes 196616 | tf_op jit(solution)/shard_map/ppermute | solution.py:1079
  44.3 1.3 collective-permute-start.8
  49.5 4.5 %collective-permute-start.9 = (bf16[2,64,256]{2,1,0:T(8,128)(2,1)S(1)}, bf16[2,64,256]{2,1,0:T(8,128)(2,1)S(1)}, u32[]{:S(2)}, u32[]{:S(2)}) collective-permute-start(bf16[2,64,256]{2,1,0:T(8,128)(2,1)S(1)} %get-tuple-element.199.refs_11_), channel_id=1, source_target_pairs={{0,1},{1,0},{2,3},{3,2},{4,5},{5,4},{6,7},{7,6},{8,9},{9,8},{10,11... | collective-permute-start | bytes 196616 | tf_op jit(solution)/shard_map/ppermute | solution.py:1085
  50.1 5.0 %collective-permute-start.10 = (bf16[2,64,256]{2,1,0:T(8,128)(2,1)S(1)}, bf16[2,64,256]{2,1,0:T(8,128)(2,1)S(1)}, u32[]{:S(2)}, u32[]{:S(2)}) collective-permute-start(bf16[2,64,256]{2,1,0:T(8,128)(2,1)S(1)} %get-tuple-element.199.refs_11_), channel_id=1, source_target_pairs={{0,16},{16,0},{1,17},{17,1},{2,18},{18,2},{3,19},{19,3},{4,20},{20... | collective-permute-start | bytes 196616 | tf_op jit(solution)/shard_map/ppermute | solution.py:1079
  54.0 1.3 collective-permute-start.11
  59.7 3.7 %collective-permute-start.14 = (f32[40,128]{1,0:T(8,128)S(1)}, f32[40,128]{1,0:T(8,128)S(1)}, u32[]{:S(2)}, u32[]{:S(2)}) collective-permute-start(f32[40,128]{1,0:T(8,128)S(1)} %get-tuple-element.204.refs_8_.refs_0_), channel_id=1, source_target_pairs={{0,17},{1,16},{2,19},{3,18},{4,21},{5,20},{6,23},{7,22},{8,25},{9,... | collective-permute-start | bytes 61448 | tf_op jit(solution)/shard_map/ppermute | solution.py:1099
  60.3 3.1 %collective-permute-start.13 = (f32[40,128]{1,0:T(8,128)S(1)}, f32[40,128]{1,0:T(8,128)S(1)}, u32[]{:S(2)}, u32[]{:S(2)}) collective-permute-start(f32[40,128]{1,0:T(8,128)S(1)} %get-tuple-element.204.refs_8_.refs_0_), channel_id=1, source_target_pairs={{0,16},{16,0},{1,17},{17,1},{2,18},{18,2},{3,19},{19,3},{4,20},{20... | collective-permute-start | bytes 61448 | tf_op jit(solution)/shard_map/ppermute | solution.py:1079
  60.3 3.8 %collective-permute-start.12 = (f32[40,128]{1,0:T(8,128)S(1)}, f32[40,128]{1,0:T(8,128)S(1)}, u32[]{:S(2)}, u32[]{:S(2)}) collective-permute-start(f32[40,128]{1,0:T(8,128)S(1)} %get-tuple-element.204.refs_8_.refs_0_), channel_id=1, source_target_pairs={{0,1},{1,0},{2,3},{3,2},{4,5},{5,4},{6,7},{7,6},{8,9},{9,8},{10,11... | collective-permute-start | bytes 61448 | tf_op jit(solution)/shard_map/ppermute | solution.py:1099
  67.4 5.4 %collective-permute-start.16 = (bf16[2,64,256]{2,1,0:T(8,128)(2,1)S(1)}, bf16[2,64,256]{2,1,0:T(8,128)(2,1)S(1)}, u32[]{:S(2)}, u32[]{:S(2)}) collective-permute-start(bf16[2,64,256]{2,1,0:T(8,128)(2,1)S(1)} %get-tuple-element.212.refs_10_), channel_id=1, source_target_pairs={{0,16},{16,0},{1,17},{17,1},{2,18},{18,2},{3,19},{19,3},{4,20},{20... | collective-permute-start | bytes 196616 | tf_op jit(solution)/shard_map/ppermute | solution.py:1079
  67.4 4.5 %collective-permute-start.15 = (bf16[2,64,256]{2,1,0:T(8,128)(2,1)S(1)}, bf16[2,64,256]{2,1,0:T(8,128)(2,1)S(1)}, u32[]{:S(2)}, u32[]{:S(2)}) collective-permute-start(bf16[2,64,256]{2,1,0:T(8,128)(2,1)S(1)} %get-tuple-element.212.refs_10_), channel_id=1, source_target_pairs={{0,1},{1,0},{2,3},{3,2},{4,5},{5,4},{6,7},{7,6},{8,9},{9,8},{10,11... | collective-permute-start | bytes 196616 | tf_op jit(solution)/shard_map/ppermute | solution.py:1085
  72.0 1.3 collective-permute-start.17
  76.9 5.4 %collective-permute-start.19 = (bf16[2,64,256]{2,1,0:T(8,128)(2,1)S(1)}, bf16[2,64,256]{2,1,0:T(8,128)(2,1)S(1)}, u32[]{:S(2)}, u32[]{:S(2)}) collective-permute-start(bf16[2,64,256]{2,1,0:T(8,128)(2,1)S(1)} %get-tuple-element.221.refs_10_), channel_id=1, source_target_pairs={{0,16},{16,0},{1,17},{17,1},{2,18},{18,2},{3,19},{19,3},{4,20},{20... | collective-permute-start | bytes 196616 | tf_op jit(solution)/shard_map/ppermute | solution.py:1079
  77.0 4.3 %collective-permute-start.18 = (bf16[2,64,256]{2,1,0:T(8,128)(2,1)S(1)}, bf16[2,64,256]{2,1,0:T(8,128)(2,1)S(1)}, u32[]{:S(2)}, u32[]{:S(2)}) collective-permute-start(bf16[2,64,256]{2,1,0:T(8,128)(2,1)S(1)} %get-tuple-element.221.refs_10_), channel_id=1, source_target_pairs={{0,1},{1,0},{2,3},{3,2},{4,5},{5,4},{6,7},{7,6},{8,9},{9,8},{10,11... | collective-permute-start | bytes 196616 | tf_op jit(solution)/shard_map/ppermute | solution.py:1085
  81.4 1.3 collective-permute-start.20
  86.3 4.5 %collective-permute-start.22 = (bf16[2,64,256]{2,1,0:T(8,128)(2,1)S(1)}, bf16[2,64,256]{2,1,0:T(8,128)(2,1)S(1)}, u32[]{:S(2)}, u32[]{:S(2)}) collective-permute-start(bf16[2,64,256]{2,1,0:T(8,128)(2,1)S(1)} %get-tuple-element.234.refs_10_), channel_id=1, source_target_pairs={{0,16},{16,0},{1,17},{17,1},{2,18},{18,2},{3,19},{19,3},{4,20},{20... | collective-permute-start | bytes 196616 | tf_op jit(solution)/shard_map/ppermute | solution.py:1079
  86.5 4.3 %collective-permute-start.21 = (bf16[2,64,256]{2,1,0:T(8,128)(2,1)S(1)}, bf16[2,64,256]{2,1,0:T(8,128)(2,1)S(1)}, u32[]{:S(2)}, u32[]{:S(2)}) collective-permute-start(bf16[2,64,256]{2,1,0:T(8,128)(2,1)S(1)} %get-tuple-element.234.refs_10_), channel_id=1, source_target_pairs={{0,1},{1,0},{2,3},{3,2},{4,5},{5,4},{6,7},{7,6},{8,9},{9,8},{10,11... | collective-permute-start | bytes 196616 | tf_op jit(solution)/shard_map/ppermute | solution.py:1085
  90.8 1.3 collective-permute-start.23
  95.0 27.5 %copy-start.9 = (f32[384,256]{1,0:T(8,128)S(1)}, f32[384,256]{1,0:T(8,128)}, u32[]{:S(2)}) copy-start(f32[384,256]{1,0:T(8,128)} %refs_10_.1) | copy-start | bytes 1179652
  97.2 25.3 %copy-start.1 = (f32[256,384]{1,0:T(8,128)S(1)}, f32[256,384]{1,0:T(8,128)}, u32[]{:S(2)}) copy-start(f32[256,384]{1,0:T(8,128)} %refs_0_.1) | copy-start | bytes 1179652
  97.2 25.3 %copy-start.2 = (f32[384,256]{1,0:T(8,128)S(1)}, f32[384,256]{1,0:T(8,128)}, u32[]{:S(2)}) copy-start(f32[384,256]{1,0:T(8,128)} %refs_2_.9) | copy-start | bytes 1179652
  97.3 1.7 %collective-permute-start.24 = (bf16[1408,128]{1,0:T(8,128)(2,1)S(1)}, bf16[1408,128]{1,0:T(8,128)(2,1)S(1)}, u32[]{:S(2)}, u32[]{:S(2)}) collective-permute-start(bf16[1408,128]{1,0:T(8,128)(2,1)S(1)} %get-tuple-element.252), channel_id=1, source_target_pairs={{0,16},{16,0},{1,17},{17,1},{2,18},{18,2},{3,19},{19,3},{4,20},{20... | collective-permute-start | bytes 1081352 | tf_op jit(solution)/shard_map/ppermute | solution.py:1079
  120.8 1.7 %collective-permute-start.25 = (bf16[1408,128]{1,0:T(8,128)(2,1)S(1)}, bf16[1408,128]{1,0:T(8,128)(2,1)S(1)}, u32[]{:S(2)}, u32[]{:S(2)}) collective-permute-start(bf16[1408,128]{1,0:T(8,128)(2,1)S(1)} %bitcast.10), channel_id=1, source_target_pairs={{0,16},{16,0},{1,17},{17,1},{2,18},{18,2},{3,19},{19,3},{4,20},{20... | collective-permute-start | bytes 1081352 | tf_op jit(solution)/shard_map/ppermute | solution.py:1079
  (11 other events, 264.3 us)

commit v7 on v6

--- a/solution.py
+++ b/solution.py
@@ -484,7 +484,8 @@
     rows_blk = pair_rows(plan)
     refs = list(refs)
     take = lambda: refs.pop(0)
-    state, table, ffw, lt, w1, w2, w3, nb = [take() for _ in range(8)]
+    state = [take() for _ in range(2 if first else 1)]
+    table, ffw, lt, w1, w2, w3, nb = [take() for _ in range(7)]
     if last:
         avail, nums_in = take(), take()
     if not first:
@@ -503,13 +504,14 @@
 
     @pl.when(i == 0)
     def _():
-        for p in range(2):
-            st = state[p]
-            if not first:
-                spec = dot(links[...], jnp.concatenate([piece[p] for piece in pieces], axis=0))
-                st = st + STEP_SCALE * spec
-                if not last:
-                    state_out[p] = st
+        for p, ref in zip((info[0], 1 - info[0]), state if first else ()):
+            high = ref[:, 0 : plan.degrees, :].reshape(waves * plan.degrees, chans)
+            sums[p] = dot(lt[...], high).astype(BF16)
+        for p in range(0 if first else 2):
+            spec = dot(links[...], jnp.concatenate([piece[p] for piece in pieces], axis=0))
+            st = state[0][p] + STEP_SCALE * spec
+            if not last:
+                state_out[p] = st
             sums[p] = dot(lt[...], st.astype(BF16)).astype(BF16)
         if last:
             num_acc[...] = jnp.zeros_like(num_acc)
@@ -592,7 +594,7 @@
     first, last = step == 0, step == steps - 1
     rows_blk = pair_rows(plan)
     cols = rows * lons
-    ins = [state, table, ffw, lt, *weights, nb]
+    ins = [*state, table, ffw, lt, *weights, nb]
     if last:
         ins += [avail, nums]
     if not first:
@@ -606,7 +608,7 @@
     else:
         shapes += [VM(sums, BF16), VM((cols, chans), F32), VM(sums, BF16)]
         if not first:
-            shapes.append(VM(state.shape, F32))
+            shapes.append(VM(state[0].shape, F32))
     flops = 2 * hidden * (2 * chans + hidden)
     return step_call(
         partial(forward_kernel, plan, step), f"forward_{step}", rows // rows_blk, shapes, ins, scalars, (cols, flops), scratch
@@ -1126,16 +1128,19 @@
     made = links_call(plan, info, wave_slots, lat_order, got, inv32, ffw32, tgt)
     got_o, (state, links, lt, inv_t, ffw_t, tgt) = lax.optimization_barrier((got_o, made))
     scalars = (info, lat_order, quad_weights)
-    state, avail, nums = fields_call(plan, scalars, state, got, got_o)
-
-    saved, pieces = [], None
+
+    saved, pieces, avail, nums = [], None, None, None
     for s in range(steps):
         units, inners, scales, *rest = forward_call(
-            plan, s, scalars, state, avail, nums, inv_t, ffw, lt, weights, nb, links, pieces
+            plan, s, scalars, [state] if s else [got, got_o], avail, nums, inv_t, ffw, lt, weights, nb, links, pieces
         )
         fill = lambda: slopes_call(plan, s, inners, scales)
+        if s == 0:
+            fields = lambda: fields_call(plan, scalars, state, got, got_o)
+            pieces, (slopes, (state, avail, nums)) = to_members(rest[2], lambda: (fill(), fields()))
+        elif s < steps - 1:
+            pieces, slopes = to_members(rest[2], fill)
         if s < steps - 1:
-            pieces, slopes = to_members(rest[2], fill)
             nums = counts_call(plan, s, scalars, [rest[0], rest[1], avail, nums, inv_t])
             pieces, nums = lax.optimization_barrier((pieces, nums))
             if s:

time: 127 us -> 126 us (level)
  no operation moved by 1% of the time
where the time goes in v7:
time: 126 us; the launch traced here: 125 us
  Pallas kernels  57 us (45%)
  waiting for transfers between devices  22.6 us (18%)
  blocking collectives  21.6 us (17%)
  starting transfers between devices  18.2 us (14%)
  other arithmetic  3.82 us (3%)
  between operations  1.27 us (1%)
    pallas_call x24, Pallas kernels, step_call(): pl.pallas_call(kernel, out_shape=shapes, grid_spec=pltpu.PrefetchScalarGr...  51.9 us
    all_to_all x2, blocking collectives, grouped_device(): lax.all_to_all(a, 'lat', split_axis=0, concat_axis=0, tiled=True, axis_in...  21.6 us
    all_to_all x1, starting transfers between devices, grouped_device(): lax.all_to_all(spread.reshape(waves, *times.shape[1:]), 'lat', split_axis...  8.2 us
    all_to_all x1, waiting for transfers between devices, grouped_device(): lax.all_to_all(spread.reshape(waves, *times.shape[1:]), 'lat', split_axis...  7.93 us
    ppermute x6, waiting for transfers between devices, to_members(): lax.ppermute(v, 'lat', [(n, n ^ bit) for n in range(waves)])  7.31 us
    ppermute x18, waiting for transfers between devices, grouped_device(): across = lambda a: lax.ppermute(a, 'tm', swap)  6.62 us
    ppermute x6, starting transfers between devices, to_members(): lax.ppermute(v, 'lat', [(n, n ^ bit) for n in range(waves)])  6.21 us
    pallas_call x1, Pallas kernels, update_call(): pl.pallas_call(partial(update_kernel, plan), out_shape=[jax.ShapeDtypeStr...  3.4 us
  transfers between devices with their start and end apart: 27, of which 18 were waited for; matrix products, arithmetic and copies ran while one was open for 4% of the time, Pallas kernels for 16%

profile of v7, /device:TPU:0, one launch (start us, length us, event | category | flops | bytes accessed | tf_op | source)
XLA Modules:
  0.0 125.5 jit_solution(6993102620949328961)
XLA Ops:
  0.8 1.5 %pack.1 = (bf16[2,40,256]{2,1,0:T(8,128)(2,1)S(1)}, bf16[2,40,256]{2,1,0:T(8,128)(2,1)S(1)}) custom-call(s32[2]{0:T(128)S(1)} %pad_add_fusion.info, f32[2,1,2,16,256]{4,3,2,1,0:T(8,128)} %state_in.1, s32[2,8,1,256]{3,2,1,0:T(1,128)} %seen_in.1, bf16[1,16,16]{2,1,0:T(8,128)(2,1)} %legendre_in.1), custom_call_target="tpu_custom_call" | custom-call | tf_op jit(solution)/shard_map/pack/pallas_call | solution.py:353
  4.6 8.2 %all-to-all-start = ((bf16[16,40,256]{2,1,0:T(8,128)(2,1)}), bf16[16,40,256]{2,1,0:T(8,128)(2,1)S(1)}, u32[]{:S(2)}, u32[]{:S(2)}) async-start(bf16[16,40,256]{2,1,0:T(8,128)(2,1)} %bitcast.2), calls=%async_computation | async-start | bytes 655360 | tf_op jit(solution)/shard_map/all_to_all | solution.py:1110
  16.5 7.9 %all-to-all-done.got.refs_0_ = bf16[16,40,256]{2,1,0:T(8,128)(2,1)S(1)} async-done(((bf16[16,40,256]{2,1,0:T(8,128)(2,1)}), bf16[16,40,256]{2,1,0:T(8,128)(2,1)S(1)}, u32[]{:S(2)}, u32[]{:S(2)}) %all-to-all-start) | async-done | bytes 327712 | tf_op jit(solution)/shard_map/all_to_all | solution.py:1110
  26.1 3.6 %forward_0.1 = (f32[1024,1024]{1,0:T(8,128)S(1)}, f32[1024,768]{1,0:T(8,128)S(1)}, f32[1024,384]{1,0:T(8,128)S(1)}, bf16[2,64,256]{2,1,0:T(8,128)(2,1)S(1)}, f32...) custom-call(s32[2]{0:T(128)S(1)} %pad_add_fusion.info, s32[16]{0:T(128)S(1)} %copy-done.10, f32[16]{0:T(128)S(1)} %copy-done.11, ...), custom_call_target="tpu_custom_call" | custom-call | flops 704643072 | bytes 8388608 | tf_op jit(solution)/shard_map/forward_0/pallas_call | solution.py:575
  30.9 1.5 %slopes_0.1.refs_1_ = f32[1024,768]{1,0:T(8,128)S(1)} custom-call(f32[1024,768]{1,0:T(8,128)S(1)} %get-tuple-element.162.inners, f32[1024,384]{1,0:T(8,128)S(1)} %get-tuple-element.163.scales.refs_2_), custom_call_target="tpu_custom_call", output_to_operand_aliasing={{}: (0, {})} | custom-call | flops 6291456 | bytes 8388608 | tf_op jit(solution)/shard_map/slopes_0/pallas_call | solution.py:575
  32.5 1.5 %collective-permute-done.3.refs_10_ = bf16[2,64,256]{2,1,0:T(8,128)(2,1)S(1)} collective-permute-done((bf16[2,64,256]{2,1,0:T(8,128)(2,1)S(1)}, bf16[2,64,256]{2,1,0:T(8,128)(2,1)S(1)}, u32[]{:S(2)}, u32[]{:S(2)}) %collective-permute-start.3) | collective-permute-done | bytes 65568 | tf_op jit(solution)/shard_map/ppermute | solution.py:1087
  35.2 4.0 %forward_1.1 = (f32[1024,1024]{1,0:T(8,128)S(1)}, f32[1024,768]{1,0:T(8,128)S(1)}, f32[1024,384]{1,0:T(8,128)S(1)}, bf16[2,64,256]{2,1,0:T(8,128)(2,1)S(1)}, f32...) custom-call(s32[2]{0:T(128)S(1)} %pad_add_fusion.info, s32[16]{0:T(128)S(1)} %copy-done.10, ...), custom_call_target="tpu_custom_call" | custom-call | flops 704643072 | bytes 8388608 | tf_op jit(solution)/shard_map/forward_1/pallas_call | solution.py:575
  39.9 1.5 %slopes_1.1.refs_1_ = f32[1024,768]{1,0:T(8,128)S(1)} custom-call(f32[1024,768]{1,0:T(8,128)S(1)} %get-tuple-element.182.inners, f32[1024,384]{1,0:T(8,128)S(1)} %get-tuple-element.183.scales.refs_2_), custom_call_target="tpu_custom_call", output_to_operand_aliasing={{}: (0, {})} | custom-call | flops 6291456 | bytes 8388608 | tf_op jit(solution)/shard_map/slopes_1/pallas_call | solution.py:575
  41.5 2.2 %collective-permute-done.6.refs_10_ = bf16[2,64,256]{2,1,0:T(8,128)(2,1)S(1)} collective-permute-done((bf16[2,64,256]{2,1,0:T(8,128)(2,1)S(1)}, bf16[2,64,256]{2,1,0:T(8,128)(2,1)S(1)}, u32[]{:S(2)}, u32[]{:S(2)}) %collective-permute-start.6) | collective-permute-done | bytes 65568 | tf_op jit(solution)/shard_map/ppermute | solution.py:1087
  44.9 4.0 %forward_2.1 = (f32[1024,1024]{1,0:T(8,128)S(1)}, f32[1024,768]{1,0:T(8,128)S(1)}, f32[1024,384]{1,0:T(8,128)S(1)}, bf16[2,64,256]{2,1,0:T(8,128)(2,1)S(1)}, f32...) custom-call(s32[2]{0:T(128)S(1)} %pad_add_fusion.info, s32[16]{0:T(128)S(1)} %copy-done.10, ...), custom_call_target="tpu_custom_call" | custom-call | flops 704643072 | bytes 8388608 | tf_op jit(solution)/shard_map/forward_2/pallas_call | solution.py:575
  49.6 1.7 %slopes_2.1.refs_1_ = f32[1024,768]{1,0:T(8,128)S(1)} custom-call(f32[1024,768]{1,0:T(8,128)S(1)} %get-tuple-element.196.inners, f32[1024,384]{1,0:T(8,128)S(1)} %get-tuple-element.197.scales.refs_2_), custom_call_target="tpu_custom_call", output_to_operand_aliasing={{}: (0, {})} | custom-call | flops 6291456 | bytes 8388608 | tf_op jit(solution)/shard_map/slopes_2/pallas_call | solution.py:575
  51.3 2.0 %collective-permute-done.9.refs_12_ = bf16[2,64,256]{2,1,0:T(8,128)(2,1)S(1)} collective-permute-done((bf16[2,64,256]{2,1,0:T(8,128)(2,1)S(1)}, bf16[2,64,256]{2,1,0:T(8,128)(2,1)S(1)}, u32[]{:S(2)}, u32[]{:S(2)}) %collective-permute-start.9) | collective-permute-done | bytes 65568 | tf_op jit(solution)/shard_map/ppermute | solution.py:1087
  54.6 4.4 %forward_3.1 = (f32[1024,1024]{1,0:T(8,128)S(1)}, f32[1024,768]{1,0:T(8,128)S(1)}, f32[1024,384]{1,0:T(8,128)S(1)}, f32[40,128]{1,0:T(8,128)S(1)}) custom-call(s32[2]{0:T(128)S(1)} %pad_add_fusion.info, s32[16]{0:T(128)S(1)} %copy-done.10, f32[16]{0:T(128)S(1)} %copy-done.11, f32[2,256,256]{2,1,0:T(8,128)S(1)} %get-tuple-element.199.refs_0_, ...), custom_call_target="tpu_custom_call" | custom-call | flops 704643072 | bytes 8388608 | tf_op jit(solution)/shard_map/forward_3/pallas_call | solution.py:575
  59.7 1.5 %collective-permute-start.12 = (f32[40,128]{1,0:T(8,128)S(1)}, f32[40,128]{1,0:T(8,128)S(1)}, u32[]{:S(2)}, u32[]{:S(2)}) collective-permute-start(f32[40,128]{1,0:T(8,128)S(1)} %get-tuple-element.210.refs_8_.refs_0_), channel_id=1, source_target_pairs={{0,1},{1,0},{2,3},{3,2},{4,5},{5,4},{6,7},{7,6},{8,9},{9,8},{10,11... | collective-permute-start | bytes 61448 | tf_op jit(solution)/shard_map/ppermute | solution.py:1101
  61.1 1.5 %slopes_3.1.refs_1_ = f32[1024,768]{1,0:T(8,128)S(1)} custom-call(f32[1024,768]{1,0:T(8,128)S(1)} %get-tuple-element.211.inners, f32[1024,384]{1,0:T(8,128)S(1)} %get-tuple-element.212.scales.refs_2_), custom_call_target="tpu_custom_call", output_to_operand_aliasing={{}: (0, {})} | custom-call | flops 6291456 | bytes 8388608 | tf_op jit(solution)/shard_map/slopes_3/pallas_call | solution.py:575
  63.5 3.3 %backward_3.1 = (bf16[1024,1024]{1,0:T(8,128)(2,1)S(1)}, bf16[2,64,256]{2,1,0:T(8,128)(2,1)S(1)}, f32[8,128]{1,0:T(8,128)S(1)}) custom-call(s32[2]{0:T(128)S(1)} %pad_add_fusion.info, s32[16]{0:T(128)S(1)} %copy-done.10, f32[16]{0:T(128)S(1)} %copy-done.11, f32[1024,1024]{1,0:T(8,128)S(1)} %get-tuple-element.209.refs_0_, f32[1024,768]{1,0:T(8,128)S(1)} %slopes_3.1.refs_1_, ...), custom_call_target="tpu_custom_call" | custom-call | flops 704643072 | bytes 8388608 | tf_op jit(solution)/shard_map/backward_3/pallas_call | solution.py:575
  66.8 1.5 %collective-permute-start.15 = (bf16[2,64,256]{2,1,0:T(8,128)(2,1)S(1)}, bf16[2,64,256]{2,1,0:T(8,128)(2,1)S(1)}, u32[]{:S(2)}, u32[]{:S(2)}) collective-permute-start(bf16[2,64,256]{2,1,0:T(8,128)(2,1)S(1)} %get-tuple-element.218.refs_10_), channel_id=1, source_target_pairs={{0,1},{1,0},{2,3},{3,2},{4,5},{5,4},{6,7},{7,6},{8,9},{9,8},{10,11... | collective-permute-start | bytes 196616 | tf_op jit(solution)/shard_map/ppermute | solution.py:1087
  69.2 1.9 %grads_3.1 = (f32[256,384]{1,0:T(8,128)S(1)}, f32[384,384]{1,0:T(8,128)S(1)}, f32[384,256]{1,0:T(8,128)S(1)}, f32[8,1024]{1,0:T(8,128)S(1)}) custom-call(s32[2]{0:T(128)S(1)} %pad_add_fusion.info, f32[1024,1024]{1,0:T(8,128)S(1)} %get-tuple-element.209.refs_0_, bf16[1024,1024]{1,0:T(8,128)(2,1)S(1)} %get-tuple-element.219.refs_1_, f32[2,1024]{1,0:T(2,128)S(1)} %copy-done.3), custom_call_target="tpu_custom_call" | custom-call | flops 704643072 | bytes 8388608 | tf_op jit(solution)/shard_map/grads_3/pallas_call | solution.py:575
  72.5 3.6 %backward_2.1 = (bf16[1024,1024]{1,0:T(8,128)(2,1)S(1)}, bf16[2,64,256]{2,1,0:T(8,128)(2,1)S(1)}, f32[2,256,256]{2,1,0:T(8,128)S(1)}) custom-call(s32[2]{0:T(128)S(1)} %pad_add_fusion.info, s32[16]{0:T(128)S(1)} %copy-done.10, f32[16]{0:T(128)S(1)} %copy-done.11, f32[1024,1024]{1,0:T(8,128)S(1)} %get-tuple-element.194.refs_0_, ...), custom_call_target="tpu_custom_call" | custom-call | flops 704643072 | bytes 8388608 | tf_op jit(solution)/shard_map/backward_2/pallas_call | solution.py:575
  76.4 1.5 %collective-permute-start.18 = (bf16[2,64,256]{2,1,0:T(8,128)(2,1)S(1)}, bf16[2,64,256]{2,1,0:T(8,128)(2,1)S(1)}, u32[]{:S(2)}, u32[]{:S(2)}) collective-permute-start(bf16[2,64,256]{2,1,0:T(8,128)(2,1)S(1)} %get-tuple-element.227.refs_10_), channel_id=1, source_target_pairs={{0,1},{1,0},{2,3},{3,2},{4,5},{5,4},{6,7},{7,6},{8,9},{9,8},{10,11... | collective-permute-start | bytes 196616 | tf_op jit(solution)/shard_map/ppermute | solution.py:1087
  77.8 2.0 %grads_2.1 = (f32[256,384]{1,0:T(8,128)S(1)}, f32[384,384]{1,0:T(8,128)S(1)}, f32[384,256]{1,0:T(8,128)S(1)}, f32[8,1024]{1,0:T(8,128)S(1)}) custom-call(s32[2]{0:T(128)S(1)} %pad_add_fusion.info, f32[1024,1024]{1,0:T(8,128)S(1)} %get-tuple-element.194.refs_0_, ...), custom_call_target="tpu_custom_call", output_to_operand_aliasing={{0}: (4, {}), {1}: (5, {}), {2}: (6, {}), {3}: (7, {})} | custom-call | flops 704643072 | bytes 8388608 | tf_op jit(solution)/shard_map/grads_2/pallas_call | solution.py:575
  82.0 3.7 %backward_1.1 = (bf16[1024,1024]{1,0:T(8,128)(2,1)S(1)}, bf16[2,64,256]{2,1,0:T(8,128)(2,1)S(1)}, f32[2,256,256]{2,1,0:T(8,128)S(1)}) custom-call(s32[2]{0:T(128)S(1)} %pad_add_fusion.info, s32[16]{0:T(128)S(1)} %copy-done.10, f32[16]{0:T(128)S(1)} %copy-done.11, f32[1024,1024]{1,0:T(8,128)S(1)} %get-tuple-element.180.refs_0_, ...), custom_call_target="tpu_custom_call" | custom-call | flops 704643072 | bytes 8388608 | tf_op jit(solution)/shard_map/backward_1/pallas_call | solution.py:575
  85.8 1.5 %collective-permute-start.21 = (bf16[2,64,256]{2,1,0:T(8,128)(2,1)S(1)}, bf16[2,64,256]{2,1,0:T(8,128)(2,1)S(1)}, u32[]{:S(2)}, u32[]{:S(2)}) collective-permute-start(bf16[2,64,256]{2,1,0:T(8,128)(2,1)S(1)} %get-tuple-element.240.refs_10_), channel_id=1, source_target_pairs={{0,1},{1,0},{2,3},{3,2},{4,5},{5,4},{6,7},{7,6},{8,9},{9,8},{10,11... | collective-permute-start | bytes 196616 | tf_op jit(solution)/shard_map/ppermute | solution.py:1087
  87.3 2.3 %grads_1.1 = (f32[256,384]{1,0:T(8,128)S(1)}, f32[384,384]{1,0:T(8,128)S(1)}, f32[384,256]{1,0:T(8,128)S(1)}, f32[8,1024]{1,0:T(8,128)S(1)}) custom-call(s32[2]{0:T(128)S(1)} %pad_add_fusion.info, f32[1024,1024]{1,0:T(8,128)S(1)} %get-tuple-element.180.refs_0_, ...), custom_call_target="tpu_custom_call", output_to_operand_aliasing={{0}: (4, {}), {1}: (5, {}), {2}: (6, {}), {3}: (7, {})} | custom-call | flops 704643072 | bytes 8388608 | tf_op jit(solution)/shard_map/grads_1/pallas_call | solution.py:575
  90.1 1.2 collective-permute-done.23.refs_13_
  91.4 2.9 %backward_0.1.refs_1_ = bf16[1024,1024]{1,0:T(8,128)(2,1)S(1)} custom-call(s32[2]{0:T(128)S(1)} %pad_add_fusion.info, s32[16]{0:T(128)S(1)} %copy-done.10, f32[16]{0:T(128)S(1)} %copy-done.11, f32[1024,1024]{1,0:T(8,128)S(1)} %get-tuple-element.160.refs_0_, f32[1024,768]{1,0:T(8,128)S(1)} %slopes_0.1.refs_1_, ...), custom_call_target="tpu_custom_call" | custom-call | flops 704643072 | bytes 8388608 | tf_op jit(solution)/shard_map/backward_0/pallas_call | solution.py:575
  94.3 2.2 %grads_0.1 = (f32[1408,128]{1,0:T(8,128)S(1)}, bf16[1408,128]{1,0:T(8,128)(2,1)S(1)}) custom-call(s32[2]{0:T(128)S(1)} %pad_add_fusion.info, f32[1024,1024]{1,0:T(8,128)S(1)} %get-tuple-element.160.refs_0_, bf16[1024,1024]{1,0:T(8,128)(2,1)S(1)} %backward_0.1.refs_1_, f32[2,1024]{1,0:T(2,128)S(1)} %copy-done.3, f32[256,384]{1,0:T(8,128)S(1)} %get-tuple-element.253.refs_3_, ...), custom_call_target="tpu_custom_call" | custom-call | flops 704643072 | bytes 8388608 | tf_op jit(solution)/shard_map/grads_0/pallas_call | solution.py:575
  96.9 1.5 %collective-permute-done.24.got = bf16[1408,128]{1,0:T(8,128)(2,1)S(1)} collective-permute-done((bf16[1408,128]{1,0:T(8,128)(2,1)S(1)}, bf16[1408,128]{1,0:T(8,128)(2,1)S(1)}, u32[]{:S(2)}, u32[]{:S(2)}) %collective-permute-start.24) | collective-permute-done | bytes 360480 | tf_op jit(solution)/shard_map/ppermute | solution.py:1081
  98.4 11.8 %all_to_all.15.got = bf16[8,192,128]{2,1,0:T(8,128)(2,1)S(1)} all-to-all(bf16[8,192,128]{2,1,0:T(8,128)(2,1)S(1)} %pairs.1), channel_id=1, replica_groups={{0,1,2,3,4,5,6,7},{8,9,10,11,12,13,14,15},{16,17,18,19,20,21,22,23},{24..., dimensions={0} | all-to-all | bytes 786432 | tf_op jit(solution)/shard_map/all_to_all | solution.py:1168
  110.3 9.9 %all_to_all.16 = bf16[8,176,128]{2,1,0:T(8,128)(2,1)S(1)} all-to-all(bf16[8,176,128]{2,1,0:T(8,128)(2,1)S(1)} %get-tuple-element.260), channel_id=1, replica_groups={{0,1,2,3,4,5,6,7},{8,9,10,11,12,13,14,15},{16,17,18,19,20,21,22,23},{24..., dimensions={0} | all-to-all | bytes 720896 | tf_op jit(solution)/shard_map/all_to_all | solution.py:1168
  120.1 1.7 %collective-permute-done.25.part_o = bf16[1408,128]{1,0:T(8,128)(2,1)S(1)} collective-permute-done((bf16[1408,128]{1,0:T(8,128)(2,1)S(1)}, bf16[1408,128]{1,0:T(8,128)(2,1)S(1)}, u32[]{:S(2)}, u32[]{:S(2)}) %collective-permute-start.25) | collective-permute-done | bytes 360480 | tf_op jit(solution)/shard_map/ppermute | solution.py:1081
  121.9 3.4 %update.1 = (f32[1,1]{1,0:T(1,128)}, f32[1,1]{1,0:T(1,128)}, f32[256,384]{1,0:T(8,128)}, f32[384,384]{1,0:T(8,128)}, f32[384,256]{1,0:T(8,128)}, /*index=5*/f32[...) custom-call(s32[2]{0:T(128)S(1)} %pad_add_fusion.info, ...), custom_call_target="tpu_custom_call" | custom-call | tf_op jit(solution)/shard_map/update/pallas_call | solution.py:1025
  (100 shorter events, 21.4 us)
Async XLA Ops:
  0.7 25.3 %copy-start.11 = (f32[16]{0:T(128)S(1)}, f32[16]{0:T(128)}, u32[]{:S(2)}) copy-start(f32[16]{0:T(128)} %quad.29) | copy-start | bytes 196
  0.7 25.3 %copy-start.3 = (f32[2,1024]{1,0:T(2,128)S(1)}, f32[2,1024]{1,0:T(2,128)}, u32[]{:S(2)}) copy-start(f32[2,1024]{1,0:T(2,128)} %refs_3_.1) | copy-start | bytes 24580
  2.4 1.4 %collective-permute-start = (bf16[2,40,256]{2,1,0:T(8,128)(2,1)S(1)}, bf16[2,40,256]{2,1,0:T(8,128)(2,1)S(1)}, u32[]{:S(2)}, u32[]{:S(2)}) collective-permute-start(bf16[2,40,256]{2,1,0:T(8,128)(2,1)S(1)} %get-tuple-element.150), channel_id=1, source_target_pairs={{0,16},{16,0},{1,17},{17,1},{2,18},{18,2},{3,19},{19,3},{4,20},{20... | collective-permute-start | bytes 122888 | tf_op jit(solution)/shard_map/ppermute | solution.py:1081
  2.9 21.5 %collective-permute-start.2 = (f32[2,4,8]{2,1,0:T(4,128)}, f32[2,4,8]{2,1,0:T(4,128)S(1)}, u32[]{:S(2)}, u32[]{:S(2)}) collective-permute-start(f32[2,4,8]{2,1,0:T(4,128)} %param.25), channel_id=1, source_target_pairs={{0,16},{16,0},{1,17},{17,1},{2,18},{18,2},{3,19},{19,3},{4,20},{20... | collective-permute-start | bytes 776 | tf_op jit(solution)/shard_map/ppermute | solution.py:1081
  4.6 19.8 %all-to-all-start = ((bf16[16,40,256]{2,1,0:T(8,128)(2,1)}), bf16[16,40,256]{2,1,0:T(8,128)(2,1)S(1)}, u32[]{:S(2)}, u32[]{:S(2)}) async-start(bf16[16,40,256]{2,1,0:T(8,128)(2,1)} %bitcast.2), calls=%async_computation | async-start | bytes 655360 | tf_op jit(solution)/shard_map/all_to_all | solution.py:1110
  24.4 1.6 %collective-permute-start.1 = (bf16[16,40,256]{2,1,0:T(8,128)(2,1)S(1)}, bf16[16,40,256]{2,1,0:T(8,128)(2,1)S(1)}, u32[]{:S(2)}, u32[]{:S(2)}) collective-permute-start(bf16[16,40,256]{2,1,0:T(8,128)(2,1)S(1)} %all-to-all-done.got.refs_0_), channel_id=1, source_target_pairs={{0,16},{16,0},{1,17},{17,1},{2,18},{18,2},{3,19},{19,3},{4,20},{20... | collective-permute-start | bytes 983048 | tf_op jit(solution)/shard_map/ppermute | solution.py:1081
  29.7 4.3 %collective-permute-start.3 = (bf16[2,64,256]{2,1,0:T(8,128)(2,1)S(1)}, bf16[2,64,256]{2,1,0:T(8,128)(2,1)S(1)}, u32[]{:S(2)}, u32[]{:S(2)}) collective-permute-start(bf16[2,64,256]{2,1,0:T(8,128)(2,1)S(1)} %get-tuple-element.176.refs_9_), channel_id=1, source_target_pairs={{0,1},{1,0},{2,3},{3,2},{4,5},{5,4},{6,7},{7,6},{8,9},{9,8},{10,11... | collective-permute-start | bytes 196616 | tf_op jit(solution)/shard_map/ppermute | solution.py:1087
  30.2 4.9 %collective-permute-start.4 = (bf16[2,64,256]{2,1,0:T(8,128)(2,1)S(1)}, bf16[2,64,256]{2,1,0:T(8,128)(2,1)S(1)}, u32[]{:S(2)}, u32[]{:S(2)}) collective-permute-start(bf16[2,64,256]{2,1,0:T(8,128)(2,1)S(1)} %get-tuple-element.176.refs_9_), channel_id=1, source_target_pairs={{0,16},{16,0},{1,17},{17,1},{2,18},{18,2},{3,19},{19,3},{4,20},{20... | collective-permute-start | bytes 196616 | tf_op jit(solution)/shard_map/ppermute | solution.py:1081
  33.9 1.3 %collective-permute-start.5 = (bf16[2,64,256]{2,1,0:T(8,128)(2,1)S(1)}, bf16[2,64,256]{2,1,0:T(8,128)(2,1)S(1)}, u32[]{:S(2)}, u32[]{:S(2)}) collective-permute-start(bf16[2,64,256]{2,1,0:T(8,128)(2,1)S(1)} %collective-permute-done.3.refs_10_), channel_id=1, source_target_pairs={{0,16},{16,0},{1,17},{17,1},{2,18},{18,2},{3,19},{19,3},{4,20},{20... | collective-permute-start | bytes 196616 | tf_op jit(solution)/shard_map/ppermute | solution.py:1081
  39.2 4.5 %collective-permute-start.6 = (bf16[2,64,256]{2,1,0:T(8,128)(2,1)S(1)}, bf16[2,64,256]{2,1,0:T(8,128)(2,1)S(1)}, u32[]{:S(2)}, u32[]{:S(2)}) collective-permute-start(bf16[2,64,256]{2,1,0:T(8,128)(2,1)S(1)} %get-tuple-element.190.refs_9_), channel_id=1, source_target_pairs={{0,1},{1,0},{2,3},{3,2},{4,5},{5,4},{6,7},{7,6},{8,9},{9,8},{10,11... | collective-permute-start | bytes 196616 | tf_op jit(solution)/shard_map/ppermute | solution.py:1087
  39.8 5.0 %collective-permute-start.7 = (bf16[2,64,256]{2,1,0:T(8,128)(2,1)S(1)}, bf16[2,64,256]{2,1,0:T(8,128)(2,1)S(1)}, u32[]{:S(2)}, u32[]{:S(2)}) collective-permute-start(bf16[2,64,256]{2,1,0:T(8,128)(2,1)S(1)} %get-tuple-element.190.refs_9_), channel_id=1, source_target_pairs={{0,16},{16,0},{1,17},{17,1},{2,18},{18,2},{3,19},{19,3},{4,20},{20... | collective-permute-start | bytes 196616 | tf_op jit(solution)/shard_map/ppermute | solution.py:1081
  43.6 1.3 %collective-permute-start.8 = (bf16[2,64,256]{2,1,0:T(8,128)(2,1)S(1)}, bf16[2,64,256]{2,1,0:T(8,128)(2,1)S(1)}, u32[]{:S(2)}, u32[]{:S(2)}) collective-permute-start(bf16[2,64,256]{2,1,0:T(8,128)(2,1)S(1)} %collective-permute-done.6.refs_10_), channel_id=1, source_target_pairs={{0,16},{16,0},{1,17},{17,1},{2,18},{18,2},{3,19},{19,3},{4,20},{20... | collective-permute-start | bytes 196616 | tf_op jit(solution)/shard_map/ppermute | solution.py:1081
  48.9 4.5 %collective-permute-start.9 = (bf16[2,64,256]{2,1,0:T(8,128)(2,1)S(1)}, bf16[2,64,256]{2,1,0:T(8,128)(2,1)S(1)}, u32[]{:S(2)}, u32[]{:S(2)}) collective-permute-start(bf16[2,64,256]{2,1,0:T(8,128)(2,1)S(1)} %get-tuple-element.205.refs_11_), channel_id=1, source_target_pairs={{0,1},{1,0},{2,3},{3,2},{4,5},{5,4},{6,7},{7,6},{8,9},{9,8},{10,11... | collective-permute-start | bytes 196616 | tf_op jit(solution)/shard_map/ppermute | solution.py:1087
  49.5 5.0 %collective-permute-start.10 = (bf16[2,64,256]{2,1,0:T(8,128)(2,1)S(1)}, bf16[2,64,256]{2,1,0:T(8,128)(2,1)S(1)}, u32[]{:S(2)}, u32[]{:S(2)}) collective-permute-start(bf16[2,64,256]{2,1,0:T(8,128)(2,1)S(1)} %get-tuple-element.205.refs_11_), channel_id=1, source_target_pairs={{0,16},{16,0},{1,17},{17,1},{2,18},{18,2},{3,19},{19,3},{4,20},{20... | collective-permute-start | bytes 196616 | tf_op jit(solution)/shard_map/ppermute | solution.py:1081
  53.3 1.3 %collective-permute-start.11 = (bf16[2,64,256]{2,1,0:T(8,128)(2,1)S(1)}, bf16[2,64,256]{2,1,0:T(8,128)(2,1)S(1)}, u32[]{:S(2)}, u32[]{:S(2)}) collective-permute-start(bf16[2,64,256]{2,1,0:T(8,128)(2,1)S(1)} %collective-permute-done.9.refs_12_), channel_id=1, source_target_pairs={{0,16},{16,0},{1,17},{17,1},{2,18},{18,2},{3,19},{19,3},{4,20},{20... | collective-permute-start | bytes 196616 | tf_op jit(solution)/shard_map/ppermute | solution.py:1081
  59.0 3.7 %collective-permute-start.14 = (f32[40,128]{1,0:T(8,128)S(1)}, f32[40,128]{1,0:T(8,128)S(1)}, u32[]{:S(2)}, u32[]{:S(2)}) collective-permute-start(f32[40,128]{1,0:T(8,128)S(1)} %get-tuple-element.210.refs_8_.refs_0_), channel_id=1, source_target_pairs={{0,17},{1,16},{2,19},{3,18},{4,21},{5,20},{6,23},{7,22},{8,25},{9,... | collective-permute-start | bytes 61448 | tf_op jit(solution)/shard_map/ppermute | solution.py:1101
  59.6 3.1 %collective-permute-start.13 = (f32[40,128]{1,0:T(8,128)S(1)}, f32[40,128]{1,0:T(8,128)S(1)}, u32[]{:S(2)}, u32[]{:S(2)}) collective-permute-start(f32[40,128]{1,0:T(8,128)S(1)} %get-tuple-element.210.refs_8_.refs_0_), channel_id=1, source_target_pairs={{0,16},{16,0},{1,17},{17,1},{2,18},{18,2},{3,19},{19,3},{4,20},{20... | collective-permute-start | bytes 61448 | tf_op jit(solution)/shard_map/ppermute | solution.py:1081
  59.7 3.8 %collective-permute-start.12 = (f32[40,128]{1,0:T(8,128)S(1)}, f32[40,128]{1,0:T(8,128)S(1)}, u32[]{:S(2)}, u32[]{:S(2)}) collective-permute-start(f32[40,128]{1,0:T(8,128)S(1)} %get-tuple-element.210.refs_8_.refs_0_), channel_id=1, source_target_pairs={{0,1},{1,0},{2,3},{3,2},{4,5},{5,4},{6,7},{7,6},{8,9},{9,8},{10,11... | collective-permute-start | bytes 61448 | tf_op jit(solution)/shard_map/ppermute | solution.py:1101
  66.8 5.4 %collective-permute-start.16 = (bf16[2,64,256]{2,1,0:T(8,128)(2,1)S(1)}, bf16[2,64,256]{2,1,0:T(8,128)(2,1)S(1)}, u32[]{:S(2)}, u32[]{:S(2)}) collective-permute-start(bf16[2,64,256]{2,1,0:T(8,128)(2,1)S(1)} %get-tuple-element.218.refs_10_), channel_id=1, source_target_pairs={{0,16},{16,0},{1,17},{17,1},{2,18},{18,2},{3,19},{19,3},{4,20},{20... | collective-permute-start | bytes 196616 | tf_op jit(solution)/shard_map/ppermute | solution.py:1081
  66.8 4.5 %collective-permute-start.15 = (bf16[2,64,256]{2,1,0:T(8,128)(2,1)S(1)}, bf16[2,64,256]{2,1,0:T(8,128)(2,1)S(1)}, u32[]{:S(2)}, u32[]{:S(2)}) collective-permute-start(bf16[2,64,256]{2,1,0:T(8,128)(2,1)S(1)} %get-tuple-element.218.refs_10_), channel_id=1, source_target_pairs={{0,1},{1,0},{2,3},{3,2},{4,5},{5,4},{6,7},{7,6},{8,9},{9,8},{10,11... | collective-permute-start | bytes 196616 | tf_op jit(solution)/shard_map/ppermute | solution.py:1087
  71.3 1.3 %collective-permute-start.17 = (bf16[2,64,256]{2,1,0:T(8,128)(2,1)S(1)}, bf16[2,64,256]{2,1,0:T(8,128)(2,1)S(1)}, u32[]{:S(2)}, u32[]{:S(2)}) collective-permute-start(bf16[2,64,256]{2,1,0:T(8,128)(2,1)S(1)} %collective-permute-done.15.refs_11_), channel_id=1, source_target_pairs={{0,16},{16,0},{1,17},{17,1},{2,18},{18,2},{3,19},{19,3},{4,20},{20... | collective-permute-start | bytes 196616 | tf_op jit(solution)/shard_map/ppermute | solution.py:1081
  76.2 5.4 %collective-permute-start.19 = (bf16[2,64,256]{2,1,0:T(8,128)(2,1)S(1)}, bf16[2,64,256]{2,1,0:T(8,128)(2,1)S(1)}, u32[]{:S(2)}, u32[]{:S(2)}) collective-permute-start(bf16[2,64,256]{2,1,0:T(8,128)(2,1)S(1)} %get-tuple-element.227.refs_10_), channel_id=1, source_target_pairs={{0,16},{16,0},{1,17},{17,1},{2,18},{18,2},{3,19},{19,3},{4,20},{20... | collective-permute-start | bytes 196616 | tf_op jit(solution)/shard_map/ppermute | solution.py:1081
  76.4 4.3 %collective-permute-start.18 = (bf16[2,64,256]{2,1,0:T(8,128)(2,1)S(1)}, bf16[2,64,256]{2,1,0:T(8,128)(2,1)S(1)}, u32[]{:S(2)}, u32[]{:S(2)}) collective-permute-start(bf16[2,64,256]{2,1,0:T(8,128)(2,1)S(1)} %get-tuple-element.227.refs_10_), channel_id=1, source_target_pairs={{0,1},{1,0},{2,3},{3,2},{4,5},{5,4},{6,7},{7,6},{8,9},{9,8},{10,11... | collective-permute-start | bytes 196616 | tf_op jit(solution)/shard_map/ppermute | solution.py:1087
  80.7 1.3 %collective-permute-start.20 = (bf16[2,64,256]{2,1,0:T(8,128)(2,1)S(1)}, bf16[2,64,256]{2,1,0:T(8,128)(2,1)S(1)}, u32[]{:S(2)}, u32[]{:S(2)}) collective-permute-start(bf16[2,64,256]{2,1,0:T(8,128)(2,1)S(1)} %collective-permute-done.18.refs_11_), channel_id=1, source_target_pairs={{0,16},{16,0},{1,17},{17,1},{2,18},{18,2},{3,19},{19,3},{4,20},{20... | collective-permute-start | bytes 196616 | tf_op jit(solution)/shard_map/ppermute | solution.py:1081
  85.6 4.5 %collective-permute-start.22 = (bf16[2,64,256]{2,1,0:T(8,128)(2,1)S(1)}, bf16[2,64,256]{2,1,0:T(8,128)(2,1)S(1)}, u32[]{:S(2)}, u32[]{:S(2)}) collective-permute-start(bf16[2,64,256]{2,1,0:T(8,128)(2,1)S(1)} %get-tuple-element.240.refs_10_), channel_id=1, source_target_pairs={{0,16},{16,0},{1,17},{17,1},{2,18},{18,2},{3,19},{19,3},{4,20},{20... | collective-permute-start | bytes 196616 | tf_op jit(solution)/shard_map/ppermute | solution.py:1081
  85.8 4.3 %collective-permute-start.21 = (bf16[2,64,256]{2,1,0:T(8,128)(2,1)S(1)}, bf16[2,64,256]{2,1,0:T(8,128)(2,1)S(1)}, u32[]{:S(2)}, u32[]{:S(2)}) collective-permute-start(bf16[2,64,256]{2,1,0:T(8,128)(2,1)S(1)} %get-tuple-element.240.refs_10_), channel_id=1, source_target_pairs={{0,1},{1,0},{2,3},{3,2},{4,5},{5,4},{6,7},{7,6},{8,9},{9,8},{10,11... | collective-permute-start | bytes 196616 | tf_op jit(solution)/shard_map/ppermute | solution.py:1087
  90.1 1.3 %collective-permute-start.23 = (bf16[2,64,256]{2,1,0:T(8,128)(2,1)S(1)}, bf16[2,64,256]{2,1,0:T(8,128)(2,1)S(1)}, u32[]{:S(2)}, u32[]{:S(2)}) collective-permute-start(bf16[2,64,256]{2,1,0:T(8,128)(2,1)S(1)} %collective-permute-done.21.refs_11_), channel_id=1, source_target_pairs={{0,16},{16,0},{1,17},{17,1},{2,18},{18,2},{3,19},{19,3},{4,20},{20... | collective-permute-start | bytes 196616 | tf_op jit(solution)/shard_map/ppermute | solution.py:1081
  94.3 27.5 %copy-start.9 = (f32[384,256]{1,0:T(8,128)S(1)}, f32[384,256]{1,0:T(8,128)}, u32[]{:S(2)}) copy-start(f32[384,256]{1,0:T(8,128)} %refs_10_.1) | copy-start | bytes 1179652
  96.5 25.3 %copy-start.1 = (f32[256,384]{1,0:T(8,128)S(1)}, f32[256,384]{1,0:T(8,128)}, u32[]{:S(2)}) copy-start(f32[256,384]{1,0:T(8,128)} %refs_0_.1) | copy-start | bytes 1179652
  96.5 25.3 %copy-start.2 = (f32[384,256]{1,0:T(8,128)S(1)}, f32[384,256]{1,0:T(8,128)}, u32[]{:S(2)}) copy-start(f32[384,256]{1,0:T(8,128)} %refs_2_.9) | copy-start | bytes 1179652
  96.6 1.7 %collective-permute-start.24 = (bf16[1408,128]{1,0:T(8,128)(2,1)S(1)}, bf16[1408,128]{1,0:T(8,128)(2,1)S(1)}, u32[]{:S(2)}, u32[]{:S(2)}) collective-permute-start(bf16[1408,128]{1,0:T(8,128)(2,1)S(1)} %get-tuple-element.258), channel_id=1, source_target_pairs={{0,16},{16,0},{1,17},{17,1},{2,18},{18,2},{3,19},{19,3},{4,20},{20... | collective-permute-start | bytes 1081352 | tf_op jit(solution)/shard_map/ppermute | solution.py:1081
  120.1 1.7 %collective-permute-start.25 = (bf16[1408,128]{1,0:T(8,128)(2,1)S(1)}, bf16[1408,128]{1,0:T(8,128)(2,1)S(1)}, u32[]{:S(2)}, u32[]{:S(2)}) collective-permute-start(bf16[1408,128]{1,0:T(8,128)(2,1)S(1)} %bitcast.10), channel_id=1, source_target_pairs={{0,16},{16,0},{1,17},{17,1},{2,18},{18,2},{3,19},{19,3},{4,20},{20... | collective-permute-start | bytes 1081352 | tf_op jit(solution)/shard_map/ppermute | solution.py:1081
  (11 other events, 264.5 us)
